TPU v7x, 32 devices: a whole 2x2x4 slice. The times are simulated.
32 devices in a mesh: dp: 4 (over y, x), expert: 8 (over z, core).
Axes of the slice: x: 2, y: 2, z: 4, core: 2. Of those that a mesh axis runs over, the one named last changes fastest.
Arguments:
- tables: float32 [4, 8192, 256], P(None, ('dp', 'expert')), may hold values from -3 to 3
- accum: float32 [4, 8192], P(None, ('dp', 'expert')), may hold values from 0.01 to 1
- bag_owner: int32 [4096, 16], P(('dp', 'expert')), may hold values from 0 to 31, all different within a row; in each aligned block of 128 rows (0 to 127, 128 to 255, ...) at most 81 rows name the same one
- bag_row: int32 [4096, 16], P(('dp', 'expert')), may hold values from 0 to 255
- bag_len: int32 [4, 4096], P(None, ('dp', 'expert')), may hold values from 1 to 4, 10240 in all within a row
- route: int32 [4096, 2], P(('dp', 'expert')), may hold values from 0 to 7, all different within a row; in each aligned block of 128 rows (0 to 127, 128 to 255, ...) at most 33 rows name the same one
- labels: float32 [4096, 2], P(('dp', 'expert')), may hold values from 0 to 1
- w_in: bfloat16 [8, 1024, 2048], P('expert', None, 'dp'), may hold values from -0.1875 to 0.1875
- w_out: bfloat16 [8, 2048, 1024], P('expert', 'dp'), may hold values from -0.125 to 0.125
- gate_w: bfloat16 [2, 1024, 8], replicated, may hold values from -0.1875 to 0.1875
- head: float32 [2, 1024], replicated, may hold values from -0.375 to 0.375
Outputs:
- logits: float32 [4096, 2], P(('dp', 'expert'))
- new_tables: float32 [4, 8192, 256], P(None, ('dp', 'expert'))
- new_accum: float32 [4, 8192], P(None, ('dp', 'expert'))
Inputs may be any that keep to these rules, and one draw needn't show every extreme that they name: `bag_owner`: each sample names 16 different owners; the rows of one device name any one owner at most 81 times. `route`: each sample names two different experts; the rows of one device name any one expert at most 33 times.
All inputs are finite; a program needn't handle non-finite values. No bound on the sum of `bag_len` on one device may be relied on, other than what follows from the above.
Results may differ from a plain program's by a relative error of at most 0.0062.
Values may be sent and summed in bfloat16 or wider, within the bound.
No kernel may reach another device: no remote copies, remote signals or barrier semaphores. Data moves between devices by JAX's collectives and lax.ppermute only.
A program may use at most 128 MiB of HBM per device.

v0:
```python
import jax
import jax.numpy as jnp
from jax import lax
from jax.experimental import pallas as pl
from jax.experimental.pallas import tpu as pltpu
from jax.sharding import PartitionSpec as P


learn_rate = 0.3
norm_eps = 1e-05
LANES = 128
F32 = jnp.float32
BF16 = jnp.bfloat16
I32 = jnp.int32


def vmem(count):
    return [pl.BlockSpec(memory_space=pltpu.VMEM)] * count


def hbm(count):
    return [pl.BlockSpec(memory_space=pltpu.HBM)] * count


def params(mib):
    return pltpu.CompilerParams(vmem_limit_bytes=mib << 20)


def seq(count, body):
    if count <= 32:
        for i in range(count):
            body(i)
    else:
        lax.fori_loop(0, count, lambda i, c: (body(i), c)[1], 0)


def part(refs, o, a, b):
    return refs[o].at[a:b, :] if isinstance(refs, (list, tuple)) else refs.at[o, a:b, :]


class Slots:
    def __init__(self, peers, cap, width, group, apart=False):
        self.apart = apart
        self.peers, self.width = peers, width
        self.main, self.ext = (cap - 1, 1) if cap % 16 == 1 else (-(-cap // 16) * 16, 0)
        self.lane_blocks = width // LANES
        self.group = min(peers, group)
        self.blocks = peers // self.group
        self.rows = self.group * (self.main + self.ext)
        self.ext_units = -(-self.lane_blocks // 8) * 8 * self.ext
        self.units = self.main * self.lane_blocks + self.ext_units

    @property
    def arrays(self):
        return self.peers if self.apart else 1

    def refs(self, refs):
        return refs[0 : self.peers] if self.apart else refs[0]

    def shapes(self):
        if self.apart:
            return [jax.ShapeDtypeStruct((self.units, LANES), BF16)] * self.peers
        return [jax.ShapeDtypeStruct((self.peers, self.units, LANES), BF16)]

    def pick(self, axis):
        shape = (self.group, self.rows) if axis == 1 else (self.rows, self.group)
        c = lax.broadcasted_iota(I32, shape, axis)
        o = lax.broadcasted_iota(I32, shape, 1 - axis)
        base = o * self.main
        bulk = self.group * self.main
        own = (c >= base) & (c < base + self.main)
        rank = c - base + 1
        if self.ext:
            own = own | (c == bulk + o)
            rank = jnp.where(c < bulk, rank, self.main + 1)
        expand = jnp.where(own, 1.0, 0.0).astype(BF16)
        rank = jnp.sum(jnp.where(own, rank.astype(F32), 0.0), axis=1 - axis, keepdims=True)
        return expand, rank

    def spread(self, ranks, picks):
        expand, rank = picks
        held = jnp.dot(ranks.astype(BF16), expand, preferred_element_type=F32)
        return jnp.where(held == rank, 1.0, 0.0).astype(BF16)

    def spread_t(self, ranks, picks):
        expand, rank = picks
        held = lax.dot_general(
            expand, ranks.astype(BF16), (((1,), (1,)), ((), ())), preferred_element_type=F32
        )
        return jnp.where(held == rank, 1.0, 0.0).astype(BF16)

    def ext_pick(self, j):
        shape = (self.group * self.ext_units, self.group)
        u = lax.broadcasted_iota(I32, shape, 0)
        o = lax.broadcasted_iota(I32, shape, 1)
        return jnp.where(u == o * self.ext_units + j, 1.0, 0.0).astype(BF16)

    def pack(self, block, rows_ref, out_ref):
        main, first = self.main, block * self.group

        def one(o):
            start = o * main if isinstance(o, int) else pl.multiple_of(o * main, 16)
            for j in range(self.lane_blocks):
                part(out_ref, first + o, j * main, (j + 1) * main)[...] = rows_ref[
                    pl.ds(start, main), j * LANES : (j + 1) * LANES
                ]

        seq(self.group, one)
        if self.ext:
            extra = jnp.zeros((self.group * self.ext_units, LANES), F32)
            tail = rows_ref[self.group * main : self.rows, :]
            for j in range(self.lane_blocks):
                extra = extra + jnp.dot(
                    self.ext_pick(j), tail[:, j * LANES : (j + 1) * LANES], preferred_element_type=F32
                )
            for o in range(self.group):
                part(out_ref, first + o, self.lane_blocks * main, self.units)[...] = extra[
                    o * self.ext_units : (o + 1) * self.ext_units
                ].astype(BF16)

    def unpack(self, block, in_ref, rows_ref):
        main, first = self.main, block * self.group

        def one(o):
            start = o * main if isinstance(o, int) else pl.multiple_of(o * main, 16)
            for j in range(self.lane_blocks):
                rows_ref[pl.ds(start, main), j * LANES : (j + 1) * LANES] = part(
                    in_ref, first + o, j * main, (j + 1) * main
                )[...]

        seq(self.group, one)
        if self.ext:
            extra = [
                part(in_ref, first + o, self.lane_blocks * main, self.units)[...].astype(F32)
                for o in range(self.group)
            ]
            extra = jnp.concatenate(extra, axis=0).astype(BF16)
            for j in range(self.lane_blocks):
                rows_ref[self.group * main : self.rows, j * LANES : (j + 1) * LANES] = (
                    lax.dot_general(
                        self.ext_pick(j),
                        extra,
                        (((0,), (0,)), ((), ())),
                        preferred_element_type=F32,
                    ).astype(BF16)
                )


def one_hot_rows(slots, block, want_ref, hot_ref):
    group, main = slots.group, slots.main
    want = want_ref[block * group : (block + 1) * group, :].astype(F32)
    fill = jnp.zeros((LANES - group, LANES), F32)
    cols = jnp.concatenate([want, fill], axis=0).T
    entry = lax.broadcasted_iota(I32, (main, hot_ref.shape[1]), 1).astype(F32)
    for o in range(group):
        hit = cols[0:main, o : o + 1] == entry
        hot_ref[o * main : (o + 1) * main, :] = jnp.where(hit, 1.0, 0.0).astype(BF16)
    if slots.ext:
        entry = lax.broadcasted_iota(I32, (group, hot_ref.shape[1]), 1).astype(F32)
        hit = want[:, main : main + 1] == entry
        hot_ref[group * main : slots.rows, :] = jnp.where(hit, 1.0, 0.0).astype(BF16)


def index_kernel(cap, table_rows, me_ref, owner_ref, row_ref, len_ref, route_ref, rank_ref, want_ref, erank_ref, stage_ref, tmp_ref, sems):
    tables, samples, owners = rank_ref.shape
    experts = erank_ref.shape[2]
    columns = owner_ref.shape[0]
    slots = columns // tables
    lines = (0, columns, 2 * columns, 2 * columns + 8)
    counts = (columns, columns, tables, 2)
    copies = [
        pltpu.make_async_copy(ref, stage_ref.at[line : line + count, :], sems.at[i])
        for i, (ref, line, count) in enumerate(zip((owner_ref, row_ref, len_ref, route_ref), lines, counts))
    ]
    for copy in copies:
        copy.start()
    tmp_ref[...] = jnp.zeros(tmp_ref.shape, F32)
    for copy in copies:
        copy.wait()
    for line, count in zip(lines, counts):
        tmp_ref[line : line + count, 0:samples] = stage_ref[line : line + count, :].astype(F32)
    args = tmp_ref[:, 0:samples].T
    peer = lax.broadcasted_iota(I32, (samples, owners), 1).astype(F32)
    entry = jnp.zeros((samples, owners), F32)
    named = []
    for t in range(tables):
        mine = jnp.zeros((samples, owners), F32)
        length = args[:, 2 * columns + t : 2 * columns + t + 1]
        for b in range(slots):
            j = t * slots + b
            live = jnp.where(length > float(b), args[:, j : j + 1], -1.0)
            hit = live == peer
            mine = jnp.where(hit, 1.0, mine)
            entry = jnp.where(hit, args[:, columns + j : columns + j + 1] + float(t * table_rows + 1), entry)
        named.append(mine)
    every = sum(named)
    before = (
        lax.broadcasted_iota(I32, (samples, samples), 0) > lax.broadcasted_iota(I32, (samples, samples), 1)
    )
    before = jnp.where(before, 1.0, 0.0).astype(BF16)
    rank = jnp.dot(before, every.astype(BF16), preferred_element_type=F32) + 1.0
    for t in range(tables):
        rank_ref[t] = named[t] * rank
    rank = every * rank
    tmp_ref[...] = jnp.zeros(tmp_ref.shape, F32)
    for r in range(cap):
        tmp_ref[r : r + 1, 0:owners] = jnp.sum(
            jnp.where(rank == float(r + 1), entry, 0.0), axis=0, keepdims=True
        )
    want_ref[...] = tmp_ref[...].T[0:owners, :].astype(I32) - 1
    expert = lax.broadcasted_iota(I32, (samples, experts), 1)
    routes = [args[:, 2 * columns + 8 + k : 2 * columns + 9 + k] for k in range(2)]
    for k in range(2):
        erank_ref[2 + k] = jnp.where(routes[k] == expert.astype(F32), 1.0, 0.0)
    expert = (expert ^ me_ref[0]).astype(F32)
    hits = [jnp.where(routes[k] == expert, 1.0, 0.0) for k in range(2)]
    rank = jnp.dot(before, (hits[0] + hits[1]).astype(BF16), preferred_element_type=F32) + 1.0
    for k in range(2):
        erank_ref[k] = hits[k] * rank


def gather_kernel(slots, want_ref, table_ref, out_ref, held_ref, hot_ref, rows_ref, sem):
    copy = pltpu.make_async_copy(table_ref, held_ref, sem)
    copy.start()
    for block in range(slots.blocks):
        one_hot_rows(slots, block, want_ref, hot_ref)
        if block == 0:
            copy.wait()
        rows_ref[...] = jnp.dot(
            hot_ref[...], held_ref[...].astype(BF16), preferred_element_type=F32
        ).astype(BF16)
        slots.pack(block, rows_ref, out_ref)


def pool_kernel(slots, eslots, got_ref, rank_ref, erank_ref, gate_ref, *refs):
    out_ref = eslots.refs(refs)
    first_ref, rows_ref, feat_ref, send_ref = refs[eslots.arrays :]
    tables = rank_ref.shape[0]
    width = slots.width
    group = slots.group
    picks = slots.pick(1)
    sums = [0.0] * tables
    for block in range(slots.blocks):
        slots.unpack(block, got_ref, rows_ref)
        rows = rows_ref[...]
        for t in range(tables):
            ranks = rank_ref[t, :, block * group : (block + 1) * group]
            sums[t] = sums[t] + jnp.dot(slots.spread(ranks, picks), rows, preferred_element_type=F32)
    for t in range(tables):
        feat_ref[:, t * width : (t + 1) * width] = sums[t].astype(BF16)
    feats = feat_ref[...]
    eranks = [erank_ref[k] for k in range(2)]
    hot = eslots.spread_t(eranks[0] + eranks[1], eslots.pick(0))
    send_ref[...] = jnp.dot(hot, feats, preferred_element_type=F32).astype(BF16)
    eslots.pack(0, send_ref, out_ref)
    for t in range(first_ref.shape[1]):
        score = lax.dot_general(feats, gate_ref[t], (((1,), (1,)), ((), ())), preferred_element_type=F32)
        z = [jnp.sum(erank_ref[2 + k] * score, axis=1, keepdims=True) for k in range(2)]
        first_ref[:, t : t + 1] = jax.nn.sigmoid(z[0] - z[1])


def forward_kernel(eslots, *refs):
    n = eslots.arrays
    x_ref, refs = eslots.refs(refs), refs[n:]
    in_refs, out_refs, refs = refs[0:5], refs[5:10], refs[10:]
    y_ref = eslots.refs(refs)
    hidden_ref, rows_ref = refs[n:]
    eslots.unpack(0, x_ref, rows_ref)
    rows = rows_ref[...]
    half = rows.shape[1] // 2
    total = 0.0
    for i in range(4):
        if i < 3:
            pre = jnp.dot(rows, in_refs[i][...], preferred_element_type=F32)
        else:
            pre = jnp.dot(rows[:, :half], in_refs[3][...], preferred_element_type=F32)
            pre = pre + jnp.dot(rows[:, half:], in_refs[4][...], preferred_element_type=F32)
        hidden = jnp.maximum(pre, 0.0).astype(BF16)
        hidden_ref[i] = hidden
        if i < 3:
            total = total + jnp.dot(hidden, out_refs[i][...], preferred_element_type=F32)
        else:
            part = hidden.shape[1] // 2
            total = total + jnp.dot(hidden[:, :part], out_refs[3][...], preferred_element_type=F32)
            total = total + jnp.dot(hidden[:, part:], out_refs[4][...], preferred_element_type=F32)
    rows_ref[...] = total.astype(BF16)
    eslots.pack(0, rows_ref, y_ref)


def backward_kernel(eslots, *refs):
    n = eslots.arrays
    dy_ref, hidden_ref, refs = eslots.refs(refs), refs[n], refs[n + 1 :]
    in_refs, out_refs, refs = refs[0:5], refs[5:10], refs[10:]
    dx_ref = eslots.refs(refs)
    (rows_ref,) = refs[n:]
    eslots.unpack(0, dy_ref, rows_ref)
    rows = rows_ref[...]
    nt = (((1,), (1,)), ((), ()))
    half = rows.shape[1] // 2
    dots = lambda a, refs: [lax.dot_general(a, r[...], nt, preferred_element_type=F32) for r in refs]
    total = low = high = 0.0
    for i in range(4):
        dhidden = jnp.concatenate(dots(rows, out_refs[i : i + 1] if i < 3 else out_refs[3:5]), axis=1)
        dpre = jnp.where(hidden_ref[i].astype(F32) > 0.0, dhidden, 0.0).astype(BF16)
        if i < 3:
            total = total + dots(dpre, in_refs[i : i + 1])[0]
        else:
            low, high = dots(dpre, in_refs[3:5])
    rows_ref[:, :half] = (total[:, :half] + low).astype(BF16)
    rows_ref[:, half:] = (total[:, half:] + high).astype(BF16)
    eslots.pack(0, rows_ref, dx_ref)


def middle_kernel(eslots, *refs):
    n = eslots.arrays
    y_ref, refs = eslots.refs(refs), refs[n:]
    erank_ref, first_ref, label_ref, head_ref, gate_ref, logit_ref, dgate_ref = refs[0:7]
    out_ref = eslots.refs(refs[7:])
    rows_ref, tmp_ref = refs[7 + n :]
    samples, tasks = first_ref.shape
    tmp_ref[...] = jnp.zeros(tmp_ref.shape, F32)
    tmp_ref[0:tasks, 0:samples] = label_ref[...]
    labels = tmp_ref[:, 0:samples].T
    width = eslots.width
    eslots.unpack(0, y_ref, rows_ref)
    rows = rows_ref[...]
    eranks = [erank_ref[k] for k in range(2)]
    picks = eslots.pick(1)
    y0, y1 = [
        jnp.dot(eslots.spread(eranks[k], picks), rows, preferred_element_type=F32) for k in range(2)
    ]
    gap = y0 - y1
    sign = erank_ref[2] - erank_ref[3]
    lane = lax.broadcasted_iota(I32, (samples, LANES), 1)
    logits = jnp.zeros((samples, LANES), F32)
    dy0 = dy1 = dgate = 0.0
    for t in range(tasks):
        g = first_ref[:, t : t + 1]
        rest = 1.0 - g
        comb = g * y0 + rest * y1
        scale = jnp.sqrt(jnp.sum(comb * comb, axis=1, keepdims=True) * (1.0 / width) + norm_eps)
        inv = 1.0 / scale
        normed = comb * inv
        head = head_ref[t : t + 1, :]
        logit = jnp.sum(normed * head, axis=1, keepdims=True)
        logits = jnp.where(lane == t, logit, logits)
        dlogit = jax.nn.sigmoid(logit) - labels[:, t : t + 1]
        drop = dlogit * logit * (1.0 / width)
        dcomb = (dlogit * head - normed * drop) * inv
        dy0 = dy0 + g * dcomb
        dy1 = dy1 + rest * dcomb
        ddelta = jnp.sum(dcomb * gap, axis=1, keepdims=True) * g * rest
        dgate = dgate + jnp.dot(
            ddelta * sign,
            gate_ref[t].astype(F32),
            precision=lax.Precision.HIGHEST,
            preferred_element_type=F32,
        )
    dgate_ref[...] = dgate
    logit_ref[...] = logits.T[0:tasks, :]
    picks = eslots.pick(0)
    send = sum(
        jnp.dot(eslots.spread_t(eranks[k], picks), dy.astype(BF16), preferred_element_type=F32)
        for k, dy in enumerate((dy0, dy1))
    )
    rows_ref[...] = send.astype(BF16)
    eslots.pack(0, rows_ref, out_ref)


def spread_grads_kernel(slots, eslots, *refs):
    dx_ref, refs = eslots.refs(refs), refs[eslots.arrays :]
    erank_ref, dgate_ref, rank_ref, out_ref, rows_ref, grad_ref = refs
    tables = rank_ref.shape[0]
    width, group = slots.width, slots.group
    eslots.unpack(0, dx_ref, rows_ref)
    total = dgate_ref[...] + spread_pair(eslots, erank_ref, rows_ref)
    total = total.astype(BF16)
    picks = slots.pick(0)
    for block in range(slots.blocks):
        grads = 0.0
        for t in range(tables):
            ranks = rank_ref[t, :, block * group : (block + 1) * group]
            grads = grads + jnp.dot(
                slots.spread_t(ranks, picks), total[:, t * width : (t + 1) * width], preferred_element_type=F32
            )
        grad_ref[...] = grads.astype(BF16)
        slots.pack(block, grad_ref, out_ref)


def spread_pair(eslots, erank_ref, rows_ref):
    picks = eslots.pick(1)
    rows = rows_ref[...]
    hot = eslots.spread(erank_ref[0], picks) + eslots.spread(erank_ref[1], picks)
    return jnp.dot(hot, rows, preferred_element_type=F32)


def update_kernel(slots, got_ref, want_ref, table_ref, accum_ref, new_table_ref, new_accum_ref, held_ref, hot_ref, rows_ref, sem):
    copy = pltpu.make_async_copy(table_ref, held_ref, sem)
    copy.start()
    tables, table_rows = accum_ref.shape
    width = slots.width
    grads = 0.0
    for block in range(slots.blocks):
        one_hot_rows(slots, block, want_ref, hot_ref)
        slots.unpack(block, got_ref, rows_ref)
        grads = grads + lax.dot_general(
            rows_ref[...], hot_ref[...], (((0,), (0,)), ((), ())), preferred_element_type=F32
        )
    copy.wait()
    for t in range(tables):
        part = grads[:, t * table_rows : (t + 1) * table_rows]
        total = accum_ref[t : t + 1, :] + jnp.sum(part * part, axis=0, keepdims=True) * (1.0 / width)
        new_accum_ref[t : t + 1, :] = total
        step = part * (learn_rate / jnp.sqrt(total))
        new_table_ref[t] = held_ref[t] - step.T


def gather_weight(w):
    half = w.shape[0] // 2

    def send(x, bit):
        return lax.ppermute(x, "dp", [(i, i ^ bit) for i in range(4)])

    by1 = send(w, 1)
    by2 = send(w, 2)
    low = send(by1[:half], 2)
    high = send(by2[half:], 1)
    return [w, by1, by2, low, high]


def trade(eslots, chunks):
    if not eslots.apart:
        return [lax.all_to_all(chunks[0], "expert", 0, 0, tiled=True)]
    order = sorted(range(1, eslots.peers), key=lambda k: (-(k // 2), k))
    got = {0: chunks[0]}
    for k in order:
        got[k] = lax.ppermute(chunks[k], "expert", [(i, i ^ k) for i in range(eslots.peers)])
    return [got[k] for k in range(eslots.peers)]


def per_device(
    tables, accum, bag_owner, bag_row, bag_len, route, labels, w_in, w_out, gate_w, head
):
    dp_count = lax.axis_size("dp")
    expert_count = lax.axis_size("expert")
    device_count = dp_count * expert_count
    samples = route.shape[0]
    table_count, table_rows, emb = tables.shape
    entries = table_count * table_rows
    lookups = samples * bag_owner.shape[1]
    width = table_count * emb
    tasks = labels.shape[1]
    cap_rows = (5 * lookups + 4 * device_count - 1) // (4 * device_count) + 1
    cap_expert = (2 * samples + expert_count - 1) // expert_count + 1
    slots = Slots(device_count, cap_rows, emb, 32)
    apart = expert_count <= 8
    eslots = Slots(expert_count, cap_expert, width, expert_count, apart)
    shape = jax.ShapeDtypeStruct
    both = ("dp", "expert")
    me = lax.axis_index("expert").astype(I32) if apart else jnp.int32(0)
    me = me.reshape(1)

    ins = gather_weight(w_in[0])
    outs = gather_weight(w_out[0])

    def call(kernel, out_shape, scratch, *args, in_specs=None):
        many = isinstance(out_shape, (list, tuple))
        return pl.pallas_call(
            kernel,
            out_shape=out_shape,
            in_specs=in_specs or vmem(len(args)),
            out_specs=vmem(len(out_shape)) if many else vmem(1)[0],
            scratch_shapes=scratch,
            compiler_params=params(24 if eslots.rows <= 512 else 60),
        )(*args)

    def bind(fn, *static):
        return lambda *refs: fn(*static, *refs)

    square = pltpu.VMEM((LANES, max(LANES, device_count)), F32)
    rank, want, erank = call(
        bind(index_kernel, cap_rows, table_rows),
        [
            shape((table_count, samples, device_count), F32),
            shape((device_count, LANES), I32),
            shape((4, samples, expert_count), F32),
        ],
        [
            pltpu.VMEM((2 * bag_owner.shape[1] + 16, samples), I32),
            square,
            pltpu.SemaphoreType.DMA((4,)),
        ],
        me,
        bag_owner.T,
        bag_row.T,
        bag_len,
        route.T,
        in_specs=[pl.BlockSpec(memory_space=pltpu.SMEM)] + hbm(4),
    )
    gate_t = jnp.swapaxes(gate_w, 1, 2)
    wanted = lax.all_to_all(want, both, 0, 0, tiled=True)
    row_shape = slots.shapes()[0]
    exp_shapes = eslots.shapes()
    hot = pltpu.VMEM((slots.rows, entries), BF16)
    rows = pltpu.VMEM((slots.rows, emb), BF16)
    erows = pltpu.VMEM((eslots.rows, width), BF16)
    served = call(
        bind(gather_kernel, slots),
        row_shape,
        [pltpu.VMEM((entries, emb), F32), hot, rows, pltpu.SemaphoreType.DMA(())],
        wanted,
        tables.reshape(entries, emb),
        in_specs=vmem(1) + hbm(1),
    )
    returned = lax.all_to_all(served, both, 0, 0, tiled=True)
    *outgoing, first = call(
        bind(pool_kernel, slots, eslots),
        exp_shapes + [shape((samples, tasks), F32)],
        [rows, pltpu.VMEM((samples, width), BF16), erows],
        returned,
        rank,
        erank,
        gate_t,
    )
    arrived = trade(eslots, outgoing)
    share = w_in.shape[2]
    *result, hidden = call(
        bind(forward_kernel, eslots),
        exp_shapes + [shape((4, eslots.rows, share), BF16)],
        [erows],
        *arrived,
        *ins,
        *outs,
    )
    back = trade(eslots, result)
    logits, dgate, *grads_out = call(
        bind(middle_kernel, eslots),
        [shape((tasks, samples), F32), shape((samples, width), F32)] + exp_shapes,
        [erows, pltpu.VMEM((LANES, samples), F32)],
        *back,
        erank,
        first,
        labels.T,
        head,
        gate_t,
    )
    arrived_grads = trade(eslots, grads_out)
    dinput = call(bind(backward_kernel, eslots), exp_shapes, [erows], *arrived_grads, hidden, *ins, *outs)
    back_grads = trade(eslots, dinput)
    row_out = call(bind(spread_grads_kernel, slots, eslots), row_shape, [erows, rows], *back_grads, erank, dgate, rank)
    row_in = lax.all_to_all(row_out, both, 0, 0, tiled=True)
    new_tables, new_accum = call(
        bind(update_kernel, slots),
        [shape(tables.shape, F32), shape(accum.shape, F32)],
        [pltpu.VMEM(tables.shape, F32), hot, rows, pltpu.SemaphoreType.DMA(())],
        row_in,
        wanted,
        tables,
        accum,
        in_specs=vmem(2) + hbm(1) + vmem(1),
    )
    return (logits.T, new_tables, new_accum)


def solution(mesh):
    in_specs = (
        P(None, ("dp", "expert"), None),
        P(None, ("dp", "expert")),
        P(("dp", "expert"), None),
        P(("dp", "expert"), None),
        P(None, ("dp", "expert")),
        P(("dp", "expert"), None),
        P(("dp", "expert"), None),
        P("expert", None, "dp"),
        P("expert", "dp", None),
        P(),
        P(),
    )
    out_specs = (
        P(("dp", "expert"), None),
        P(None, ("dp", "expert"), None),
        P(None, ("dp", "expert")),
    )

    return jax.shard_map(per_device, mesh=mesh, in_specs=in_specs, out_specs=out_specs, check_vma=False)
```

profile of v0, /device:TPU:0, one launch (start us, length us, event | category | flops | bytes accessed | tf_op | source)
XLA Modules:
  0.0 237.4 jit_solution(2555234139272875768)
XLA Ops:
  3.4 2.7 %shard_map.130 = (f32[4,128,32]{2,1,0:T(8,128)S(1)}, s32[32,128]{1,0:T(8,128)S(1)}, f32[4,128,8]{2,1,0:T(8,128)S(1)}) custom-call(s32[1]{0:T(128)} %bitcast.refs_0_, s32[16,128]{1,0:T(8,128)S(1)} %bitcast.20, s32[16,128]{1,0:T(8,128)S(1)} %bitcast.21, s32[4,128]{1,0:T(4,128)S(1)} %copy-done.12, s32[2,128]{1,0:T(2,128)S(1)} %bitcast.22), custom_call_target="tpu_custom_call" | custom-call | tf_op jit(solution)/shard_map/pallas_call | solution.py:468
  6.8 14.3 %all_to_all.21 = s32[32,1,128]{2,1,0:T(1,128)S(1)} all-to-all(s32[32,1,128]{2,1,0:T(1,128)S(1)} %bitcast.19), channel_id=1, replica_groups=mesh['dp'=4,'expert'=8] {'dp','expert'}, dimensions={0} | all-to-all | bytes 32768 | tf_op jit(solution)/shard_map/all_to_all | solution.py:501
  22.4 3.8 %shard_map.131 = bf16[32,168,128]{2,1,0:T(8,128)(2,1)} custom-call(s32[32,128]{1,0:T(8,128)S(1)} %bitcast.15, f32[1024,256]{1,0:T(8,128)S(1)} %bitcast.14), custom_call_target="tpu_custom_call" | custom-call | tf_op jit(solution)/shard_map/pallas_call | solution.py:468
  26.1 3.6 %all-to-all-start.1 = ((bf16[32,168,128]{2,1,0:T(8,128)(2,1)}), bf16[32,168,128]{2,1,0:T(8,128)(2,1)}, u32[]{:S(2)}, u32[]{:S(2)}) async-start(bf16[32,168,128]{2,1,0:T(8,128)(2,1)} %shard_map.131), calls=%async_computation.1 | async-start | bytes 2752512 | tf_op jit(solution)/shard_map/all_to_all | solution.py:515
  33.9 36.1 %collective-permute-done.8.refs_10_.refs_11_ = bf16[1024,512]{1,0:T(8,128)(2,1)S(1)} collective-permute-done((bf16[1024,512]{1,0:T(8,128)(2,1)}, bf16[1024,512]{1,0:T(8,128)(2,1)S(1)}, u32[]{:S(2)}, u32[]{:S(2)}) %collective-permute-start.8) | collective-permute-done | bytes 1048608 | tf_op jit(solution)/shard_map/ppermute | solution.py:422
  73.0 19.4 %collective-permute-done.12.refs_15_.refs_16_ = bf16[512,1024]{1,0:T(8,128)(2,1)S(1)} collective-permute-done((bf16[512,1024]{1,0:T(8,128)(2,1)}, bf16[512,1024]{1,0:T(8,128)(2,1)S(1)}, u32[]{:S(2)}, u32[]{:S(2)}) %collective-permute-start.12) | collective-permute-done | bytes 1048608 | tf_op jit(solution)/shard_map/ppermute | solution.py:422
  97.5 3.9 %shard_map.132 = (bf16[264,128]{1,0:T(8,128)(2,1)S(1)}, bf16[264,128]{1,0:T(8,128)(2,1)S(1)}, bf16[264,128]{1,0:T(8,128)(2,1)S(1)}, bf16[264,128]{1,0:T(8,128)(2...) custom-call(bf16[32,168,128]{2,1,0:T(8,128)(2,1)} %all-to-all-done.1, ...), custom_call_target="tpu_custom_call" | custom-call | tf_op jit(solution)/shard_map/pallas_call | solution.py:468
  101.5 2.2 collective-permute-done.10.refs_12_.refs_13_
  105.3 9.1 %collective-permute-done.14.refs_17_.refs_18_ = bf16[256,1024]{1,0:T(8,128)(2,1)} collective-permute-done((bf16[256,1024]{1,0:T(8,128)(2,1)}, bf16[256,1024]{1,0:T(8,128)(2,1)}, u32[]{:S(2)}, u32[]{:S(2)}) %collective-permute-start.14) | collective-permute-done | bytes 524320 | tf_op jit(solution)/shard_map/ppermute | solution.py:422
  114.4 2.5 %collective-permute-start.3 = (bf16[264,128]{1,0:T(8,128)(2,1)S(1)}, bf16[264,128]{1,0:T(8,128)(2,1)S(1)}, u32[]{:S(2)}, u32[]{:S(2)}) collective-permute-start(bf16[264,128]{1,0:T(8,128)(2,1)S(1)} %get-tuple-element.51), channel_id=1, source_target_pairs={{0,4},{1,5},{2,6},{3,7},{4,0},{5,1},{6,2},{7,3},{8,12},{9,13},{10,... | collective-permute-start | bytes 202760 | tf_op jit(solution)/shard_map/ppermute | solution.py:437
  116.9 3.0 %collective-permute-start.5 = (bf16[264,128]{1,0:T(8,128)(2,1)S(1)}, bf16[264,128]{1,0:T(8,128)(2,1)S(1)}, u32[]{:S(2)}, u32[]{:S(2)}) collective-permute-start(bf16[264,128]{1,0:T(8,128)(2,1)S(1)} %get-tuple-element.53), channel_id=1, source_target_pairs={{0,6},{1,7},{2,4},{3,5},{4,2},{5,3},{6,0},{7,1},{8,14},{9,15},{10,... | collective-permute-start | bytes 202760 | tf_op jit(solution)/shard_map/ppermute | solution.py:437
  120.7 5.9 %collective-permute-done.4.refs_5_ = bf16[264,128]{1,0:T(8,128)(2,1)S(1)} collective-permute-done((bf16[264,128]{1,0:T(8,128)(2,1)S(1)}, bf16[264,128]{1,0:T(8,128)(2,1)S(1)}, u32[]{:S(2)}, u32[]{:S(2)}) %collective-permute-start.4) | collective-permute-done | bytes 67616 | tf_op jit(solution)/shard_map/ppermute | solution.py:437
  126.6 5.2 %shard_map.133 = (bf16[264,128]{1,0:T(8,128)(2,1)S(1)}, bf16[264,128]{1,0:T(8,128)(2,1)S(1)}, bf16[264,128]{1,0:T(8,128)(2,1)S(1)}, bf16[264,128]{1,0:T(8,128)(2...) custom-call(bf16[264,128]{1,0:T(8,128)(2,1)S(1)} %get-tuple-element., ...), custom_call_target="tpu_custom_call" | custom-call | tf_op jit(solution)/shard_map/pallas_call | solution.py:468
  131.9 3.4 %collective-permute-start.16 = (bf16[264,128]{1,0:T(8,128)(2,1)S(1)}, bf16[264,128]{1,0:T(8,128)(2,1)S(1)}, u32[]{:S(2)}, u32[]{:S(2)}) collective-permute-start(bf16[264,128]{1,0:T(8,128)(2,1)S(1)} %get-tuple-element.57), channel_id=1, source_target_pairs={{0,2},{1,3},{2,0},{3,1},{4,6},{5,7},{6,4},{7,5},{8,10},{9,11},{10,... | collective-permute-start | bytes 202760 | tf_op jit(solution)/shard_map/ppermute | solution.py:437
  135.3 3.0 %collective-permute-start.18 = (bf16[264,128]{1,0:T(8,128)(2,1)S(1)}, bf16[264,128]{1,0:T(8,128)(2,1)S(1)}, u32[]{:S(2)}, u32[]{:S(2)}) collective-permute-start(bf16[264,128]{1,0:T(8,128)(2,1)S(1)} %get-tuple-element.59), channel_id=1, source_target_pairs={{0,4},{1,5},{2,6},{3,7},{4,0},{5,1},{6,2},{7,3},{8,12},{9,13},{10,... | collective-permute-start | bytes 202760 | tf_op jit(solution)/shard_map/ppermute | solution.py:437
  138.5 2.1 collective-permute-start.20
  141.7 6.9 %collective-permute-done.19.refs_5_ = bf16[264,128]{1,0:T(8,128)(2,1)S(1)} collective-permute-done((bf16[264,128]{1,0:T(8,128)(2,1)S(1)}, bf16[264,128]{1,0:T(8,128)(2,1)S(1)}, u32[]{:S(2)}, u32[]{:S(2)}) %collective-permute-start.19) | collective-permute-done | bytes 67616 | tf_op jit(solution)/shard_map/ppermute | solution.py:437
  148.7 3.5 %shard_map.134 = (f32[2,128]{1,0:T(2,128)}, f32[128,1024]{1,0:T(8,128)S(1)}, bf16[264,128]{1,0:T(8,128)(2,1)S(1)}, bf16[264,128]{1,0:T(8,128)(2,1)S(1)}, bf16[26...) custom-call(bf16[264,128]{1,0:T(8,128)(2,1)S(1)} %get-tuple-element., ...), custom_call_target="tpu_custom_call" | custom-call | tf_op jit(solution)/shard_map/pallas_call | solution.py:468
  152.4 3.3 %collective-permute-start.23 = (bf16[264,128]{1,0:T(8,128)(2,1)S(1)}, bf16[264,128]{1,0:T(8,128)(2,1)S(1)}, u32[]{:S(2)}, u32[]{:S(2)}) collective-permute-start(bf16[264,128]{1,0:T(8,128)(2,1)S(1)} %get-tuple-element.67), channel_id=1, source_target_pairs={{0,2},{1,3},{2,0},{3,1},{4,6},{5,7},{6,4},{7,5},{8,10},{9,11},{10,... | collective-permute-start | bytes 202760 | tf_op jit(solution)/shard_map/ppermute | solution.py:437
  155.7 2.1 collective-permute-start.25
  158.1 1.9 collective-permute-start.27
  159.9 2.0 collective-permute-start.28
  161.9 6.5 %collective-permute-done.26.refs_5_ = bf16[264,128]{1,0:T(8,128)(2,1)S(1)} collective-permute-done((bf16[264,128]{1,0:T(8,128)(2,1)S(1)}, bf16[264,128]{1,0:T(8,128)(2,1)S(1)}, u32[]{:S(2)}, u32[]{:S(2)}) %collective-permute-start.26) | collective-permute-done | bytes 67616 | tf_op jit(solution)/shard_map/ppermute | solution.py:437
  168.4 5.2 %shard_map.135 = (bf16[264,128]{1,0:T(8,128)(2,1)S(1)}, bf16[264,128]{1,0:T(8,128)(2,1)S(1)}, bf16[264,128]{1,0:T(8,128)(2,1)S(1)}, bf16[264,128]{1,0:T(8,128)(2...) custom-call(bf16[264,128]{1,0:T(8,128)(2,1)S(1)} %get-tuple-element., ...), custom_call_target="tpu_custom_call" | custom-call | tf_op jit(solution)/shard_map/pallas_call | solution.py:468
  173.8 3.4 %collective-permute-start.30 = (bf16[264,128]{1,0:T(8,128)(2,1)S(1)}, bf16[264,128]{1,0:T(8,128)(2,1)S(1)}, u32[]{:S(2)}, u32[]{:S(2)}) collective-permute-start(bf16[264,128]{1,0:T(8,128)(2,1)S(1)} %get-tuple-element.76), channel_id=1, source_target_pairs={{0,2},{1,3},{2,0},{3,1},{4,6},{5,7},{6,4},{7,5},{8,10},{9,11},{10,... | collective-permute-start | bytes 202760 | tf_op jit(solution)/shard_map/ppermute | solution.py:437
  177.2 2.3 collective-permute-start.32
  179.6 2.0 collective-permute-start.34
  181.6 1.8 collective-permute-start.35
  183.4 6.6 %collective-permute-done.33.refs_5_ = bf16[264,128]{1,0:T(8,128)(2,1)S(1)} collective-permute-done((bf16[264,128]{1,0:T(8,128)(2,1)S(1)}, bf16[264,128]{1,0:T(8,128)(2,1)S(1)}, u32[]{:S(2)}, u32[]{:S(2)}) %collective-permute-start.33) | collective-permute-done | bytes 67616 | tf_op jit(solution)/shard_map/ppermute | solution.py:437
  190.0 4.3 %shard_map.136 = bf16[32,168,128]{2,1,0:T(8,128)(2,1)S(1)} custom-call(bf16[264,128]{1,0:T(8,128)(2,1)S(1)} %get-tuple-element.74.refs_0_, bf16[264,128]{1,0:T(8,128)(2,1)S(1)} %collective-permute-done.29.refs_1_, bf16[264,128]{1,0:T(8,128)(2,1)S(1)} %collective-permute-done.30.refs_2_, bf16[264,128]{1,0:T(8,128)(2,1)S(1)} %collective-permute-done.31.refs_3_, ...), custom_call_target="tpu_custom_call" | custom-call | tf_op jit(solution)/shard_map/pallas_call | solution.py:468
  194.3 39.4 %all_to_all.22.refs_0_ = bf16[32,168,128]{2,1,0:T(8,128)(2,1)S(1)} all-to-all(bf16[32,168,128]{2,1,0:T(8,128)(2,1)S(1)} %shard_map.136), channel_id=1, replica_groups=mesh['dp'=4,'expert'=8] {'dp','expert'}, dimensions={0} | all-to-all | bytes 2752512 | tf_op jit(solution)/shard_map/all_to_all | solution.py:551
  233.7 3.5 %shard_map.137 = (f32[4,256,256]{2,1,0:T(8,128)}, f32[4,256]{1,0:T(4,128)}) custom-call(bf16[32,168,128]{2,1,0:T(8,128)(2,1)S(1)} %all_to_all.22.refs_0_, s32[32,128]{1,0:T(8,128)S(1)} %bitcast.16, f32[4,256,256]{2,1,0:T(8,128)S(1)} %copy-done.3, f32[4,256]{1,0:T(4,128)S(1)} %copy-done.11), custom_call_target="tpu_custom_call" | custom-call | tf_op jit(solution)/shard_map/pallas_call | solution.py:468
  (86 shorter events, 21.7 us)
Async XLA Ops:
  26.1 70.3 %all-to-all-start.1 = ((bf16[32,168,128]{2,1,0:T(8,128)(2,1)}), bf16[32,168,128]{2,1,0:T(8,128)(2,1)}, u32[]{:S(2)}, u32[]{:S(2)}) async-start(bf16[32,168,128]{2,1,0:T(8,128)(2,1)} %shard_map.131), calls=%async_computation.1 | async-start | bytes 2752512 | tf_op jit(solution)/shard_map/all_to_all | solution.py:515
  29.7 40.2 %collective-permute-start.8 = (bf16[1024,512]{1,0:T(8,128)(2,1)}, bf16[1024,512]{1,0:T(8,128)(2,1)S(1)}, u32[]{:S(2)}, u32[]{:S(2)}) collective-permute-start(bf16[1024,512]{1,0:T(8,128)(2,1)} %bitcast.9.refs_8_.refs_9_), channel_id=1, source_target_pairs={{0,16},{8,24},{16,0},{24,8},{1,17},{9,25},{17,1},{25,9},{2,18},{10... | collective-permute-start | bytes 3145736 | tf_op jit(solution)/shard_map/ppermute | solution.py:422
  31.4 40.4 %collective-permute-start.11 = (bf16[512,1024]{1,0:T(8,128)(2,1)}, bf16[512,1024]{1,0:T(8,128)(2,1)S(1)}, u32[]{:S(2)}, u32[]{:S(2)}) collective-permute-start(bf16[512,1024]{1,0:T(8,128)(2,1)} %bitcast.10.refs_13_.refs_14_), channel_id=1, source_target_pairs={{0,8},{8,0},{16,24},{24,16},{1,9},{9,1},{17,25},{25,17},{2,10},{10... | collective-permute-start | bytes 3145736 | tf_op jit(solution)/shard_map/ppermute | solution.py:422
  32.9 59.5 %collective-permute-start.12 = (bf16[512,1024]{1,0:T(8,128)(2,1)}, bf16[512,1024]{1,0:T(8,128)(2,1)S(1)}, u32[]{:S(2)}, u32[]{:S(2)}) collective-permute-start(bf16[512,1024]{1,0:T(8,128)(2,1)} %bitcast.10.refs_13_.refs_14_), channel_id=1, source_target_pairs={{0,16},{8,24},{16,0},{24,8},{1,17},{9,25},{17,1},{25,9},{2,18},{10... | collective-permute-start | bytes 3145736 | tf_op jit(solution)/shard_map/ppermute | solution.py:422
  33.4 60.9 %collective-permute-start.7 = (bf16[1024,512]{1,0:T(8,128)(2,1)}, bf16[1024,512]{1,0:T(8,128)(2,1)S(1)}, u32[]{:S(2)}, u32[]{:S(2)}) collective-permute-start(bf16[1024,512]{1,0:T(8,128)(2,1)} %bitcast.9.refs_8_.refs_9_), channel_id=1, source_target_pairs={{0,8},{8,0},{16,24},{24,16},{1,9},{9,1},{17,25},{25,17},{2,10},{10... | collective-permute-start | bytes 3145736 | tf_op jit(solution)/shard_map/ppermute | solution.py:422
  70.8 33.0 %collective-permute-start.10 = (bf16[512,512]{1,0:T(8,128)(2,1)}, bf16[512,512]{1,0:T(8,128)(2,1)}, u32[]{:S(2)}, u32[]{:S(2)}) collective-permute-start(bf16[512,512]{1,0:T(8,128)(2,1)} %slice.17), channel_id=1, source_target_pairs={{0,8},{8,0},{16,24},{24,16},{1,9},{9,1},{17,25},{25,17},{2,10},{10... | collective-permute-start | bytes 1572872 | tf_op jit(solution)/shard_map/ppermute | solution.py:422
  72.6 32.6 %collective-permute-start.13 = (bf16[256,1024]{1,0:T(8,128)(2,1)}, bf16[256,1024]{1,0:T(8,128)(2,1)}, u32[]{:S(2)}, u32[]{:S(2)}) collective-permute-start(bf16[256,1024]{1,0:T(8,128)(2,1)} %slice.18), channel_id=1, source_target_pairs={{0,16},{8,24},{16,0},{24,8},{1,17},{9,25},{17,1},{25,9},{2,18},{10... | collective-permute-start | bytes 1572872 | tf_op jit(solution)/shard_map/ppermute | solution.py:422
  93.3 21.1 %collective-permute-start.14 = (bf16[256,1024]{1,0:T(8,128)(2,1)}, bf16[256,1024]{1,0:T(8,128)(2,1)}, u32[]{:S(2)}, u32[]{:S(2)}) collective-permute-start(bf16[256,1024]{1,0:T(8,128)(2,1)} %slice.19), channel_id=1, source_target_pairs={{0,8},{8,0},{16,24},{24,16},{1,9},{9,1},{17,25},{25,17},{2,10},{10... | collective-permute-start | bytes 1572872 | tf_op jit(solution)/shard_map/ppermute | solution.py:422
  96.1 20.8 %collective-permute-start.9 = (bf16[512,512]{1,0:T(8,128)(2,1)}, bf16[512,512]{1,0:T(8,128)(2,1)}, u32[]{:S(2)}, u32[]{:S(2)}) collective-permute-start(bf16[512,512]{1,0:T(8,128)(2,1)} %slice.16), channel_id=1, source_target_pairs={{0,16},{8,24},{16,0},{24,8},{1,17},{9,25},{17,1},{25,9},{2,18},{10... | collective-permute-start | bytes 1572872 | tf_op jit(solution)/shard_map/ppermute | solution.py:422
  101.5 15.5 %collective-permute-start = (bf16[264,128]{1,0:T(8,128)(2,1)S(1)}, bf16[264,128]{1,0:T(8,128)(2,1)S(1)}, u32[]{:S(2)}, u32[]{:S(2)}) collective-permute-start(bf16[264,128]{1,0:T(8,128)(2,1)S(1)} %get-tuple-element.48), channel_id=1, source_target_pairs={{0,1},{1,0},{2,3},{3,2},{4,5},{5,4},{6,7},{7,6},{8,9},{9,8},{10,11... | collective-permute-start | bytes 202760 | tf_op jit(solution)/shard_map/ppermute | solution.py:437
  103.7 16.2 %collective-permute-start.1 = (bf16[264,128]{1,0:T(8,128)(2,1)S(1)}, bf16[264,128]{1,0:T(8,128)(2,1)S(1)}, u32[]{:S(2)}, u32[]{:S(2)}) collective-permute-start(bf16[264,128]{1,0:T(8,128)(2,1)S(1)} %get-tuple-element.49), channel_id=1, source_target_pairs={{0,2},{1,3},{2,0},{3,1},{4,6},{5,7},{6,4},{7,5},{8,10},{9,11},{10,... | collective-permute-start | bytes 202760 | tf_op jit(solution)/shard_map/ppermute | solution.py:437
  105.3 15.3 %collective-permute-start.2 = (bf16[264,128]{1,0:T(8,128)(2,1)S(1)}, bf16[264,128]{1,0:T(8,128)(2,1)S(1)}, u32[]{:S(2)}, u32[]{:S(2)}) collective-permute-start(bf16[264,128]{1,0:T(8,128)(2,1)S(1)} %get-tuple-element.50), channel_id=1, source_target_pairs={{0,3},{1,2},{2,1},{3,0},{4,7},{5,6},{6,5},{7,4},{8,11},{9,10},{10,... | collective-permute-start | bytes 202760 | tf_op jit(solution)/shard_map/ppermute | solution.py:437
  114.4 6.3 %collective-permute-start.3 = (bf16[264,128]{1,0:T(8,128)(2,1)S(1)}, bf16[264,128]{1,0:T(8,128)(2,1)S(1)}, u32[]{:S(2)}, u32[]{:S(2)}) collective-permute-start(bf16[264,128]{1,0:T(8,128)(2,1)S(1)} %get-tuple-element.51), channel_id=1, source_target_pairs={{0,4},{1,5},{2,6},{3,7},{4,0},{5,1},{6,2},{7,3},{8,12},{9,13},{10,... | collective-permute-start | bytes 202760 | tf_op jit(solution)/shard_map/ppermute | solution.py:437
  116.9 9.7 %collective-permute-start.4 = (bf16[264,128]{1,0:T(8,128)(2,1)S(1)}, bf16[264,128]{1,0:T(8,128)(2,1)S(1)}, u32[]{:S(2)}, u32[]{:S(2)}) collective-permute-start(bf16[264,128]{1,0:T(8,128)(2,1)S(1)} %get-tuple-element.52), channel_id=1, source_target_pairs={{0,5},{1,4},{2,7},{3,6},{4,1},{5,0},{6,3},{7,2},{8,13},{9,12},{10,... | collective-permute-start | bytes 202760 | tf_op jit(solution)/shard_map/ppermute | solution.py:437
  116.9 9.7 %collective-permute-start.5 = (bf16[264,128]{1,0:T(8,128)(2,1)S(1)}, bf16[264,128]{1,0:T(8,128)(2,1)S(1)}, u32[]{:S(2)}, u32[]{:S(2)}) collective-permute-start(bf16[264,128]{1,0:T(8,128)(2,1)S(1)} %get-tuple-element.53), channel_id=1, source_target_pairs={{0,6},{1,7},{2,4},{3,5},{4,2},{5,3},{6,0},{7,1},{8,14},{9,15},{10,... | collective-permute-start | bytes 202760 | tf_op jit(solution)/shard_map/ppermute | solution.py:437
  119.9 6.7 %collective-permute-start.6 = (bf16[264,128]{1,0:T(8,128)(2,1)S(1)}, bf16[264,128]{1,0:T(8,128)(2,1)S(1)}, u32[]{:S(2)}, u32[]{:S(2)}) collective-permute-start(bf16[264,128]{1,0:T(8,128)(2,1)S(1)} %get-tuple-element.54), channel_id=1, source_target_pairs={{0,7},{1,6},{2,5},{3,4},{4,3},{5,2},{6,1},{7,0},{8,15},{9,14},{10,... | collective-permute-start | bytes 202760 | tf_op jit(solution)/shard_map/ppermute | solution.py:437
  131.8 6.7 %collective-permute-start.15 = (bf16[264,128]{1,0:T(8,128)(2,1)S(1)}, bf16[264,128]{1,0:T(8,128)(2,1)S(1)}, u32[]{:S(2)}, u32[]{:S(2)}) collective-permute-start(bf16[264,128]{1,0:T(8,128)(2,1)S(1)} %get-tuple-element.56), channel_id=1, source_target_pairs={{0,1},{1,0},{2,3},{3,2},{4,5},{5,4},{6,7},{7,6},{8,9},{9,8},{10,11... | collective-permute-start | bytes 202760 | tf_op jit(solution)/shard_map/ppermute | solution.py:437
  131.9 8.7 %collective-permute-start.16 = (bf16[264,128]{1,0:T(8,128)(2,1)S(1)}, bf16[264,128]{1,0:T(8,128)(2,1)S(1)}, u32[]{:S(2)}, u32[]{:S(2)}) collective-permute-start(bf16[264,128]{1,0:T(8,128)(2,1)S(1)} %get-tuple-element.57), channel_id=1, source_target_pairs={{0,2},{1,3},{2,0},{3,1},{4,6},{5,7},{6,4},{7,5},{8,10},{9,11},{10,... | collective-permute-start | bytes 202760 | tf_op jit(solution)/shard_map/ppermute | solution.py:437
  135.3 6.5 %collective-permute-start.17 = (bf16[264,128]{1,0:T(8,128)(2,1)S(1)}, bf16[264,128]{1,0:T(8,128)(2,1)S(1)}, u32[]{:S(2)}, u32[]{:S(2)}) collective-permute-start(bf16[264,128]{1,0:T(8,128)(2,1)S(1)} %get-tuple-element.58), channel_id=1, source_target_pairs={{0,3},{1,2},{2,1},{3,0},{4,7},{5,6},{6,5},{7,4},{8,11},{9,10},{10,... | collective-permute-start | bytes 202760 | tf_op jit(solution)/shard_map/ppermute | solution.py:437
  135.3 6.4 %collective-permute-start.18 = (bf16[264,128]{1,0:T(8,128)(2,1)S(1)}, bf16[264,128]{1,0:T(8,128)(2,1)S(1)}, u32[]{:S(2)}, u32[]{:S(2)}) collective-permute-start(bf16[264,128]{1,0:T(8,128)(2,1)S(1)} %get-tuple-element.59), channel_id=1, source_target_pairs={{0,4},{1,5},{2,6},{3,7},{4,0},{5,1},{6,2},{7,3},{8,12},{9,13},{10,... | collective-permute-start | bytes 202760 | tf_op jit(solution)/shard_map/ppermute | solution.py:437
  138.3 10.4 %collective-permute-start.19 = (bf16[264,128]{1,0:T(8,128)(2,1)S(1)}, bf16[264,128]{1,0:T(8,128)(2,1)S(1)}, u32[]{:S(2)}, u32[]{:S(2)}) collective-permute-start(bf16[264,128]{1,0:T(8,128)(2,1)S(1)} %get-tuple-element.60), channel_id=1, source_target_pairs={{0,5},{1,4},{2,7},{3,6},{4,1},{5,0},{6,3},{7,2},{8,13},{9,12},{10,... | collective-permute-start | bytes 202760 | tf_op jit(solution)/shard_map/ppermute | solution.py:437
  138.5 10.2 %collective-permute-start.20 = (bf16[264,128]{1,0:T(8,128)(2,1)S(1)}, bf16[264,128]{1,0:T(8,128)(2,1)S(1)}, u32[]{:S(2)}, u32[]{:S(2)}) collective-permute-start(bf16[264,128]{1,0:T(8,128)(2,1)S(1)} %get-tuple-element.61), channel_id=1, source_target_pairs={{0,6},{1,7},{2,4},{3,5},{4,2},{5,3},{6,0},{7,1},{8,14},{9,15},{10,... | collective-permute-start | bytes 202760 | tf_op jit(solution)/shard_map/ppermute | solution.py:437
  140.5 8.1 %collective-permute-start.21 = (bf16[264,128]{1,0:T(8,128)(2,1)S(1)}, bf16[264,128]{1,0:T(8,128)(2,1)S(1)}, u32[]{:S(2)}, u32[]{:S(2)}) collective-permute-start(bf16[264,128]{1,0:T(8,128)(2,1)S(1)} %get-tuple-element.62), channel_id=1, source_target_pairs={{0,7},{1,6},{2,5},{3,4},{4,3},{5,2},{6,1},{7,0},{8,15},{9,14},{10,... | collective-permute-start | bytes 202760 | tf_op jit(solution)/shard_map/ppermute | solution.py:437
  152.4 7.5 %collective-permute-start.23 = (bf16[264,128]{1,0:T(8,128)(2,1)S(1)}, bf16[264,128]{1,0:T(8,128)(2,1)S(1)}, u32[]{:S(2)}, u32[]{:S(2)}) collective-permute-start(bf16[264,128]{1,0:T(8,128)(2,1)S(1)} %get-tuple-element.67), channel_id=1, source_target_pairs={{0,2},{1,3},{2,0},{3,1},{4,6},{5,7},{6,4},{7,5},{8,10},{9,11},{10,... | collective-permute-start | bytes 202760 | tf_op jit(solution)/shard_map/ppermute | solution.py:437
  157.8 10.5 %collective-permute-start.26 = (bf16[264,128]{1,0:T(8,128)(2,1)S(1)}, bf16[264,128]{1,0:T(8,128)(2,1)S(1)}, u32[]{:S(2)}, u32[]{:S(2)}) collective-permute-start(bf16[264,128]{1,0:T(8,128)(2,1)S(1)} %get-tuple-element.70), channel_id=1, source_target_pairs={{0,5},{1,4},{2,7},{3,6},{4,1},{5,0},{6,3},{7,2},{8,13},{9,12},{10,... | collective-permute-start | bytes 202760 | tf_op jit(solution)/shard_map/ppermute | solution.py:437
  158.1 10.3 %collective-permute-start.27 = (bf16[264,128]{1,0:T(8,128)(2,1)S(1)}, bf16[264,128]{1,0:T(8,128)(2,1)S(1)}, u32[]{:S(2)}, u32[]{:S(2)}) collective-permute-start(bf16[264,128]{1,0:T(8,128)(2,1)S(1)} %get-tuple-element.71), channel_id=1, source_target_pairs={{0,6},{1,7},{2,4},{3,5},{4,2},{5,3},{6,0},{7,1},{8,14},{9,15},{10,... | collective-permute-start | bytes 202760 | tf_op jit(solution)/shard_map/ppermute | solution.py:437
  159.9 8.4 %collective-permute-start.28 = (bf16[264,128]{1,0:T(8,128)(2,1)S(1)}, bf16[264,128]{1,0:T(8,128)(2,1)S(1)}, u32[]{:S(2)}, u32[]{:S(2)}) collective-permute-start(bf16[264,128]{1,0:T(8,128)(2,1)S(1)} %get-tuple-element.72), channel_id=1, source_target_pairs={{0,7},{1,6},{2,5},{3,4},{4,3},{5,2},{6,1},{7,0},{8,15},{9,14},{10,... | collective-permute-start | bytes 202760 | tf_op jit(solution)/shard_map/ppermute | solution.py:437
  173.8 7.8 %collective-permute-start.30 = (bf16[264,128]{1,0:T(8,128)(2,1)S(1)}, bf16[264,128]{1,0:T(8,128)(2,1)S(1)}, u32[]{:S(2)}, u32[]{:S(2)}) collective-permute-start(bf16[264,128]{1,0:T(8,128)(2,1)S(1)} %get-tuple-element.76), channel_id=1, source_target_pairs={{0,2},{1,3},{2,0},{3,1},{4,6},{5,7},{6,4},{7,5},{8,10},{9,11},{10,... | collective-permute-start | bytes 202760 | tf_op jit(solution)/shard_map/ppermute | solution.py:437
  177.2 6.2 %collective-permute-start.32 = (bf16[264,128]{1,0:T(8,128)(2,1)S(1)}, bf16[264,128]{1,0:T(8,128)(2,1)S(1)}, u32[]{:S(2)}, u32[]{:S(2)}) collective-permute-start(bf16[264,128]{1,0:T(8,128)(2,1)S(1)} %get-tuple-element.78), channel_id=1, source_target_pairs={{0,4},{1,5},{2,6},{3,7},{4,0},{5,1},{6,2},{7,3},{8,12},{9,13},{10,... | collective-permute-start | bytes 202760 | tf_op jit(solution)/shard_map/ppermute | solution.py:437
  179.5 10.5 %collective-permute-start.33 = (bf16[264,128]{1,0:T(8,128)(2,1)S(1)}, bf16[264,128]{1,0:T(8,128)(2,1)S(1)}, u32[]{:S(2)}, u32[]{:S(2)}) collective-permute-start(bf16[264,128]{1,0:T(8,128)(2,1)S(1)} %get-tuple-element.79), channel_id=1, source_target_pairs={{0,5},{1,4},{2,7},{3,6},{4,1},{5,0},{6,3},{7,2},{8,13},{9,12},{10,... | collective-permute-start | bytes 202760 | tf_op jit(solution)/shard_map/ppermute | solution.py:437
  179.6 10.4 %collective-permute-start.34 = (bf16[264,128]{1,0:T(8,128)(2,1)S(1)}, bf16[264,128]{1,0:T(8,128)(2,1)S(1)}, u32[]{:S(2)}, u32[]{:S(2)}) collective-permute-start(bf16[264,128]{1,0:T(8,128)(2,1)S(1)} %get-tuple-element.80), channel_id=1, source_target_pairs={{0,6},{1,7},{2,4},{3,5},{4,2},{5,3},{6,0},{7,1},{8,14},{9,15},{10,... | collective-permute-start | bytes 202760 | tf_op jit(solution)/shard_map/ppermute | solution.py:437
  181.6 8.4 %collective-permute-start.35 = (bf16[264,128]{1,0:T(8,128)(2,1)S(1)}, bf16[264,128]{1,0:T(8,128)(2,1)S(1)}, u32[]{:S(2)}, u32[]{:S(2)}) collective-permute-start(bf16[264,128]{1,0:T(8,128)(2,1)S(1)} %get-tuple-element.81), channel_id=1, source_target_pairs={{0,7},{1,6},{2,5},{3,4},{4,3},{5,2},{6,1},{7,0},{8,15},{9,14},{10,... | collective-permute-start | bytes 202760 | tf_op jit(solution)/shard_map/ppermute | solution.py:437
  (20 other events, 237.7 us)
where the time goes:
time: 238 us; the launch traced here: 237 us
  waiting for transfers between devices  92.8 us (39%)
  blocking collectives  53.7 us (23%)
  starting transfers between devices  47.8 us (20%)
  Pallas kernels  32 us (13%)
  local copies, waits for them, and re-layouts  10 us (4%)
    ppermute x8, waiting for transfers between devices, send(): return lax.ppermute(x, 'dp', [(i, i ^ bit) for i in range(4)])  66.8 us
    all_to_all x1, blocking collectives, per_device(): row_in = lax.all_to_all(row_out, both, 0, 0, tiled=True)  39.4 us
    ppermute x28, starting transfers between devices, trade(): lax.ppermute(chunks[k], 'expert', [(i, i ^ k) for i in range(eslots.peers)])  37.3 us
    pallas_call x8, Pallas kernels, call(): pl.pallas_call(kernel, out_shape=out_shape, in_specs=in_specs or vmem(len...  32 us
    ppermute x28, waiting for transfers between devices, trade(): lax.ppermute(chunks[k], 'expert', [(i, i ^ k) for i in range(eslots.peers)])  26 us
    all_to_all x1, blocking collectives, per_device(): wanted = lax.all_to_all(want, both, 0, 0, tiled=True)  14.3 us
    ppermute x8, starting transfers between devices, send(): return lax.ppermute(x, 'dp', [(i, i ^ bit) for i in range(4)])  6.92 us
    unnamed x30, local copies, waits for them, and re-layouts  6.71 us
  transfers between devices with their start and end apart: 37, of which 9 were waited for; matrix products, arithmetic and copies ran while one was open for 1% of the time, Pallas kernels for 2%

commit v1 on v0

--- a/solution.py
+++ b/solution.py
@@ -96,6 +96,10 @@
         return jnp.where(u == o * self.ext_units + j, 1.0, 0.0).astype(BF16)
 
     def pack(self, block, rows_ref, out_ref):
+        self.pack_main(block, rows_ref, out_ref, range(self.group))
+        self.pack_ext(block, rows_ref, out_ref)
+
+    def pack_main(self, block, rows_ref, out_ref, peers):
         main, first = self.main, block * self.group
 
         def one(o):
@@ -105,7 +109,10 @@
                     pl.ds(start, main), j * LANES : (j + 1) * LANES
                 ]
 
-        seq(self.group, one)
+        seq(len(peers), lambda i: one(peers[0] + i))
+
+    def pack_ext(self, block, rows_ref, out_ref):
+        main, first = self.main, block * self.group
         if self.ext:
             extra = jnp.zeros((self.group * self.ext_units, LANES), F32)
             tail = rows_ref[self.group * main : self.rows, :]
@@ -161,10 +168,30 @@
         hot_ref[group * main : slots.rows, :] = jnp.where(hit, 1.0, 0.0).astype(BF16)
 
 
-def index_kernel(cap, table_rows, me_ref, owner_ref, row_ref, len_ref, route_ref, rank_ref, want_ref, erank_ref, stage_ref, tmp_ref, sems):
-    tables, samples, owners = rank_ref.shape
-    experts = erank_ref.shape[2]
-    columns = owner_ref.shape[0]
+def plan_spans(columns, tables, owners):
+    experts = (columns - tables * owners) // 4
+    base = tables * owners
+    ranks = [(t * owners, (t + 1) * owners) for t in range(tables)]
+    parts = [(base + i * experts, base + (i + 1) * experts) for i in range(4)]
+    return ranks, parts[0:2], parts[2:4]
+
+
+def plan_views(plan_ref, tables, owners):
+    plan = plan_ref[...]
+    spans = plan_spans(plan.shape[1], tables, owners)
+    return [[plan[:, first:last] for first, last in part] for part in spans]
+
+
+def index_kernel(cap, table_rows, me_ref, owner_ref, row_ref, len_ref, route_ref, plan_ref, want_ref, stage_ref, tmp_ref, sems):
+    owners = want_ref.shape[0]
+    tables = len_ref.shape[0]
+    columns, samples = owner_ref.shape
+    ranks, eranks, ehits = plan_spans(plan_ref.shape[1], tables, owners)
+    experts = eranks[0][1] - eranks[0][0]
+
+    def keep(span, value):
+        plan_ref[:, span[0] : span[1]] = value
+
     slots = columns // tables
     lines = (0, columns, 2 * columns, 2 * columns + 8)
     counts = (columns, columns, tables, 2)
@@ -200,7 +227,7 @@
     before = jnp.where(before, 1.0, 0.0).astype(BF16)
     rank = jnp.dot(before, every.astype(BF16), preferred_element_type=F32) + 1.0
     for t in range(tables):
-        rank_ref[t] = named[t] * rank
+        keep(ranks[t], named[t] * rank)
     rank = every * rank
     tmp_ref[...] = jnp.zeros(tmp_ref.shape, F32)
     for r in range(cap):
@@ -211,31 +238,55 @@
     expert = lax.broadcasted_iota(I32, (samples, experts), 1)
     routes = [args[:, 2 * columns + 8 + k : 2 * columns + 9 + k] for k in range(2)]
     for k in range(2):
-        erank_ref[2 + k] = jnp.where(routes[k] == expert.astype(F32), 1.0, 0.0)
+        keep(ehits[k], jnp.where(routes[k] == expert.astype(F32), 1.0, 0.0))
     expert = (expert ^ me_ref[0]).astype(F32)
     hits = [jnp.where(routes[k] == expert, 1.0, 0.0) for k in range(2)]
     rank = jnp.dot(before, (hits[0] + hits[1]).astype(BF16), preferred_element_type=F32) + 1.0
     for k in range(2):
-        erank_ref[k] = hits[k] * rank
-
-
-def gather_kernel(slots, want_ref, table_ref, out_ref, held_ref, hot_ref, rows_ref, sem):
-    copy = pltpu.make_async_copy(table_ref, held_ref, sem)
-    copy.start()
+        keep(eranks[k], hits[k] * rank)
+
+
+def gather_kernel(slots, want_ref, table_ref, out_ref, held_ref, hot_ref, rows_ref, stage_ref, sems):
+    load = pltpu.make_async_copy(table_ref, held_ref, sems.at[0])
+    load.start()
+    steps = 4 if slots.group % 4 == 0 else 1
+    count = slots.group // steps
+    bulk = slots.group * slots.main
+    stores = []
     for block in range(slots.blocks):
         one_hot_rows(slots, block, want_ref, hot_ref)
         if block == 0:
-            copy.wait()
-        rows_ref[...] = jnp.dot(
-            hot_ref[...], held_ref[...].astype(BF16), preferred_element_type=F32
-        ).astype(BF16)
-        slots.pack(block, rows_ref, out_ref)
-
-
-def pool_kernel(slots, eslots, got_ref, rank_ref, erank_ref, gate_ref, *refs):
+            load.wait()
+            table = held_ref[...].astype(BF16)
+
+        def look_up(first, last):
+            rows_ref[first:last, :] = jnp.dot(
+                hot_ref[first:last, :], table, preferred_element_type=F32
+            ).astype(BF16)
+
+        if slots.ext:
+            look_up(bulk, slots.rows)
+            slots.pack_ext(block, rows_ref, stage_ref)
+        for step in range(steps):
+            peers = range(step * count, (step + 1) * count)
+            look_up(peers[0] * slots.main, (peers[-1] + 1) * slots.main)
+            slots.pack_main(block, rows_ref, stage_ref, peers)
+            first = block * slots.group + peers[0]
+            store = pltpu.make_async_copy(
+                stage_ref.at[first : first + count],
+                out_ref.at[first : first + count],
+                sems.at[1 + block * steps + step],
+            )
+            store.start()
+            stores.append(store)
+    for store in stores:
+        store.wait()
+
+
+def pool_kernel(slots, eslots, tables, got_ref, plan_ref, gate_ref, *refs):
     out_ref = eslots.refs(refs)
     first_ref, rows_ref, feat_ref, send_ref = refs[eslots.arrays :]
-    tables = rank_ref.shape[0]
+    ranks, eranks, ehits = plan_views(plan_ref, tables, slots.peers)
     width = slots.width
     group = slots.group
     picks = slots.pick(1)
@@ -244,45 +295,61 @@
         slots.unpack(block, got_ref, rows_ref)
         rows = rows_ref[...]
         for t in range(tables):
-            ranks = rank_ref[t, :, block * group : (block + 1) * group]
-            sums[t] = sums[t] + jnp.dot(slots.spread(ranks, picks), rows, preferred_element_type=F32)
+            held = ranks[t][:, block * group : (block + 1) * group]
+            sums[t] = sums[t] + jnp.dot(slots.spread(held, picks), rows, preferred_element_type=F32)
     for t in range(tables):
         feat_ref[:, t * width : (t + 1) * width] = sums[t].astype(BF16)
     feats = feat_ref[...]
-    eranks = [erank_ref[k] for k in range(2)]
     hot = eslots.spread_t(eranks[0] + eranks[1], eslots.pick(0))
     send_ref[...] = jnp.dot(hot, feats, preferred_element_type=F32).astype(BF16)
     eslots.pack(0, send_ref, out_ref)
     for t in range(first_ref.shape[1]):
         score = lax.dot_general(feats, gate_ref[t], (((1,), (1,)), ((), ())), preferred_element_type=F32)
-        z = [jnp.sum(erank_ref[2 + k] * score, axis=1, keepdims=True) for k in range(2)]
+        z = [jnp.sum(ehits[k] * score, axis=1, keepdims=True) for k in range(2)]
         first_ref[:, t : t + 1] = jax.nn.sigmoid(z[0] - z[1])
 
 
 def forward_kernel(eslots, *refs):
     n = eslots.arrays
     x_ref, refs = eslots.refs(refs), refs[n:]
-    in_refs, out_refs, refs = refs[0:5], refs[5:10], refs[10:]
-    y_ref = eslots.refs(refs)
-    hidden_ref, rows_ref = refs[n:]
+    in_refs, out_refs, refs = refs[0:7], refs[7:12], refs[12:]
+    total_ref, hidden_ref, rows_ref, in_buf, out_buf, sems = refs
+    own = [
+        pltpu.make_async_copy(in_refs[0], in_buf, sems.at[0]),
+        pltpu.make_async_copy(out_refs[0], out_buf, sems.at[1]),
+    ]
+    for copy in own:
+        copy.start()
     eslots.unpack(0, x_ref, rows_ref)
     rows = rows_ref[...]
     half = rows.shape[1] // 2
+    share = hidden_ref.shape[2]
+    dot = lambda a, b: jnp.dot(a, b, preferred_element_type=F32)
     total = 0.0
-    for i in range(4):
-        if i < 3:
-            pre = jnp.dot(rows, in_refs[i][...], preferred_element_type=F32)
+    for i in (1, 2, 3, 0):
+        low, high = 2 * i - 1, 2 * i
+        if i == 0:
+            for copy in own:
+                copy.wait()
+            pre = dot(rows, in_buf[...])
         else:
-            pre = jnp.dot(rows[:, :half], in_refs[3][...], preferred_element_type=F32)
-            pre = pre + jnp.dot(rows[:, half:], in_refs[4][...], preferred_element_type=F32)
+            pre = dot(rows[:, :half], in_refs[low][...]) + dot(rows[:, half:], in_refs[high][...])
         hidden = jnp.maximum(pre, 0.0).astype(BF16)
         hidden_ref[i] = hidden
-        if i < 3:
-            total = total + jnp.dot(hidden, out_refs[i][...], preferred_element_type=F32)
-        else:
-            part = hidden.shape[1] // 2
-            total = total + jnp.dot(hidden[:, :part], out_refs[3][...], preferred_element_type=F32)
-            total = total + jnp.dot(hidden[:, part:], out_refs[4][...], preferred_element_type=F32)
+        if i == 0:
+            total = total + dot(hidden, out_buf[...])
+        elif i < 3:
+            total = total + dot(hidden[:, : share // 2], out_refs[low][...])
+            total = total + dot(hidden[:, share // 2 :], out_refs[high][...])
+    total_ref[...] = total
+
+
+def finish_kernel(eslots, total_ref, hidden_ref, low_ref, high_ref, *refs):
+    y_ref, rows_ref = eslots.refs(refs), refs[eslots.arrays]
+    hidden = hidden_ref[3]
+    half = hidden.shape[1] // 2
+    dot = lambda a, b: jnp.dot(a, b, preferred_element_type=F32)
+    total = total_ref[...] + dot(hidden[:, :half], low_ref[...]) + dot(hidden[:, half:], high_ref[...])
     rows_ref[...] = total.astype(BF16)
     eslots.pack(0, rows_ref, y_ref)
 
@@ -290,31 +357,33 @@
 def backward_kernel(eslots, *refs):
     n = eslots.arrays
     dy_ref, hidden_ref, refs = eslots.refs(refs), refs[n], refs[n + 1 :]
-    in_refs, out_refs, refs = refs[0:5], refs[5:10], refs[10:]
+    in_refs, out_refs, refs = refs[0:7], refs[7:14], refs[14:]
     dx_ref = eslots.refs(refs)
     (rows_ref,) = refs[n:]
     eslots.unpack(0, dy_ref, rows_ref)
     rows = rows_ref[...]
     nt = (((1,), (1,)), ((), ()))
     half = rows.shape[1] // 2
-    dots = lambda a, refs: [lax.dot_general(a, r[...], nt, preferred_element_type=F32) for r in refs]
-    total = low = high = 0.0
+    dot = lambda a, b: lax.dot_general(a, b, nt, preferred_element_type=F32)
+    low = high = 0.0
     for i in range(4):
-        dhidden = jnp.concatenate(dots(rows, out_refs[i : i + 1] if i < 3 else out_refs[3:5]), axis=1)
+        parts = (0,) if i == 0 else (2 * i - 1, 2 * i)
+        dhidden = [dot(rows, out_refs[p][...]) for p in parts]
+        dhidden = dhidden[0] if i == 0 else jnp.concatenate(dhidden, axis=1)
         dpre = jnp.where(hidden_ref[i].astype(F32) > 0.0, dhidden, 0.0).astype(BF16)
-        if i < 3:
-            total = total + dots(dpre, in_refs[i : i + 1])[0]
+        if i == 0:
+            low, high = low + dot(dpre, in_refs[0][:half, :]), high + dot(dpre, in_refs[0][half:, :])
         else:
-            low, high = dots(dpre, in_refs[3:5])
-    rows_ref[:, :half] = (total[:, :half] + low).astype(BF16)
-    rows_ref[:, half:] = (total[:, half:] + high).astype(BF16)
+            low, high = low + dot(dpre, in_refs[parts[0]][...]), high + dot(dpre, in_refs[parts[1]][...])
+    rows_ref[:, :half] = low.astype(BF16)
+    rows_ref[:, half:] = high.astype(BF16)
     eslots.pack(0, rows_ref, dx_ref)
 
 
-def middle_kernel(eslots, *refs):
+def middle_kernel(eslots, tables, owners, *refs):
     n = eslots.arrays
     y_ref, refs = eslots.refs(refs), refs[n:]
-    erank_ref, first_ref, label_ref, head_ref, gate_ref, logit_ref, dgate_ref = refs[0:7]
+    plan_ref, first_ref, label_ref, head_ref, gate_ref, logit_ref, dgate_ref = refs[0:7]
     out_ref = eslots.refs(refs[7:])
     rows_ref, tmp_ref = refs[7 + n :]
     samples, tasks = first_ref.shape
@@ -324,13 +393,13 @@
     width = eslots.width
     eslots.unpack(0, y_ref, rows_ref)
     rows = rows_ref[...]
-    eranks = [erank_ref[k] for k in range(2)]
+    _, eranks, ehits = plan_views(plan_ref, tables, owners)
     picks = eslots.pick(1)
     y0, y1 = [
         jnp.dot(eslots.spread(eranks[k], picks), rows, preferred_element_type=F32) for k in range(2)
     ]
     gap = y0 - y1
-    sign = erank_ref[2] - erank_ref[3]
+    sign = ehits[0] - ehits[1]
     lane = lax.broadcasted_iota(I32, (samples, LANES), 1)
     logits = jnp.zeros((samples, LANES), F32)
     dy0 = dy1 = dgate = 0.0
@@ -367,30 +436,30 @@
     eslots.pack(0, rows_ref, out_ref)
 
 
-def spread_grads_kernel(slots, eslots, *refs):
+def spread_grads_kernel(slots, eslots, tables, *refs):
     dx_ref, refs = eslots.refs(refs), refs[eslots.arrays :]
-    erank_ref, dgate_ref, rank_ref, out_ref, rows_ref, grad_ref = refs
-    tables = rank_ref.shape[0]
+    plan_ref, dgate_ref, out_ref, rows_ref, grad_ref = refs
+    ranks, eranks, _ = plan_views(plan_ref, tables, slots.peers)
     width, group = slots.width, slots.group
     eslots.unpack(0, dx_ref, rows_ref)
-    total = dgate_ref[...] + spread_pair(eslots, erank_ref, rows_ref)
+    total = dgate_ref[...] + spread_pair(eslots, eranks, rows_ref)
     total = total.astype(BF16)
     picks = slots.pick(0)
     for block in range(slots.blocks):
         grads = 0.0
         for t in range(tables):
-            ranks = rank_ref[t, :, block * group : (block + 1) * group]
+            held = ranks[t][:, block * group : (block + 1) * group]
             grads = grads + jnp.dot(
-                slots.spread_t(ranks, picks), total[:, t * width : (t + 1) * width], preferred_element_type=F32
+                slots.spread_t(held, picks), total[:, t * width : (t + 1) * width], preferred_element_type=F32
             )
         grad_ref[...] = grads.astype(BF16)
         slots.pack(block, grad_ref, out_ref)
 
 
-def spread_pair(eslots, erank_ref, rows_ref):
+def spread_pair(eslots, eranks, rows_ref):
     picks = eslots.pick(1)
     rows = rows_ref[...]
-    hot = eslots.spread(erank_ref[0], picks) + eslots.spread(erank_ref[1], picks)
+    hot = eslots.spread(eranks[0], picks) + eslots.spread(eranks[1], picks)
     return jnp.dot(hot, rows, preferred_element_type=F32)
 
 
@@ -415,17 +484,16 @@
         new_table_ref[t] = held_ref[t] - step.T
 
 
-def gather_weight(w):
+def gather_weight(w, later):
     half = w.shape[0] // 2
 
     def send(x, bit):
         return lax.ppermute(x, "dp", [(i, i ^ bit) for i in range(4)])
 
-    by1 = send(w, 1)
-    by2 = send(w, 2)
-    low = send(by1[:half], 2)
-    high = send(by2[half:], 1)
-    return [w, by1, by2, low, high]
+    low, high = w[:half], lax.optimization_barrier((w, later))[0][half:]
+    low1, low2 = send(low, 1), send(low, 2)
+    high1, high2 = send(high, 1), send(high, 2)
+    return [w, low1, high1, low2, high2, send(low1, 2), send(high2, 1)]
 
 
 def trade(eslots, chunks):
@@ -460,16 +528,16 @@
     me = lax.axis_index("expert").astype(I32) if apart else jnp.int32(0)
     me = me.reshape(1)
 
-    ins = gather_weight(w_in[0])
-    outs = gather_weight(w_out[0])
-
-    def call(kernel, out_shape, scratch, *args, in_specs=None):
+    def off(x):
+        return pltpu.with_memory_space_constraint(x, pltpu.HBM)
+
+    def call(kernel, out_shape, scratch, *args, in_specs=None, out_specs=None):
         many = isinstance(out_shape, (list, tuple))
         return pl.pallas_call(
             kernel,
             out_shape=out_shape,
             in_specs=in_specs or vmem(len(args)),
-            out_specs=vmem(len(out_shape)) if many else vmem(1)[0],
+            out_specs=out_specs or (vmem(len(out_shape)) if many else vmem(1)[0]),
             scratch_shapes=scratch,
             compiler_params=params(24 if eslots.rows <= 512 else 60),
         )(*args)
@@ -478,12 +546,11 @@
         return lambda *refs: fn(*static, *refs)
 
     square = pltpu.VMEM((LANES, max(LANES, device_count)), F32)
-    rank, want, erank = call(
+    plan, want = call(
         bind(index_kernel, cap_rows, table_rows),
         [
-            shape((table_count, samples, device_count), F32),
+            shape((samples, table_count * device_count + 4 * expert_count), F32),
             shape((device_count, LANES), I32),
-            shape((4, samples, expert_count), F32),
         ],
         [
             pltpu.VMEM((2 * bag_owner.shape[1] + 16, samples), I32),
@@ -491,63 +558,90 @@
             pltpu.SemaphoreType.DMA((4,)),
         ],
         me,
-        bag_owner.T,
-        bag_row.T,
-        bag_len,
-        route.T,
+        off(bag_owner.T),
+        off(bag_row.T),
+        off(bag_len),
+        off(route.T),
         in_specs=[pl.BlockSpec(memory_space=pltpu.SMEM)] + hbm(4),
     )
+    ins = gather_weight(w_in[0], plan)
+    outs = gather_weight(w_out[0], plan)
     gate_t = jnp.swapaxes(gate_w, 1, 2)
     wanted = lax.all_to_all(want, both, 0, 0, tiled=True)
     row_shape = slots.shapes()[0]
     exp_shapes = eslots.shapes()
+    n = len(exp_shapes)
     hot = pltpu.VMEM((slots.rows, entries), BF16)
     rows = pltpu.VMEM((slots.rows, emb), BF16)
     erows = pltpu.VMEM((eslots.rows, width), BF16)
     served = call(
         bind(gather_kernel, slots),
-        row_shape,
-        [pltpu.VMEM((entries, emb), F32), hot, rows, pltpu.SemaphoreType.DMA(())],
+        pltpu.HBM(row_shape.shape, BF16),
+        [
+            pltpu.VMEM((entries, emb), F32),
+            hot,
+            rows,
+            pltpu.VMEM(row_shape.shape, BF16),
+            pltpu.SemaphoreType.DMA((1 + 4 * slots.blocks,)),
+        ],
         wanted,
-        tables.reshape(entries, emb),
+        off(tables.reshape(entries, emb)),
         in_specs=vmem(1) + hbm(1),
+        out_specs=hbm(1)[0],
     )
     returned = lax.all_to_all(served, both, 0, 0, tiled=True)
     *outgoing, first = call(
-        bind(pool_kernel, slots, eslots),
+        bind(pool_kernel, slots, eslots, table_count),
         exp_shapes + [shape((samples, tasks), F32)],
         [rows, pltpu.VMEM((samples, width), BF16), erows],
         returned,
-        rank,
-        erank,
+        plan,
         gate_t,
     )
     arrived = trade(eslots, outgoing)
     share = w_in.shape[2]
-    *result, hidden = call(
+    own = [
+        pltpu.VMEM((width, share), BF16),
+        pltpu.VMEM((share, width), BF16),
+        pltpu.SemaphoreType.DMA((2,)),
+    ]
+    total, hidden = call(
         bind(forward_kernel, eslots),
-        exp_shapes + [shape((4, eslots.rows, share), BF16)],
-        [erows],
+        [shape((eslots.rows, width), F32), shape((4, eslots.rows, share), BF16)],
+        [erows] + own,
         *arrived,
-        *ins,
-        *outs,
-    )
+        off(ins[0]),
+        *ins[1:],
+        off(outs[0]),
+        *outs[1:5],
+        in_specs=vmem(n) + hbm(1) + vmem(6) + hbm(1) + vmem(4),
+    )
+    result = call(bind(finish_kernel, eslots), exp_shapes, [erows], total, hidden, *outs[5:7])
     back = trade(eslots, result)
     logits, dgate, *grads_out = call(
-        bind(middle_kernel, eslots),
+        bind(middle_kernel, eslots, table_count, device_count),
         [shape((tasks, samples), F32), shape((samples, width), F32)] + exp_shapes,
         [erows, pltpu.VMEM((LANES, samples), F32)],
         *back,
-        erank,
+        plan,
         first,
         labels.T,
         head,
         gate_t,
     )
     arrived_grads = trade(eslots, grads_out)
-    dinput = call(bind(backward_kernel, eslots), exp_shapes, [erows], *arrived_grads, hidden, *ins, *outs)
+    dinput = call(
+        bind(backward_kernel, eslots), exp_shapes, [erows], *arrived_grads, hidden, *ins, *outs
+    )
     back_grads = trade(eslots, dinput)
-    row_out = call(bind(spread_grads_kernel, slots, eslots), row_shape, [erows, rows], *back_grads, erank, dgate, rank)
+    row_out = call(
+        bind(spread_grads_kernel, slots, eslots, table_count),
+        row_shape,
+        [erows, rows],
+        *back_grads,
+        plan,
+        dgate,
+    )
     row_in = lax.all_to_all(row_out, both, 0, 0, tiled=True)
     new_tables, new_accum = call(
         bind(update_kernel, slots),
@@ -555,7 +649,7 @@
         [pltpu.VMEM(tables.shape, F32), hot, rows, pltpu.SemaphoreType.DMA(())],
         row_in,
         wanted,
-        tables,
+        off(tables),
         accum,
         in_specs=vmem(2) + hbm(1) + vmem(1),
     )

time: 238 us -> 228 us (0.958)
  waiting for transfers between devices: 92.8 us -> 79.5 us
  starting transfers between devices: 47.8 us -> 54.8 us
  local copies, waits for them, and re-layouts: 10 us -> 5.98 us
    ppermute x8 -> x12, waiting for transfers between devices: 66.8 us -> 55.8 us  [send(): return lax.ppermute(x, 'dp', [(i, i ^ bit) for i in range(4)])]
    ppermute x8 -> x12, starting transfers between devices: 6.92 us -> 11.3 us  [send(): return lax.ppermute(x, 'dp', [(i, i ^ bit) for i in range(4)])]
    ppermute x28, starting transfers between devices: 37.3 us -> 40.6 us  [trade(): lax.ppermute(chunks[k], 'expert', [(i, i ^ k) for i in range(eslots.peers)])]
    slice x4, local copies, waits for them, and re-layouts: 3.33 us -> 0.93 us  [gather_weight(): low, high = (w[:half], lax.optimization_barrier((w, later))[0][half:])]
    unnamed x30 -> x36, local copies, waits for them, and re-layouts: 6.71 us -> 5.05 us
    pallas_call x8 -> x9, Pallas kernels: 32 us -> 32.4 us  [call(): pl.pallas_call(kernel, out_shape=out_shape, in_specs=in_specs or vmem(len...]
  transfers between devices with their start and end apart: 37 -> 41, of which waited for: 9 -> 12; matrix products, arithmetic and copies ran while one was open for 1% -> 0% of each run, Pallas kernels for 2% -> 3%
where the time goes in v1:
time: 228 us; the launch traced here: 227 us
  waiting for transfers between devices  79.5 us (35%)
  starting transfers between devices  54.8 us (24%)
  blocking collectives  53.4 us (23%)
  Pallas kernels  32.4 us (14%)
  local copies, waits for them, and re-layouts  5.98 us (3%)
    ppermute x12, waiting for transfers between devices, send(): return lax.ppermute(x, 'dp', [(i, i ^ bit) for i in range(4)])  55.8 us
    ppermute x28, starting transfers between devices, trade(): lax.ppermute(chunks[k], 'expert', [(i, i ^ k) for i in range(eslots.peers)])  40.6 us
    all_to_all x1, blocking collectives, per_device(): row_in = lax.all_to_all(row_out, both, 0, 0, tiled=True)  39.1 us
    pallas_call x9, Pallas kernels, call(): pl.pallas_call(kernel, out_shape=out_shape, in_specs=in_specs or vmem(len...  32.4 us
    ppermute x28, waiting for transfers between devices, trade(): lax.ppermute(chunks[k], 'expert', [(i, i ^ k) for i in range(eslots.peers)])  23.8 us
    all_to_all x1, blocking collectives, per_device(): wanted = lax.all_to_all(want, both, 0, 0, tiled=True)  14.3 us
    ppermute x12, starting transfers between devices, send(): return lax.ppermute(x, 'dp', [(i, i ^ bit) for i in range(4)])  11.3 us
    unnamed x36, local copies, waits for them, and re-layouts  5.05 us
  transfers between devices with their start and end apart: 41, of which 12 were waited for; matrix products, arithmetic and copies ran while one was open for 0% of the time, Pallas kernels for 3%

profile of v1, /device:TPU:0, one launch (start us, length us, event | category | flops | bytes accessed | tf_op | source)
XLA Modules:
  0.0 227.4 jit_solution(11126578935733943327)
XLA Ops:
  0.6 3.6 %shard_map.130 = (f32[128,160]{1,0:T(8,128)S(1)}, s32[32,128]{1,0:T(8,128)S(1)}) custom-call(s32[1]{0:T(128)} %bitcast.refs_0_, s32[16,128]{1,0:T(8,128)} %bitcast.31, s32[16,128]{1,0:T(8,128)} %bitcast.32, s32[4,128]{1,0:T(4,128)} %refs_3_.2, s32[2,128]{1,0:T(2,128)} %bitcast.33), custom_call_target="tpu_custom_call" | custom-call | tf_op jit(solution)/shard_map/pallas_call | solution.py:536
  4.9 14.3 %all_to_all.21 = s32[32,1,128]{2,1,0:T(1,128)S(1)} all-to-all(s32[32,1,128]{2,1,0:T(1,128)S(1)} %bitcast.28), channel_id=1, replica_groups=mesh['dp'=4,'expert'=8] {'dp','expert'}, dimensions={0} | all-to-all | bytes 32768 | tf_op jit(solution)/shard_map/all_to_all | solution.py:570
  19.2 4.2 %shard_map.131 = bf16[32,168,128]{2,1,0:T(8,128)(2,1)} custom-call(s32[32,128]{1,0:T(8,128)S(1)} %bitcast.24, f32[1024,256]{1,0:T(8,128)} %bitcast.30), custom_call_target="tpu_custom_call" | custom-call | tf_op jit(solution)/shard_map/pallas_call | solution.py:536
  23.5 3.0 %all-to-all-start.1 = ((bf16[32,168,128]{2,1,0:T(8,128)(2,1)}), bf16[32,168,128]{2,1,0:T(8,128)(2,1)S(1)}, u32[]{:S(2)}, u32[]{:S(2)}) async-start(bf16[32,168,128]{2,1,0:T(8,128)(2,1)} %shard_map.131), calls=%async_computation.1 | async-start | bytes 2752512 | tf_op jit(solution)/shard_map/all_to_all | solution.py:592
  33.3 20.3 %collective-permute-done.15.refs_18_.refs_19_ = bf16[256,1024]{1,0:T(8,128)(2,1)S(1)} collective-permute-done((bf16[256,1024]{1,0:T(8,128)(2,1)S(1)}, bf16[256,1024]{1,0:T(8,128)(2,1)S(1)}, u32[]{:S(2)}, u32[]{:S(2)}) %collective-permute-start.15) | collective-permute-done | bytes 524320 | tf_op jit(solution)/shard_map/ppermute | solution.py:491
  56.0 10.8 %collective-permute-done.9.refs_11_.refs_12_ = bf16[512,512]{1,0:T(8,128)(2,1)S(1)} collective-permute-done((bf16[512,512]{1,0:T(8,128)(2,1)S(1)}, bf16[512,512]{1,0:T(8,128)(2,1)S(1)}, u32[]{:S(2)}, u32[]{:S(2)}) %collective-permute-start.9) | collective-permute-done | bytes 524320 | tf_op jit(solution)/shard_map/ppermute | solution.py:491
  69.0 9.1 %collective-permute-done.10.refs_12_.refs_13_ = bf16[512,512]{1,0:T(8,128)(2,1)} collective-permute-done((bf16[512,512]{1,0:T(8,128)(2,1)}, bf16[512,512]{1,0:T(8,128)(2,1)}, u32[]{:S(2)}, u32[]{:S(2)}) %collective-permute-start.10) | collective-permute-done | bytes 524320 | tf_op jit(solution)/shard_map/ppermute | solution.py:491
  79.1 10.2 %collective-permute-done.16.refs_19_.refs_20_ = bf16[256,1024]{1,0:T(8,128)(2,1)} collective-permute-done((bf16[256,1024]{1,0:T(8,128)(2,1)S(1)}, bf16[256,1024]{1,0:T(8,128)(2,1)}, u32[]{:S(2)}, u32[]{:S(2)}) %collective-permute-start.16) | collective-permute-done | bytes 524320 | tf_op jit(solution)/shard_map/ppermute | solution.py:491
  92.5 2.7 %shard_map.132 = (bf16[264,128]{1,0:T(8,128)(2,1)S(1)}, bf16[264,128]{1,0:T(8,128)(2,1)S(1)}, bf16[264,128]{1,0:T(8,128)(2,1)S(1)}, bf16[264,128]{1,0:T(8,128)(2...) custom-call(bf16[32,168,128]{2,1,0:T(8,128)(2,1)S(1)} %all-to-all-do, ...), custom_call_target="tpu_custom_call" | custom-call | tf_op jit(solution)/shard_map/pallas_call | solution.py:536
  95.3 5.3 %collective-permute-done.11.refs_13_.refs_14_ = bf16[512,512]{1,0:T(8,128)(2,1)} collective-permute-done((bf16[512,512]{1,0:T(8,128)(2,1)}, bf16[512,512]{1,0:T(8,128)(2,1)}, u32[]{:S(2)}, u32[]{:S(2)}) %collective-permute-start.11) | collective-permute-done | bytes 524320 | tf_op jit(solution)/shard_map/ppermute | solution.py:491
  102.1 2.6 %collective-permute-start.3 = (bf16[264,128]{1,0:T(8,128)(2,1)S(1)}, bf16[264,128]{1,0:T(8,128)(2,1)S(1)}, u32[]{:S(2)}, u32[]{:S(2)}) collective-permute-start(bf16[264,128]{1,0:T(8,128)(2,1)S(1)} %get-tuple-element.52), channel_id=1, source_target_pairs={{0,4},{1,5},{2,6},{3,7},{4,0},{5,1},{6,2},{7,3},{8,12},{9,13},{10,... | collective-permute-start | bytes 202760 | tf_op jit(solution)/shard_map/ppermute | solution.py:505
  106.3 2.7 %collective-permute-start.5 = (bf16[264,128]{1,0:T(8,128)(2,1)S(1)}, bf16[264,128]{1,0:T(8,128)(2,1)S(1)}, u32[]{:S(2)}, u32[]{:S(2)}) collective-permute-start(bf16[264,128]{1,0:T(8,128)(2,1)S(1)} %get-tuple-element.54), channel_id=1, source_target_pairs={{0,6},{1,7},{2,4},{3,5},{4,2},{5,3},{6,0},{7,1},{8,14},{9,15},{10,... | collective-permute-start | bytes 202760 | tf_op jit(solution)/shard_map/ppermute | solution.py:505
  109.0 4.5 %collective-permute-start.6 = (bf16[264,128]{1,0:T(8,128)(2,1)S(1)}, bf16[264,128]{1,0:T(8,128)(2,1)S(1)}, u32[]{:S(2)}, u32[]{:S(2)}) collective-permute-start(bf16[264,128]{1,0:T(8,128)(2,1)S(1)} %get-tuple-element.55), channel_id=1, source_target_pairs={{0,7},{1,6},{2,5},{3,4},{4,3},{5,2},{6,1},{7,0},{8,15},{9,14},{10,... | collective-permute-start | bytes 202760 | tf_op jit(solution)/shard_map/ppermute | solution.py:505
  114.0 1.7 collective-permute-done.6.refs_7_
  116.8 4.7 %shard_map.133 = (f32[264,1024]{1,0:T(8,128)S(1)}, bf16[4,264,512]{2,1,0:T(8,128)(2,1)S(1)}) custom-call(bf16[264,128]{1,0:T(8,128)(2,1)S(1)} %get-tuple-element.48.refs_0_, bf16[264,128]{1,0:T(8,128)(2,1)S(1)} %collective-permute-done.refs_1_, bf16[264,128]{1,0:T(8,128)(2,1)S(1)} %collective-permute-done.1.refs_2_, ...), custom_call_target="tpu_custom_call" | custom-call | tf_op jit(solution)/shard_map/pallas_call | solution.py:536
  122.7 3.0 %collective-permute-start.20 = (bf16[264,128]{1,0:T(8,128)(2,1)S(1)}, bf16[264,128]{1,0:T(8,128)(2,1)S(1)}, u32[]{:S(2)}, u32[]{:S(2)}) collective-permute-start(bf16[264,128]{1,0:T(8,128)(2,1)S(1)} %get-tuple-element.62), channel_id=1, source_target_pairs={{0,2},{1,3},{2,0},{3,1},{4,6},{5,7},{6,4},{7,5},{8,10},{9,11},{10,... | collective-permute-start | bytes 202760 | tf_op jit(solution)/shard_map/ppermute | solution.py:505
  125.7 2.6 %collective-permute-start.22 = (bf16[264,128]{1,0:T(8,128)(2,1)S(1)}, bf16[264,128]{1,0:T(8,128)(2,1)S(1)}, u32[]{:S(2)}, u32[]{:S(2)}) collective-permute-start(bf16[264,128]{1,0:T(8,128)(2,1)S(1)} %get-tuple-element.64), channel_id=1, source_target_pairs={{0,4},{1,5},{2,6},{3,7},{4,0},{5,1},{6,2},{7,3},{8,12},{9,13},{10,... | collective-permute-start | bytes 202760 | tf_op jit(solution)/shard_map/ppermute | solution.py:505
  128.2 2.2 collective-permute-start.24
  131.9 6.9 %collective-permute-done.23.refs_5_ = bf16[264,128]{1,0:T(8,128)(2,1)S(1)} collective-permute-done((bf16[264,128]{1,0:T(8,128)(2,1)S(1)}, bf16[264,128]{1,0:T(8,128)(2,1)S(1)}, u32[]{:S(2)}, u32[]{:S(2)}) %collective-permute-start.23) | collective-permute-done | bytes 67616 | tf_op jit(solution)/shard_map/ppermute | solution.py:505
  138.8 3.6 %shard_map.135 = (f32[2,128]{1,0:T(2,128)}, f32[128,1024]{1,0:T(8,128)S(1)}, bf16[264,128]{1,0:T(8,128)(2,1)S(1)}, bf16[264,128]{1,0:T(8,128)(2,1)S(1)}, bf16[26...) custom-call(bf16[264,128]{1,0:T(8,128)(2,1)S(1)} %get-tuple-element., ...), custom_call_target="tpu_custom_call" | custom-call | tf_op jit(solution)/shard_map/pallas_call | solution.py:536
  142.6 3.4 %collective-permute-start.27 = (bf16[264,128]{1,0:T(8,128)(2,1)S(1)}, bf16[264,128]{1,0:T(8,128)(2,1)S(1)}, u32[]{:S(2)}, u32[]{:S(2)}) collective-permute-start(bf16[264,128]{1,0:T(8,128)(2,1)S(1)} %get-tuple-element.72), channel_id=1, source_target_pairs={{0,2},{1,3},{2,0},{3,1},{4,6},{5,7},{6,4},{7,5},{8,10},{9,11},{10,... | collective-permute-start | bytes 202760 | tf_op jit(solution)/shard_map/ppermute | solution.py:505
  146.0 1.9 collective-permute-start.29
  150.1 2.1 collective-permute-start.32
  152.2 6.3 %collective-permute-done.30.refs_5_ = bf16[264,128]{1,0:T(8,128)(2,1)S(1)} collective-permute-done((bf16[264,128]{1,0:T(8,128)(2,1)S(1)}, bf16[264,128]{1,0:T(8,128)(2,1)S(1)}, u32[]{:S(2)}, u32[]{:S(2)}) %collective-permute-start.30) | collective-permute-done | bytes 67616 | tf_op jit(solution)/shard_map/ppermute | solution.py:505
  158.6 5.0 %shard_map.136 = (bf16[264,128]{1,0:T(8,128)(2,1)S(1)}, bf16[264,128]{1,0:T(8,128)(2,1)S(1)}, bf16[264,128]{1,0:T(8,128)(2,1)S(1)}, bf16[264,128]{1,0:T(8,128)(2...) custom-call(bf16[264,128]{1,0:T(8,128)(2,1)S(1)} %get-tuple-element., ...), custom_call_target="tpu_custom_call" | custom-call | tf_op jit(solution)/shard_map/pallas_call | solution.py:536
  164.0 3.4 %collective-permute-start.34 = (bf16[264,128]{1,0:T(8,128)(2,1)S(1)}, bf16[264,128]{1,0:T(8,128)(2,1)S(1)}, u32[]{:S(2)}, u32[]{:S(2)}) collective-permute-start(bf16[264,128]{1,0:T(8,128)(2,1)S(1)} %get-tuple-element.80), channel_id=1, source_target_pairs={{0,2},{1,3},{2,0},{3,1},{4,6},{5,7},{6,4},{7,5},{8,10},{9,11},{10,... | collective-permute-start | bytes 202760 | tf_op jit(solution)/shard_map/ppermute | solution.py:505
  167.4 2.4 %collective-permute-start.36 = (bf16[264,128]{1,0:T(8,128)(2,1)S(1)}, bf16[264,128]{1,0:T(8,128)(2,1)S(1)}, u32[]{:S(2)}, u32[]{:S(2)}) collective-permute-start(bf16[264,128]{1,0:T(8,128)(2,1)S(1)} %get-tuple-element.82), channel_id=1, source_target_pairs={{0,4},{1,5},{2,6},{3,7},{4,0},{5,1},{6,2},{7,3},{8,12},{9,13},{10,... | collective-permute-start | bytes 202760 | tf_op jit(solution)/shard_map/ppermute | solution.py:505
  169.8 2.1 collective-permute-start.38
  173.6 6.7 %collective-permute-done.37.refs_5_ = bf16[264,128]{1,0:T(8,128)(2,1)S(1)} collective-permute-done((bf16[264,128]{1,0:T(8,128)(2,1)S(1)}, bf16[264,128]{1,0:T(8,128)(2,1)S(1)}, u32[]{:S(2)}, u32[]{:S(2)}) %collective-permute-start.37) | collective-permute-done | bytes 67616 | tf_op jit(solution)/shard_map/ppermute | solution.py:505
  180.3 4.3 %shard_map.137 = bf16[32,168,128]{2,1,0:T(8,128)(2,1)S(1)} custom-call(bf16[264,128]{1,0:T(8,128)(2,1)S(1)} %get-tuple-element.78.refs_0_, bf16[264,128]{1,0:T(8,128)(2,1)S(1)} %collective-permute-done.33.refs_1_, bf16[264,128]{1,0:T(8,128)(2,1)S(1)} %collective-permute-done.34.refs_2_, bf16[264,128]{1,0:T(8,128)(2,1)S(1)} %collective-permute-done.35.refs_3_, ...), custom_call_target="tpu_custom_call" | custom-call | tf_op jit(solution)/shard_map/pallas_call | solution.py:536
  184.6 39.1 %all_to_all.22.refs_0_ = bf16[32,168,128]{2,1,0:T(8,128)(2,1)S(1)} all-to-all(bf16[32,168,128]{2,1,0:T(8,128)(2,1)S(1)} %shard_map.137), channel_id=1, replica_groups=mesh['dp'=4,'expert'=8] {'dp','expert'}, dimensions={0} | all-to-all | bytes 2752512 | tf_op jit(solution)/shard_map/all_to_all | solution.py:645
  223.7 3.5 %shard_map.138 = (f32[4,256,256]{2,1,0:T(8,128)}, f32[4,256]{1,0:T(4,128)}) custom-call(bf16[32,168,128]{2,1,0:T(8,128)(2,1)S(1)} %all_to_all.22.refs_0_, s32[32,128]{1,0:T(8,128)S(1)} %bitcast.25, f32[4,256,256]{2,1,0:T(8,128)} %refs_2_.1, f32[4,256]{1,0:T(4,128)S(1)} %copy-done.16), custom_call_target="tpu_custom_call" | custom-call | tf_op jit(solution)/shard_map/pallas_call | solution.py:536
  (101 shorter events, 27.7 us)
Async XLA Ops:
  23.5 68.1 %all-to-all-start.1 = ((bf16[32,168,128]{2,1,0:T(8,128)(2,1)}), bf16[32,168,128]{2,1,0:T(8,128)(2,1)S(1)}, u32[]{:S(2)}, u32[]{:S(2)}) async-start(bf16[32,168,128]{2,1,0:T(8,128)(2,1)} %shard_map.131), calls=%async_computation.1 | async-start | bytes 2752512 | tf_op jit(solution)/shard_map/all_to_all | solution.py:592
  26.5 27.1 %collective-permute-start.15 = (bf16[256,1024]{1,0:T(8,128)(2,1)S(1)}, bf16[256,1024]{1,0:T(8,128)(2,1)S(1)}, u32[]{:S(2)}, u32[]{:S(2)}) collective-permute-start(bf16[256,1024]{1,0:T(8,128)(2,1)S(1)} %slice_bitcast_fusion), channel_id=1, source_target_pairs={{0,16},{8,24},{16,0},{24,8},{1,17},{9,25},{17,1},{25,9},{2,18},{10... | collective-permute-start | bytes 1572872 | tf_op jit(solution)/shard_map/ppermute | solution.py:491
  28.2 26.2 %collective-permute-start.13 = (bf16[256,1024]{1,0:T(8,128)(2,1)S(1)}, bf16[256,1024]{1,0:T(8,128)(2,1)}, u32[]{:S(2)}, u32[]{:S(2)}) collective-permute-start(bf16[256,1024]{1,0:T(8,128)(2,1)S(1)} %slice_bitcast_fusion), channel_id=1, source_target_pairs={{0,8},{8,0},{16,24},{24,16},{1,9},{9,1},{17,25},{25,17},{2,10},{10... | collective-permute-start | bytes 1572872 | tf_op jit(solution)/shard_map/ppermute | solution.py:491
  29.8 37.0 %collective-permute-start.9 = (bf16[512,512]{1,0:T(8,128)(2,1)S(1)}, bf16[512,512]{1,0:T(8,128)(2,1)S(1)}, u32[]{:S(2)}, u32[]{:S(2)}) collective-permute-start(bf16[512,512]{1,0:T(8,128)(2,1)S(1)} %slice_bitcast_fusion.1), channel_id=1, source_target_pairs={{0,16},{8,24},{16,0},{24,8},{1,17},{9,25},{17,1},{25,9},{2,18},{10... | collective-permute-start | bytes 1572872 | tf_op jit(solution)/shard_map/ppermute | solution.py:491
  30.4 38.2 %collective-permute-start.7 = (bf16[512,512]{1,0:T(8,128)(2,1)S(1)}, bf16[512,512]{1,0:T(8,128)(2,1)}, u32[]{:S(2)}, u32[]{:S(2)}) collective-permute-start(bf16[512,512]{1,0:T(8,128)(2,1)S(1)} %slice_bitcast_fusion.1), channel_id=1, source_target_pairs={{0,8},{8,0},{16,24},{24,16},{1,9},{9,1},{17,25},{25,17},{2,10},{10... | collective-permute-start | bytes 1572872 | tf_op jit(solution)/shard_map/ppermute | solution.py:491
  31.6 46.6 %collective-permute-start.10 = (bf16[512,512]{1,0:T(8,128)(2,1)}, bf16[512,512]{1,0:T(8,128)(2,1)}, u32[]{:S(2)}, u32[]{:S(2)}) collective-permute-start(bf16[512,512]{1,0:T(8,128)(2,1)} %slice.20), channel_id=1, source_target_pairs={{0,16},{8,24},{16,0},{24,8},{1,17},{9,25},{17,1},{25,9},{2,18},{10... | collective-permute-start | bytes 1572872 | tf_op jit(solution)/shard_map/ppermute | solution.py:491
  54.4 35.0 %collective-permute-start.16 = (bf16[256,1024]{1,0:T(8,128)(2,1)S(1)}, bf16[256,1024]{1,0:T(8,128)(2,1)}, u32[]{:S(2)}, u32[]{:S(2)}) collective-permute-start(bf16[256,1024]{1,0:T(8,128)(2,1)S(1)} %slice.23), channel_id=1, source_target_pairs={{0,16},{8,24},{16,0},{24,8},{1,17},{9,25},{17,1},{25,9},{2,18},{10... | collective-permute-start | bytes 1572872 | tf_op jit(solution)/shard_map/ppermute | solution.py:491
  54.5 35.0 %collective-permute-start.14 = (bf16[256,1024]{1,0:T(8,128)(2,1)S(1)}, bf16[256,1024]{1,0:T(8,128)(2,1)S(1)}, u32[]{:S(2)}, u32[]{:S(2)}) collective-permute-start(bf16[256,1024]{1,0:T(8,128)(2,1)S(1)} %slice.23), channel_id=1, source_target_pairs={{0,8},{8,0},{16,24},{24,16},{1,9},{9,1},{17,25},{25,17},{2,10},{10... | collective-permute-start | bytes 1572872 | tf_op jit(solution)/shard_map/ppermute | solution.py:491
  67.6 27.6 %collective-permute-start.8 = (bf16[512,512]{1,0:T(8,128)(2,1)}, bf16[512,512]{1,0:T(8,128)(2,1)}, u32[]{:S(2)}, u32[]{:S(2)}) collective-permute-start(bf16[512,512]{1,0:T(8,128)(2,1)} %slice.20), channel_id=1, source_target_pairs={{0,8},{8,0},{16,24},{24,16},{1,9},{9,1},{17,25},{25,17},{2,10},{10... | collective-permute-start | bytes 1572872 | tf_op jit(solution)/shard_map/ppermute | solution.py:491
  68.6 32.0 %collective-permute-start.11 = (bf16[512,512]{1,0:T(8,128)(2,1)}, bf16[512,512]{1,0:T(8,128)(2,1)}, u32[]{:S(2)}, u32[]{:S(2)}) collective-permute-start(bf16[512,512]{1,0:T(8,128)(2,1)} %collective-permute-done.7.refs_9_.refs_10_), channel_id=1, source_target_pairs={{0,16},{8,24},{16,0},{24,8},{1,17},{9,25},{17,1},{25,9},{2,18},{10... | collective-permute-start | bytes 1572872 | tf_op jit(solution)/shard_map/ppermute | solution.py:491
  78.1 24.0 %collective-permute-start.12 = (bf16[512,512]{1,0:T(8,128)(2,1)}, bf16[512,512]{1,0:T(8,128)(2,1)}, u32[]{:S(2)}, u32[]{:S(2)}) collective-permute-start(bf16[512,512]{1,0:T(8,128)(2,1)} %collective-permute-done.10.refs_12_.refs_13_), channel_id=1, source_target_pairs={{0,8},{8,0},{16,24},{24,16},{1,9},{9,1},{17,25},{25,17},{2,10},{10... | collective-permute-start | bytes 1572872 | tf_op jit(solution)/shard_map/ppermute | solution.py:491
  89.4 32.2 %collective-permute-start.17 = (bf16[256,1024]{1,0:T(8,128)(2,1)}, bf16[256,1024]{1,0:T(8,128)(2,1)S(1)}, u32[]{:S(2)}, u32[]{:S(2)}) collective-permute-start(bf16[256,1024]{1,0:T(8,128)(2,1)} %collective-permute-done.13.refs_16_.refs_17_), channel_id=1, source_target_pairs={{0,16},{8,24},{16,0},{24,8},{1,17},{9,25},{17,1},{25,9},{2,18},{10... | collective-permute-start | bytes 1572872 | tf_op jit(solution)/shard_map/ppermute | solution.py:491
  90.2 31.4 %collective-permute-start.18 = (bf16[256,1024]{1,0:T(8,128)(2,1)}, bf16[256,1024]{1,0:T(8,128)(2,1)S(1)}, u32[]{:S(2)}, u32[]{:S(2)}) collective-permute-start(bf16[256,1024]{1,0:T(8,128)(2,1)} %collective-permute-done.16.refs_19_.refs_20_), channel_id=1, source_target_pairs={{0,8},{8,0},{16,24},{24,16},{1,9},{9,1},{17,25},{25,17},{2,10},{10... | collective-permute-start | bytes 1572872 | tf_op jit(solution)/shard_map/ppermute | solution.py:491
  95.2 6.9 %collective-permute-start = (bf16[264,128]{1,0:T(8,128)(2,1)S(1)}, bf16[264,128]{1,0:T(8,128)(2,1)S(1)}, u32[]{:S(2)}, u32[]{:S(2)}) collective-permute-start(bf16[264,128]{1,0:T(8,128)(2,1)S(1)} %get-tuple-element.49), channel_id=1, source_target_pairs={{0,1},{1,0},{2,3},{3,2},{4,5},{5,4},{6,7},{7,6},{8,9},{9,8},{10,11... | collective-permute-start | bytes 202760 | tf_op jit(solution)/shard_map/ppermute | solution.py:505
  102.1 6.9 %collective-permute-start.3 = (bf16[264,128]{1,0:T(8,128)(2,1)S(1)}, bf16[264,128]{1,0:T(8,128)(2,1)S(1)}, u32[]{:S(2)}, u32[]{:S(2)}) collective-permute-start(bf16[264,128]{1,0:T(8,128)(2,1)S(1)} %get-tuple-element.52), channel_id=1, source_target_pairs={{0,4},{1,5},{2,6},{3,7},{4,0},{5,1},{6,2},{7,3},{8,12},{9,13},{10,... | collective-permute-start | bytes 202760 | tf_op jit(solution)/shard_map/ppermute | solution.py:505
  104.9 9.2 %collective-permute-start.4 = (bf16[264,128]{1,0:T(8,128)(2,1)S(1)}, bf16[264,128]{1,0:T(8,128)(2,1)S(1)}, u32[]{:S(2)}, u32[]{:S(2)}) collective-permute-start(bf16[264,128]{1,0:T(8,128)(2,1)S(1)} %get-tuple-element.53), channel_id=1, source_target_pairs={{0,5},{1,4},{2,7},{3,6},{4,1},{5,0},{6,3},{7,2},{8,13},{9,12},{10,... | collective-permute-start | bytes 202760 | tf_op jit(solution)/shard_map/ppermute | solution.py:505
  106.3 7.7 %collective-permute-start.5 = (bf16[264,128]{1,0:T(8,128)(2,1)S(1)}, bf16[264,128]{1,0:T(8,128)(2,1)S(1)}, u32[]{:S(2)}, u32[]{:S(2)}) collective-permute-start(bf16[264,128]{1,0:T(8,128)(2,1)S(1)} %get-tuple-element.54), channel_id=1, source_target_pairs={{0,6},{1,7},{2,4},{3,5},{4,2},{5,3},{6,0},{7,1},{8,14},{9,15},{10,... | collective-permute-start | bytes 202760 | tf_op jit(solution)/shard_map/ppermute | solution.py:505
  109.0 6.8 %collective-permute-start.6 = (bf16[264,128]{1,0:T(8,128)(2,1)S(1)}, bf16[264,128]{1,0:T(8,128)(2,1)S(1)}, u32[]{:S(2)}, u32[]{:S(2)}) collective-permute-start(bf16[264,128]{1,0:T(8,128)(2,1)S(1)} %get-tuple-element.55), channel_id=1, source_target_pairs={{0,7},{1,6},{2,5},{3,4},{4,3},{5,2},{6,1},{7,0},{8,15},{9,14},{10,... | collective-permute-start | bytes 202760 | tf_op jit(solution)/shard_map/ppermute | solution.py:505
  122.7 7.8 %collective-permute-start.20 = (bf16[264,128]{1,0:T(8,128)(2,1)S(1)}, bf16[264,128]{1,0:T(8,128)(2,1)S(1)}, u32[]{:S(2)}, u32[]{:S(2)}) collective-permute-start(bf16[264,128]{1,0:T(8,128)(2,1)S(1)} %get-tuple-element.62), channel_id=1, source_target_pairs={{0,2},{1,3},{2,0},{3,1},{4,6},{5,7},{6,4},{7,5},{8,10},{9,11},{10,... | collective-permute-start | bytes 202760 | tf_op jit(solution)/shard_map/ppermute | solution.py:505
  128.2 10.6 %collective-permute-start.23 = (bf16[264,128]{1,0:T(8,128)(2,1)S(1)}, bf16[264,128]{1,0:T(8,128)(2,1)S(1)}, u32[]{:S(2)}, u32[]{:S(2)}) collective-permute-start(bf16[264,128]{1,0:T(8,128)(2,1)S(1)} %get-tuple-element.65), channel_id=1, source_target_pairs={{0,5},{1,4},{2,7},{3,6},{4,1},{5,0},{6,3},{7,2},{8,13},{9,12},{10,... | collective-permute-start | bytes 202760 | tf_op jit(solution)/shard_map/ppermute | solution.py:505
  128.2 10.6 %collective-permute-start.24 = (bf16[264,128]{1,0:T(8,128)(2,1)S(1)}, bf16[264,128]{1,0:T(8,128)(2,1)S(1)}, u32[]{:S(2)}, u32[]{:S(2)}) collective-permute-start(bf16[264,128]{1,0:T(8,128)(2,1)S(1)} %get-tuple-element.66), channel_id=1, source_target_pairs={{0,6},{1,7},{2,4},{3,5},{4,2},{5,3},{6,0},{7,1},{8,14},{9,15},{10,... | collective-permute-start | bytes 202760 | tf_op jit(solution)/shard_map/ppermute | solution.py:505
  130.5 8.4 %collective-permute-start.25 = (bf16[264,128]{1,0:T(8,128)(2,1)S(1)}, bf16[264,128]{1,0:T(8,128)(2,1)S(1)}, u32[]{:S(2)}, u32[]{:S(2)}) collective-permute-start(bf16[264,128]{1,0:T(8,128)(2,1)S(1)} %get-tuple-element.67), channel_id=1, source_target_pairs={{0,7},{1,6},{2,5},{3,4},{4,3},{5,2},{6,1},{7,0},{8,15},{9,14},{10,... | collective-permute-start | bytes 202760 | tf_op jit(solution)/shard_map/ppermute | solution.py:505
  142.6 7.6 %collective-permute-start.27 = (bf16[264,128]{1,0:T(8,128)(2,1)S(1)}, bf16[264,128]{1,0:T(8,128)(2,1)S(1)}, u32[]{:S(2)}, u32[]{:S(2)}) collective-permute-start(bf16[264,128]{1,0:T(8,128)(2,1)S(1)} %get-tuple-element.72), channel_id=1, source_target_pairs={{0,2},{1,3},{2,0},{3,1},{4,6},{5,7},{6,4},{7,5},{8,10},{9,11},{10,... | collective-permute-start | bytes 202760 | tf_op jit(solution)/shard_map/ppermute | solution.py:505
  146.0 6.2 %collective-permute-start.28 = (bf16[264,128]{1,0:T(8,128)(2,1)S(1)}, bf16[264,128]{1,0:T(8,128)(2,1)S(1)}, u32[]{:S(2)}, u32[]{:S(2)}) collective-permute-start(bf16[264,128]{1,0:T(8,128)(2,1)S(1)} %get-tuple-element.73), channel_id=1, source_target_pairs={{0,3},{1,2},{2,1},{3,0},{4,7},{5,6},{6,5},{7,4},{8,11},{9,10},{10,... | collective-permute-start | bytes 202760 | tf_op jit(solution)/shard_map/ppermute | solution.py:505
  146.0 6.2 %collective-permute-start.29 = (bf16[264,128]{1,0:T(8,128)(2,1)S(1)}, bf16[264,128]{1,0:T(8,128)(2,1)S(1)}, u32[]{:S(2)}, u32[]{:S(2)}) collective-permute-start(bf16[264,128]{1,0:T(8,128)(2,1)S(1)} %get-tuple-element.74), channel_id=1, source_target_pairs={{0,4},{1,5},{2,6},{3,7},{4,0},{5,1},{6,2},{7,3},{8,12},{9,13},{10,... | collective-permute-start | bytes 202760 | tf_op jit(solution)/shard_map/ppermute | solution.py:505
  147.9 10.6 %collective-permute-start.30 = (bf16[264,128]{1,0:T(8,128)(2,1)S(1)}, bf16[264,128]{1,0:T(8,128)(2,1)S(1)}, u32[]{:S(2)}, u32[]{:S(2)}) collective-permute-start(bf16[264,128]{1,0:T(8,128)(2,1)S(1)} %get-tuple-element.75), channel_id=1, source_target_pairs={{0,5},{1,4},{2,7},{3,6},{4,1},{5,0},{6,3},{7,2},{8,13},{9,12},{10,... | collective-permute-start | bytes 202760 | tf_op jit(solution)/shard_map/ppermute | solution.py:505
  148.4 10.2 %collective-permute-start.31 = (bf16[264,128]{1,0:T(8,128)(2,1)S(1)}, bf16[264,128]{1,0:T(8,128)(2,1)S(1)}, u32[]{:S(2)}, u32[]{:S(2)}) collective-permute-start(bf16[264,128]{1,0:T(8,128)(2,1)S(1)} %get-tuple-element.76), channel_id=1, source_target_pairs={{0,6},{1,7},{2,4},{3,5},{4,2},{5,3},{6,0},{7,1},{8,14},{9,15},{10,... | collective-permute-start | bytes 202760 | tf_op jit(solution)/shard_map/ppermute | solution.py:505
  150.1 8.4 %collective-permute-start.32 = (bf16[264,128]{1,0:T(8,128)(2,1)S(1)}, bf16[264,128]{1,0:T(8,128)(2,1)S(1)}, u32[]{:S(2)}, u32[]{:S(2)}) collective-permute-start(bf16[264,128]{1,0:T(8,128)(2,1)S(1)} %get-tuple-element.77), channel_id=1, source_target_pairs={{0,7},{1,6},{2,5},{3,4},{4,3},{5,2},{6,1},{7,0},{8,15},{9,14},{10,... | collective-permute-start | bytes 202760 | tf_op jit(solution)/shard_map/ppermute | solution.py:505
  164.0 8.0 %collective-permute-start.34 = (bf16[264,128]{1,0:T(8,128)(2,1)S(1)}, bf16[264,128]{1,0:T(8,128)(2,1)S(1)}, u32[]{:S(2)}, u32[]{:S(2)}) collective-permute-start(bf16[264,128]{1,0:T(8,128)(2,1)S(1)} %get-tuple-element.80), channel_id=1, source_target_pairs={{0,2},{1,3},{2,0},{3,1},{4,6},{5,7},{6,4},{7,5},{8,10},{9,11},{10,... | collective-permute-start | bytes 202760 | tf_op jit(solution)/shard_map/ppermute | solution.py:505
  169.8 10.5 %collective-permute-start.37 = (bf16[264,128]{1,0:T(8,128)(2,1)S(1)}, bf16[264,128]{1,0:T(8,128)(2,1)S(1)}, u32[]{:S(2)}, u32[]{:S(2)}) collective-permute-start(bf16[264,128]{1,0:T(8,128)(2,1)S(1)} %get-tuple-element.83), channel_id=1, source_target_pairs={{0,5},{1,4},{2,7},{3,6},{4,1},{5,0},{6,3},{7,2},{8,13},{9,12},{10,... | collective-permute-start | bytes 202760 | tf_op jit(solution)/shard_map/ppermute | solution.py:505
  169.8 10.5 %collective-permute-start.38 = (bf16[264,128]{1,0:T(8,128)(2,1)S(1)}, bf16[264,128]{1,0:T(8,128)(2,1)S(1)}, u32[]{:S(2)}, u32[]{:S(2)}) collective-permute-start(bf16[264,128]{1,0:T(8,128)(2,1)S(1)} %get-tuple-element.84), channel_id=1, source_target_pairs={{0,6},{1,7},{2,4},{3,5},{4,2},{5,3},{6,0},{7,1},{8,14},{9,15},{10,... | collective-permute-start | bytes 202760 | tf_op jit(solution)/shard_map/ppermute | solution.py:505
  171.9 8.4 %collective-permute-start.39 = (bf16[264,128]{1,0:T(8,128)(2,1)S(1)}, bf16[264,128]{1,0:T(8,128)(2,1)S(1)}, u32[]{:S(2)}, u32[]{:S(2)}) collective-permute-start(bf16[264,128]{1,0:T(8,128)(2,1)S(1)} %get-tuple-element.85), channel_id=1, source_target_pairs={{0,7},{1,6},{2,5},{3,4},{4,3},{5,2},{6,1},{7,0},{8,15},{9,14},{10,... | collective-permute-start | bytes 202760 | tf_op jit(solution)/shard_map/ppermute | solution.py:505
  (27 other events, 440.5 us)

commit v2 on v1

--- a/solution.py
+++ b/solution.py
@@ -12,6 +12,9 @@
 F32 = jnp.float32
 BF16 = jnp.bfloat16
 I32 = jnp.int32
+
+
+GRANTS = {"gather": 16, "update": 16, "pool": 12, "prepare": 12}
 
 
 def vmem(count):
@@ -151,6 +154,17 @@
                         preferred_element_type=F32,
                     ).astype(BF16)
                 )
+
+
+def prepare_kernel(slots, tables, plan_ref, tall_ref):
+    ranks, _, _ = plan_views(plan_ref, tables, slots.peers)
+    samples = plan_ref.shape[0]
+    group = slots.group
+    picks = slots.pick(0)
+    for block in range(slots.blocks):
+        for t in range(tables):
+            held = ranks[t][:, block * group : (block + 1) * group]
+            tall_ref[block, :, t * samples : (t + 1) * samples] = slots.spread_t(held, picks)
 
 
 def one_hot_rows(slots, block, want_ref, hot_ref):
@@ -313,7 +327,7 @@
     n = eslots.arrays
     x_ref, refs = eslots.refs(refs), refs[n:]
     in_refs, out_refs, refs = refs[0:7], refs[7:12], refs[12:]
-    total_ref, hidden_ref, rows_ref, in_buf, out_buf, sems = refs
+    total_ref, last_ref, *hidden_refs, rows_ref, in_buf, out_buf, sems = refs
     own = [
         pltpu.make_async_copy(in_refs[0], in_buf, sems.at[0]),
         pltpu.make_async_copy(out_refs[0], out_buf, sems.at[1]),
@@ -323,7 +337,7 @@
     eslots.unpack(0, x_ref, rows_ref)
     rows = rows_ref[...]
     half = rows.shape[1] // 2
-    share = hidden_ref.shape[2]
+    share = last_ref.shape[1]
     dot = lambda a, b: jnp.dot(a, b, preferred_element_type=F32)
     total = 0.0
     for i in (1, 2, 3, 0):
@@ -334,8 +348,18 @@
             pre = dot(rows, in_buf[...])
         else:
             pre = dot(rows[:, :half], in_refs[low][...]) + dot(rows[:, half:], in_refs[high][...])
-        hidden = jnp.maximum(pre, 0.0).astype(BF16)
-        hidden_ref[i] = hidden
+        pre = jnp.maximum(pre, 0.0)
+        hidden = pre.astype(BF16)
+        if i == 3:
+            last_ref[...] = hidden
+        count = eslots.peers // len(hidden_refs)
+        bulk, extra = count * eslots.main, count * eslots.ext
+        for part, ref in enumerate(hidden_refs):
+            ref[i, 0:bulk, :] = hidden[part * bulk : (part + 1) * bulk]
+            if extra:
+                first = eslots.peers * eslots.main
+                tail = pre[first : eslots.rows]
+                ref[i, bulk : bulk + extra, :] = tail[part * extra : (part + 1) * extra].astype(BF16)
         if i == 0:
             total = total + dot(hidden, out_buf[...])
         elif i < 3:
@@ -344,9 +368,9 @@
     total_ref[...] = total
 
 
-def finish_kernel(eslots, total_ref, hidden_ref, low_ref, high_ref, *refs):
+def finish_kernel(eslots, total_ref, last_ref, low_ref, high_ref, *refs):
     y_ref, rows_ref = eslots.refs(refs), refs[eslots.arrays]
-    hidden = hidden_ref[3]
+    hidden = last_ref[...]
     half = hidden.shape[1] // 2
     dot = lambda a, b: jnp.dot(a, b, preferred_element_type=F32)
     total = total_ref[...] + dot(hidden[:, :half], low_ref[...]) + dot(hidden[:, half:], high_ref[...])
@@ -378,6 +402,17 @@
     rows_ref[:, :half] = low.astype(BF16)
     rows_ref[:, half:] = high.astype(BF16)
     eslots.pack(0, rows_ref, dx_ref)
+
+
+def hold_kernel(*refs):
+    count = len(refs) // 2
+    copies = [
+        pltpu.make_async_copy(refs[i], refs[count + i], refs[2 * count].at[i]) for i in range(count)
+    ]
+    for copy in copies:
+        copy.start()
+    for copy in copies:
+        copy.wait()
 
 
 def middle_kernel(eslots, tables, owners, *refs):
@@ -438,21 +473,15 @@
 
 def spread_grads_kernel(slots, eslots, tables, *refs):
     dx_ref, refs = eslots.refs(refs), refs[eslots.arrays :]
-    plan_ref, dgate_ref, out_ref, rows_ref, grad_ref = refs
-    ranks, eranks, _ = plan_views(plan_ref, tables, slots.peers)
-    width, group = slots.width, slots.group
+    plan_ref, dgate_ref, tall_ref, out_ref, rows_ref, grad_ref = refs
+    _, eranks, _ = plan_views(plan_ref, tables, slots.peers)
+    width = slots.width
     eslots.unpack(0, dx_ref, rows_ref)
     total = dgate_ref[...] + spread_pair(eslots, eranks, rows_ref)
     total = total.astype(BF16)
-    picks = slots.pick(0)
+    stacked = jnp.concatenate([total[:, t * width : (t + 1) * width] for t in range(tables)], axis=0)
     for block in range(slots.blocks):
-        grads = 0.0
-        for t in range(tables):
-            held = ranks[t][:, block * group : (block + 1) * group]
-            grads = grads + jnp.dot(
-                slots.spread_t(held, picks), total[:, t * width : (t + 1) * width], preferred_element_type=F32
-            )
-        grad_ref[...] = grads.astype(BF16)
+        grad_ref[...] = jnp.dot(tall_ref[block], stacked, preferred_element_type=F32).astype(BF16)
         slots.pack(block, grad_ref, out_ref)
 
 
@@ -484,26 +513,39 @@
         new_table_ref[t] = held_ref[t] - step.T
 
 
-def gather_weight(w, later):
+def cut_kernel(w_ref, out_ref, sem):
+    copy = pltpu.make_async_copy(w_ref.at[0 : out_ref.shape[0]], out_ref, sem)
+    copy.start()
+    copy.wait()
+
+
+def gather_weight(w, low, later):
     half = w.shape[0] // 2
 
     def send(x, bit):
         return lax.ppermute(x, "dp", [(i, i ^ bit) for i in range(4)])
 
-    low, high = w[:half], lax.optimization_barrier((w, later))[0][half:]
+    high = lax.optimization_barrier((w, later))[0][half:]
     low1, low2 = send(low, 1), send(low, 2)
     high1, high2 = send(high, 1), send(high, 2)
     return [w, low1, high1, low2, high2, send(low1, 2), send(high2, 1)]
 
 
+def trade_one(eslots, chunk, k):
+    return lax.ppermute(chunk, "expert", [(i, i ^ k) for i in range(eslots.peers)])
+
+
 def trade(eslots, chunks):
     if not eslots.apart:
         return [lax.all_to_all(chunks[0], "expert", 0, 0, tiled=True)]
-    order = sorted(range(1, eslots.peers), key=lambda k: (-(k // 2), k))
     got = {0: chunks[0]}
-    for k in order:
-        got[k] = lax.ppermute(chunks[k], "expert", [(i, i ^ k) for i in range(eslots.peers)])
+    for k in sorted(range(1, eslots.peers), key=lambda k: (-(k // 2), k)):
+        got[k] = trade_one(eslots, chunks[k], k)
     return [got[k] for k in range(eslots.peers)]
+
+
+def trade_near(eslots, chunks):
+    return [chunks[0]] + [trade_one(eslots, x, k + 1) for k, x in enumerate(chunks[1:])]
 
 
 def per_device(
@@ -531,7 +573,7 @@
     def off(x):
         return pltpu.with_memory_space_constraint(x, pltpu.HBM)
 
-    def call(kernel, out_shape, scratch, *args, in_specs=None, out_specs=None):
+    def call(name, kernel, out_shape, scratch, *args, in_specs=None, out_specs=None):
         many = isinstance(out_shape, (list, tuple))
         return pl.pallas_call(
             kernel,
@@ -539,7 +581,7 @@
             in_specs=in_specs or vmem(len(args)),
             out_specs=out_specs or (vmem(len(out_shape)) if many else vmem(1)[0]),
             scratch_shapes=scratch,
-            compiler_params=params(24 if eslots.rows <= 512 else 60),
+            compiler_params=params(GRANTS.get(name, 8) if eslots.rows <= 512 else 60),
         )(*args)
 
     def bind(fn, *static):
@@ -547,6 +589,7 @@
 
     square = pltpu.VMEM((LANES, max(LANES, device_count)), F32)
     plan, want = call(
+        "index",
         bind(index_kernel, cap_rows, table_rows),
         [
             shape((samples, table_count * device_count + 4 * expert_count), F32),
@@ -564,8 +607,16 @@
         off(route.T),
         in_specs=[pl.BlockSpec(memory_space=pltpu.SMEM)] + hbm(4),
     )
-    ins = gather_weight(w_in[0], plan)
-    outs = gather_weight(w_out[0], plan)
+    low = call(
+        "cut",
+        cut_kernel,
+        shape((w_in.shape[1] // 2, w_in.shape[2]), BF16),
+        [pltpu.SemaphoreType.DMA(())],
+        off(w_in[0]),
+        in_specs=hbm(1),
+    )
+    ins = gather_weight(w_in[0], low, plan)
+    outs = gather_weight(w_out[0], w_out[0, : w_out.shape[1] // 2], plan)
     gate_t = jnp.swapaxes(gate_w, 1, 2)
     wanted = lax.all_to_all(want, both, 0, 0, tiled=True)
     row_shape = slots.shapes()[0]
@@ -575,6 +626,7 @@
     rows = pltpu.VMEM((slots.rows, emb), BF16)
     erows = pltpu.VMEM((eslots.rows, width), BF16)
     served = call(
+        "gather",
         bind(gather_kernel, slots),
         pltpu.HBM(row_shape.shape, BF16),
         [
@@ -589,8 +641,16 @@
         in_specs=vmem(1) + hbm(1),
         out_specs=hbm(1)[0],
     )
+    tall = call(
+        "prepare",
+        bind(prepare_kernel, slots, table_count),
+        shape((slots.blocks, slots.rows, table_count * samples), BF16),
+        [],
+        plan,
+    )
     returned = lax.all_to_all(served, both, 0, 0, tiled=True)
     *outgoing, first = call(
+        "pool",
         bind(pool_kernel, slots, eslots, table_count),
         exp_shapes + [shape((samples, tasks), F32)],
         [rows, pltpu.VMEM((samples, width), BF16), erows],
@@ -605,9 +665,15 @@
         pltpu.VMEM((share, width), BF16),
         pltpu.SemaphoreType.DMA((2,)),
     ]
-    total, hidden = call(
+    halves = [eslots]
+    if apart:
+        count = expert_count // 2
+        halves = [Slots(count, cap_expert, width, count, True)] * 2
+    total, last, *hidden = call(
+        "forward",
         bind(forward_kernel, eslots),
-        [shape((eslots.rows, width), F32), shape((4, eslots.rows, share), BF16)],
+        [shape((eslots.rows, width), F32), shape((eslots.rows, share), BF16)]
+        + [shape((4, part.rows, share), BF16) for part in halves],
         [erows] + own,
         *arrived,
         off(ins[0]),
@@ -616,9 +682,12 @@
         *outs[1:5],
         in_specs=vmem(n) + hbm(1) + vmem(6) + hbm(1) + vmem(4),
     )
-    result = call(bind(finish_kernel, eslots), exp_shapes, [erows], total, hidden, *outs[5:7])
+    result = call(
+        "finish", bind(finish_kernel, eslots), exp_shapes, [erows], total, last, *outs[5:7]
+    )
     back = trade(eslots, result)
     logits, dgate, *grads_out = call(
+        "middle",
         bind(middle_kernel, eslots, table_count, device_count),
         [shape((tasks, samples), F32), shape((samples, width), F32)] + exp_shapes,
         [erows, pltpu.VMEM((LANES, samples), F32)],
@@ -630,20 +699,48 @@
         gate_t,
     )
     arrived_grads = trade(eslots, grads_out)
-    dinput = call(
-        bind(backward_kernel, eslots), exp_shapes, [erows], *arrived_grads, hidden, *ins, *outs
-    )
-    back_grads = trade(eslots, dinput)
+
+    def back_pass(name, part, grads, kept):
+        return call(
+            name,
+            bind(backward_kernel, part),
+            part.shapes(),
+            [pltpu.VMEM((part.rows, width), BF16)],
+            *grads,
+            kept,
+            *ins,
+            *outs,
+        )
+
+    if apart:
+        held = call(
+            "hold",
+            hold_kernel,
+            [pltpu.VMEM(w.shape, BF16) for w in ins + outs],
+            [pltpu.SemaphoreType.DMA((14,))],
+            *[off(w) for w in ins + outs],
+            in_specs=hbm(14),
+        )
+        ins, outs = held[:7], held[7:]
+        far = back_pass("backfar", halves[1], arrived_grads[count:], hidden[1])
+        far = [trade_one(eslots, x, count + i) for i, x in enumerate(far)]
+        near = back_pass("backnear", halves[0], arrived_grads[:count], hidden[0])
+        back_grads = trade_near(eslots, near) + far
+    else:
+        back_grads = trade(eslots, back_pass("backward", eslots, arrived_grads, hidden[0]))
     row_out = call(
+        "spread",
         bind(spread_grads_kernel, slots, eslots, table_count),
         row_shape,
         [erows, rows],
         *back_grads,
         plan,
         dgate,
+        tall,
     )
     row_in = lax.all_to_all(row_out, both, 0, 0, tiled=True)
     new_tables, new_accum = call(
+        "update",
         bind(update_kernel, slots),
         [shape(tables.shape, F32), shape(accum.shape, F32)],
         [pltpu.VMEM(tables.shape, F32), hot, rows, pltpu.SemaphoreType.DMA(())],

time: 228 us -> 219 us (0.961)
  Pallas kernels: 32.4 us -> 38.2 us
  waiting for transfers between devices: 79.5 us -> 74.4 us
  starting transfers between devices: 54.8 us -> 51.2 us
  local copies, waits for them, and re-layouts: 5.98 us -> 2.56 us
    ppermute x28, waiting for transfers between devices: 23.8 us -> 18 us  [trade_one(): lax.ppermute(chunk, 'expert', [(i, i ^ k) for i in range(eslots.peers)])]
    pallas_call x9 -> x13, Pallas kernels: 32.4 us -> 38.2 us  [call(): pl.pallas_call(kernel, out_shape=out_shape, in_specs=in_specs or vmem(len...]
    ppermute x28, starting transfers between devices: 40.6 us -> 37 us  [trade_one(): lax.ppermute(chunk, 'expert', [(i, i ^ k) for i in range(eslots.peers)])]
    unnamed x36 -> x28, local copies, waits for them, and re-layouts: 5.05 us -> 1.66 us
  transfers between devices with their start and end apart: 41 -> 41, of which waited for: 12 -> 13; matrix products, arithmetic and copies ran while one was open for 0% -> 0% of each run, Pallas kernels for 3% -> 9%
where the time goes in v2:
time: 219 us
  waiting for transfers between devices  74.4 us (34%)
  blocking collectives  51.5 us (24%)
  starting transfers between devices  51.2 us (23%)
  Pallas kernels  38.2 us (17%)
  local copies, waits for them, and re-layouts  2.56 us (1%)
    ppermute x12, waiting for transfers between devices, send(): return lax.ppermute(x, 'dp', [(i, i ^ bit) for i in range(4)])  56.4 us
    pallas_call x13, Pallas kernels, call(): pl.pallas_call(kernel, out_shape=out_shape, in_specs=in_specs or vmem(len...  38.2 us
    all_to_all x1, blocking collectives, per_device(): row_in = lax.all_to_all(row_out, both, 0, 0, tiled=True)  37.1 us
    ppermute x28, starting transfers between devices, trade_one(): lax.ppermute(chunk, 'expert', [(i, i ^ k) for i in range(eslots.peers)])  37 us
    ppermute x28, waiting for transfers between devices, trade_one(): lax.ppermute(chunk, 'expert', [(i, i ^ k) for i in range(eslots.peers)])  18 us
    all_to_all x1, blocking collectives, per_device(): wanted = lax.all_to_all(want, both, 0, 0, tiled=True)  14.3 us
    ppermute x12, starting transfers between devices, send(): return lax.ppermute(x, 'dp', [(i, i ^ bit) for i in range(4)])  11.3 us
  transfers between devices with their start and end apart: 41, of which 13 were waited for; matrix products, arithmetic and copies ran while one was open for 0% of the time, Pallas kernels for 9%

profile of v2, /device:TPU:0, one launch (start us, length us, event | category | flops | bytes accessed | tf_op | source)
XLA Modules:
  0.0 218.9 jit_solution(15240079903996397340)
XLA Ops:
  0.6 3.6 %shard_map.130 = (f32[128,160]{1,0:T(8,128)S(1)}, s32[32,128]{1,0:T(8,128)S(1)}) custom-call(s32[1]{0:T(128)} %bitcast.refs_0_, s32[16,128]{1,0:T(8,128)} %bitcast.30, s32[16,128]{1,0:T(8,128)} %bitcast.31, s32[4,128]{1,0:T(4,128)} %refs_3_.2, s32[2,128]{1,0:T(2,128)} %bitcast.32), custom_call_target="tpu_custom_call" | custom-call | tf_op jit(solution)/shard_map/pallas_call | solution.py:578
  4.3 14.3 %all_to_all.21 = s32[32,1,128]{2,1,0:T(1,128)S(1)} all-to-all(s32[32,1,128]{2,1,0:T(1,128)S(1)} %bitcast.20), channel_id=1, replica_groups=mesh['dp'=4,'expert'=8] {'dp','expert'}, dimensions={0} | all-to-all | bytes 32768 | tf_op jit(solution)/shard_map/all_to_all | solution.py:621
  18.6 4.2 %shard_map.131 = bf16[32,168,128]{2,1,0:T(8,128)(2,1)} custom-call(s32[32,128]{1,0:T(8,128)S(1)} %bitcast.16, f32[1024,256]{1,0:T(8,128)} %bitcast.29), custom_call_target="tpu_custom_call" | custom-call | tf_op jit(solution)/shard_map/pallas_call | solution.py:578
  22.8 3.0 %all-to-all-start.1 = ((bf16[32,168,128]{2,1,0:T(8,128)(2,1)}), bf16[32,168,128]{2,1,0:T(8,128)(2,1)S(1)}, u32[]{:S(2)}, u32[]{:S(2)}) async-start(bf16[32,168,128]{2,1,0:T(8,128)(2,1)} %shard_map.131), calls=%async_computation.1 | async-start | bytes 2752512 | tf_op jit(solution)/shard_map/all_to_all | solution.py:651
  33.7 19.3 %collective-permute-done.15.refs_18_.refs_10_ = bf16[256,1024]{1,0:T(8,128)(2,1)S(1)} collective-permute-done((bf16[256,1024]{1,0:T(8,128)(2,1)S(1)}, bf16[256,1024]{1,0:T(8,128)(2,1)S(1)}, u32[]{:S(2)}, u32[]{:S(2)}) %collective-permute-start.15) | collective-permute-done | bytes 524320 | tf_op jit(solution)/shard_map/ppermute | solution.py:526
  54.6 11.6 %collective-permute-done.9.refs_11_.refs_3_ = bf16[512,512]{1,0:T(8,128)(2,1)S(1)} collective-permute-done((bf16[512,512]{1,0:T(8,128)(2,1)S(1)}, bf16[512,512]{1,0:T(8,128)(2,1)S(1)}, u32[]{:S(2)}, u32[]{:S(2)}) %collective-permute-start.9) | collective-permute-done | bytes 524320 | tf_op jit(solution)/shard_map/ppermute | solution.py:526
  68.3 9.1 %collective-permute-done.10.refs_12_.refs_4_ = bf16[512,512]{1,0:T(8,128)(2,1)} collective-permute-done((bf16[512,512]{1,0:T(8,128)(2,1)}, bf16[512,512]{1,0:T(8,128)(2,1)}, u32[]{:S(2)}, u32[]{:S(2)}) %collective-permute-start.10) | collective-permute-done | bytes 524320 | tf_op jit(solution)/shard_map/ppermute | solution.py:526
  78.5 10.2 %collective-permute-done.16.refs_19_.refs_11_ = bf16[256,1024]{1,0:T(8,128)(2,1)} collective-permute-done((bf16[256,1024]{1,0:T(8,128)(2,1)S(1)}, bf16[256,1024]{1,0:T(8,128)(2,1)}, u32[]{:S(2)}, u32[]{:S(2)}) %collective-permute-start.16) | collective-permute-done | bytes 524320 | tf_op jit(solution)/shard_map/ppermute | solution.py:526
  90.9 2.7 %shard_map.132 = (bf16[264,128]{1,0:T(8,128)(2,1)S(1)}, bf16[264,128]{1,0:T(8,128)(2,1)S(1)}, bf16[264,128]{1,0:T(8,128)(2,1)S(1)}, bf16[264,128]{1,0:T(8,128)(2...) custom-call(bf16[32,168,128]{2,1,0:T(8,128)(2,1)S(1)} %all-to-all-do, ...), custom_call_target="tpu_custom_call" | custom-call | tf_op jit(solution)/shard_map/pallas_call | solution.py:578
  93.8 6.2 %collective-permute-done.11.refs_13_.refs_5_ = bf16[512,512]{1,0:T(8,128)(2,1)} collective-permute-done((bf16[512,512]{1,0:T(8,128)(2,1)}, bf16[512,512]{1,0:T(8,128)(2,1)}, u32[]{:S(2)}, u32[]{:S(2)}) %collective-permute-start.11) | collective-permute-done | bytes 524320 | tf_op jit(solution)/shard_map/ppermute | solution.py:526
  101.5 2.6 %collective-permute-start.3 = (bf16[264,128]{1,0:T(8,128)(2,1)S(1)}, bf16[264,128]{1,0:T(8,128)(2,1)S(1)}, u32[]{:S(2)}, u32[]{:S(2)}) collective-permute-start(bf16[264,128]{1,0:T(8,128)(2,1)S(1)} %get-tuple-element.68), channel_id=1, source_target_pairs={{0,4},{1,5},{2,6},{3,7},{4,0},{5,1},{6,2},{7,3},{8,12},{9,13},{10,... | collective-permute-start | bytes 202760 | tf_op jit(solution)/shard_map/ppermute | solution.py:535
  105.7 2.7 %collective-permute-start.5 = (bf16[264,128]{1,0:T(8,128)(2,1)S(1)}, bf16[264,128]{1,0:T(8,128)(2,1)S(1)}, u32[]{:S(2)}, u32[]{:S(2)}) collective-permute-start(bf16[264,128]{1,0:T(8,128)(2,1)S(1)} %get-tuple-element.70), channel_id=1, source_target_pairs={{0,6},{1,7},{2,4},{3,5},{4,2},{5,3},{6,0},{7,1},{8,14},{9,15},{10,... | collective-permute-start | bytes 202760 | tf_op jit(solution)/shard_map/ppermute | solution.py:535
  108.4 4.5 %collective-permute-start.6 = (bf16[264,128]{1,0:T(8,128)(2,1)S(1)}, bf16[264,128]{1,0:T(8,128)(2,1)S(1)}, u32[]{:S(2)}, u32[]{:S(2)}) collective-permute-start(bf16[264,128]{1,0:T(8,128)(2,1)S(1)} %get-tuple-element.71), channel_id=1, source_target_pairs={{0,7},{1,6},{2,5},{3,4},{4,3},{5,2},{6,1},{7,0},{8,15},{9,14},{10,... | collective-permute-start | bytes 202760 | tf_op jit(solution)/shard_map/ppermute | solution.py:535
  115.2 5.6 %shard_map.134 = (f32[264,1024]{1,0:T(8,128)S(1)}, bf16[264,512]{1,0:T(8,128)(2,1)S(1)}, bf16[4,132,512]{2,1,0:T(8,128)(2,1)S(1)}, bf16[4,132,512]{2,1,0:T(8,128)(2,1)S(1)}) custom-call(bf16[264,128]{1,0:T(8,128)(2,1)S(1)} %get-tuple-element.64.refs_0_, bf16[264,128]{1,0:T(8,128)(2,1)S(1)} %collective-permute-done.refs_1_, ...), custom_call_target="tpu_custom_call" | custom-call | tf_op jit(solution)/shard_map/pallas_call | solution.py:578
  121.8 3.0 %collective-permute-start.20 = (bf16[264,128]{1,0:T(8,128)(2,1)S(1)}, bf16[264,128]{1,0:T(8,128)(2,1)S(1)}, u32[]{:S(2)}, u32[]{:S(2)}) collective-permute-start(bf16[264,128]{1,0:T(8,128)(2,1)S(1)} %get-tuple-element.78), channel_id=1, source_target_pairs={{0,2},{1,3},{2,0},{3,1},{4,6},{5,7},{6,4},{7,5},{8,10},{9,11},{10,... | collective-permute-start | bytes 202760 | tf_op jit(solution)/shard_map/ppermute | solution.py:535
  124.8 2.6 %collective-permute-start.22 = (bf16[264,128]{1,0:T(8,128)(2,1)S(1)}, bf16[264,128]{1,0:T(8,128)(2,1)S(1)}, u32[]{:S(2)}, u32[]{:S(2)}) collective-permute-start(bf16[264,128]{1,0:T(8,128)(2,1)S(1)} %get-tuple-element.80), channel_id=1, source_target_pairs={{0,4},{1,5},{2,6},{3,7},{4,0},{5,1},{6,2},{7,3},{8,12},{9,13},{10,... | collective-permute-start | bytes 202760 | tf_op jit(solution)/shard_map/ppermute | solution.py:535
  127.4 2.2 %collective-permute-start.24 = (bf16[264,128]{1,0:T(8,128)(2,1)S(1)}, bf16[264,128]{1,0:T(8,128)(2,1)S(1)}, u32[]{:S(2)}, u32[]{:S(2)}) collective-permute-start(bf16[264,128]{1,0:T(8,128)(2,1)S(1)} %get-tuple-element.82), channel_id=1, source_target_pairs={{0,6},{1,7},{2,4},{3,5},{4,2},{5,3},{6,0},{7,1},{8,14},{9,15},{10,... | collective-permute-start | bytes 202760 | tf_op jit(solution)/shard_map/ppermute | solution.py:535
  131.0 6.9 %collective-permute-done.23.refs_5_ = bf16[264,128]{1,0:T(8,128)(2,1)S(1)} collective-permute-done((bf16[264,128]{1,0:T(8,128)(2,1)S(1)}, bf16[264,128]{1,0:T(8,128)(2,1)S(1)}, u32[]{:S(2)}, u32[]{:S(2)}) %collective-permute-start.23) | collective-permute-done | bytes 67616 | tf_op jit(solution)/shard_map/ppermute | solution.py:535
  138.0 3.6 %shard_map.136 = (f32[2,128]{1,0:T(2,128)}, f32[128,1024]{1,0:T(8,128)S(1)}, bf16[264,128]{1,0:T(8,128)(2,1)S(1)}, bf16[264,128]{1,0:T(8,128)(2,1)S(1)}, bf16[26...) custom-call(bf16[264,128]{1,0:T(8,128)(2,1)S(1)} %get-tuple-element., ...), custom_call_target="tpu_custom_call" | custom-call | tf_op jit(solution)/shard_map/pallas_call | solution.py:578
  141.6 3.6 %collective-permute-start.32 = (bf16[264,128]{1,0:T(8,128)(2,1)S(1)}, bf16[264,128]{1,0:T(8,128)(2,1)S(1)}, u32[]{:S(2)}, u32[]{:S(2)}) collective-permute-start(bf16[264,128]{1,0:T(8,128)(2,1)S(1)} %get-tuple-element.109), channel_id=1, source_target_pairs={{0,4},{1,5},{2,6},{3,7},{4,0},{5,1},{6,2},{7,3},{8,12},{9,13},{10,... | collective-permute-start | bytes 202760 | tf_op jit(solution)/shard_map/ppermute | solution.py:535
  145.2 2.2 %collective-permute-start.34 = (bf16[264,128]{1,0:T(8,128)(2,1)S(1)}, bf16[264,128]{1,0:T(8,128)(2,1)S(1)}, u32[]{:S(2)}, u32[]{:S(2)}) collective-permute-start(bf16[264,128]{1,0:T(8,128)(2,1)S(1)} %get-tuple-element.111), channel_id=1, source_target_pairs={{0,6},{1,7},{2,4},{3,5},{4,2},{5,3},{6,0},{7,1},{8,14},{9,15},{10,... | collective-permute-start | bytes 202760 | tf_op jit(solution)/shard_map/ppermute | solution.py:535
  148.5 3.5 %shard_map.137 = (bf16[1024,512]{1,0:T(8,128)(2,1)S(1)}, bf16[512,512]{1,0:T(8,128)(2,1)S(1)}, bf16[512,512]{1,0:T(8,128)(2,1)S(1)}, bf16[512,512]{1,0:T(8,128)(...) custom-call(bf16[1024,512]{1,0:T(8,128)(2,1)} %bitcast.24, ...), custom_call_target="tpu_custom_call" | custom-call | tf_op jit(solution)/shard_map/pallas_call | solution.py:578
  153.1 2.2 %collective-permute-done.33.refs_1_ = bf16[264,128]{1,0:T(8,128)(2,1)S(1)} collective-permute-done((bf16[264,128]{1,0:T(8,128)(2,1)S(1)}, bf16[264,128]{1,0:T(8,128)(2,1)S(1)}, u32[]{:S(2)}, u32[]{:S(2)}) %collective-permute-start.33) | collective-permute-done | bytes 67616 | tf_op jit(solution)/shard_map/ppermute | solution.py:535
  155.3 3.1 %shard_map.139 = (bf16[264,128]{1,0:T(8,128)(2,1)S(1)}, bf16[264,128]{1,0:T(8,128)(2,1)S(1)}, bf16[264,128]{1,0:T(8,128)(2,1)S(1)}, bf16[264,128]{1,0:T(8,128)(2,1)S(1)}) custom-call(bf16[264,128]{1,0:T(8,128)(2,1)S(1)} %collective-permute-done.32.refs_0_, bf16[264,128]{1,0:T(8,128)(2,1)S(1)} %collective-permute-done.33.refs_1_, ...), custom_call_target="tpu_custom_call" | custom-call | tf_op jit(solution)/shard_map/pallas_call | solution.py:578
  158.4 3.7 %collective-permute-start.36 = (bf16[264,128]{1,0:T(8,128)(2,1)S(1)}, bf16[264,128]{1,0:T(8,128)(2,1)S(1)}, u32[]{:S(2)}, u32[]{:S(2)}) collective-permute-start(bf16[264,128]{1,0:T(8,128)(2,1)S(1)} %get-tuple-element.114), channel_id=1, source_target_pairs={{0,4},{1,5},{2,6},{3,7},{4,0},{5,1},{6,2},{7,3},{8,12},{9,13},{10,... | collective-permute-start | bytes 202760 | tf_op jit(solution)/shard_map/ppermute | solution.py:535
  162.2 2.1 collective-permute-start.38
  165.4 3.3 %shard_map.138 = (bf16[264,128]{1,0:T(8,128)(2,1)S(1)}, bf16[264,128]{1,0:T(8,128)(2,1)S(1)}, bf16[264,128]{1,0:T(8,128)(2,1)S(1)}, bf16[264,128]{1,0:T(8,128)(2,1)S(1)}) custom-call(bf16[264,128]{1,0:T(8,128)(2,1)S(1)} %get-tuple-element.86.refs_0_, bf16[264,128]{1,0:T(8,128)(2,1)S(1)} %collective-permute-done.26.refs_1_, ...), custom_call_target="tpu_custom_call" | custom-call | tf_op jit(solution)/shard_map/pallas_call | solution.py:578
  169.7 2.4 %collective-permute-done.37.refs_5_ = bf16[264,128]{1,0:T(8,128)(2,1)S(1)} collective-permute-done((bf16[264,128]{1,0:T(8,128)(2,1)S(1)}, bf16[264,128]{1,0:T(8,128)(2,1)S(1)}, u32[]{:S(2)}, u32[]{:S(2)}) %collective-permute-start.37) | collective-permute-done | bytes 67616 | tf_op jit(solution)/shard_map/ppermute | solution.py:535
  173.7 2.6 %collective-permute-done.31.refs_3_ = bf16[264,128]{1,0:T(8,128)(2,1)S(1)} collective-permute-done((bf16[264,128]{1,0:T(8,128)(2,1)S(1)}, bf16[264,128]{1,0:T(8,128)(2,1)S(1)}, u32[]{:S(2)}, u32[]{:S(2)}) %collective-permute-start.31) | collective-permute-done | bytes 67616 | tf_op jit(solution)/shard_map/ppermute | solution.py:535
  176.3 1.8 shard_map.141
  178.1 37.1 %all_to_all.22.refs_0_ = bf16[32,168,128]{2,1,0:T(8,128)(2,1)S(1)} all-to-all(bf16[32,168,128]{2,1,0:T(8,128)(2,1)S(1)} %shard_map.141), channel_id=1, replica_groups=mesh['dp'=4,'expert'=8] {'dp','expert'}, dimensions={0} | all-to-all | bytes 2752512 | tf_op jit(solution)/shard_map/all_to_all | solution.py:741
  215.3 3.5 %shard_map.142 = (f32[4,256,256]{2,1,0:T(8,128)}, f32[4,256]{1,0:T(4,128)}) custom-call(bf16[32,168,128]{2,1,0:T(8,128)(2,1)S(1)} %all_to_all.22.refs_0_, s32[32,128]{1,0:T(8,128)S(1)} %bitcast.17, f32[4,256,256]{2,1,0:T(8,128)} %refs_2_.1, f32[4,256]{1,0:T(4,128)S(1)} %copy-done.9), custom_call_target="tpu_custom_call" | custom-call | tf_op jit(solution)/shard_map/pallas_call | solution.py:578
  (96 shorter events, 28.8 us)
Async XLA Ops:
  22.8 68.1 %all-to-all-start.1 = ((bf16[32,168,128]{2,1,0:T(8,128)(2,1)}), bf16[32,168,128]{2,1,0:T(8,128)(2,1)S(1)}, u32[]{:S(2)}, u32[]{:S(2)}) async-start(bf16[32,168,128]{2,1,0:T(8,128)(2,1)} %shard_map.131), calls=%async_computation.1 | async-start | bytes 2752512 | tf_op jit(solution)/shard_map/all_to_all | solution.py:651
  25.9 27.0 %collective-permute-start.15 = (bf16[256,1024]{1,0:T(8,128)(2,1)S(1)}, bf16[256,1024]{1,0:T(8,128)(2,1)S(1)}, u32[]{:S(2)}, u32[]{:S(2)}) collective-permute-start(bf16[256,1024]{1,0:T(8,128)(2,1)S(1)} %slice_bitcast_fusion), channel_id=1, source_target_pairs={{0,16},{8,24},{16,0},{24,8},{1,17},{9,25},{17,1},{25,9},{2,18},{10... | collective-permute-start | bytes 1572872 | tf_op jit(solution)/shard_map/ppermute | solution.py:526
  27.6 25.4 %collective-permute-start.13 = (bf16[256,1024]{1,0:T(8,128)(2,1)S(1)}, bf16[256,1024]{1,0:T(8,128)(2,1)}, u32[]{:S(2)}, u32[]{:S(2)}) collective-permute-start(bf16[256,1024]{1,0:T(8,128)(2,1)S(1)} %slice_bitcast_fusion), channel_id=1, source_target_pairs={{0,8},{8,0},{16,24},{24,16},{1,9},{9,1},{17,25},{25,17},{2,10},{10... | collective-permute-start | bytes 1572872 | tf_op jit(solution)/shard_map/ppermute | solution.py:526
  30.2 36.0 %collective-permute-start.9 = (bf16[512,512]{1,0:T(8,128)(2,1)S(1)}, bf16[512,512]{1,0:T(8,128)(2,1)S(1)}, u32[]{:S(2)}, u32[]{:S(2)}) collective-permute-start(bf16[512,512]{1,0:T(8,128)(2,1)S(1)} %shard_map.133), channel_id=1, source_target_pairs={{0,16},{8,24},{16,0},{24,8},{1,17},{9,25},{17,1},{25,9},{2,18},{10... | collective-permute-start | bytes 1572872 | tf_op jit(solution)/shard_map/ppermute | solution.py:526
  30.8 37.2 %collective-permute-start.7 = (bf16[512,512]{1,0:T(8,128)(2,1)S(1)}, bf16[512,512]{1,0:T(8,128)(2,1)}, u32[]{:S(2)}, u32[]{:S(2)}) collective-permute-start(bf16[512,512]{1,0:T(8,128)(2,1)S(1)} %shard_map.133), channel_id=1, source_target_pairs={{0,8},{8,0},{16,24},{24,16},{1,9},{9,1},{17,25},{25,17},{2,10},{10... | collective-permute-start | bytes 1572872 | tf_op jit(solution)/shard_map/ppermute | solution.py:526
  32.0 45.5 %collective-permute-start.10 = (bf16[512,512]{1,0:T(8,128)(2,1)}, bf16[512,512]{1,0:T(8,128)(2,1)}, u32[]{:S(2)}, u32[]{:S(2)}) collective-permute-start(bf16[512,512]{1,0:T(8,128)(2,1)} %slice.9), channel_id=1, source_target_pairs={{0,16},{8,24},{16,0},{24,8},{1,17},{9,25},{17,1},{25,9},{2,18},{10... | collective-permute-start | bytes 1572872 | tf_op jit(solution)/shard_map/ppermute | solution.py:526
  52.9 35.8 %collective-permute-start.16 = (bf16[256,1024]{1,0:T(8,128)(2,1)S(1)}, bf16[256,1024]{1,0:T(8,128)(2,1)}, u32[]{:S(2)}, u32[]{:S(2)}) collective-permute-start(bf16[256,1024]{1,0:T(8,128)(2,1)S(1)} %slice.11), channel_id=1, source_target_pairs={{0,16},{8,24},{16,0},{24,8},{1,17},{9,25},{17,1},{25,9},{2,18},{10... | collective-permute-start | bytes 1572872 | tf_op jit(solution)/shard_map/ppermute | solution.py:526
  53.0 35.8 %collective-permute-start.14 = (bf16[256,1024]{1,0:T(8,128)(2,1)S(1)}, bf16[256,1024]{1,0:T(8,128)(2,1)S(1)}, u32[]{:S(2)}, u32[]{:S(2)}) collective-permute-start(bf16[256,1024]{1,0:T(8,128)(2,1)S(1)} %slice.11), channel_id=1, source_target_pairs={{0,8},{8,0},{16,24},{24,16},{1,9},{9,1},{17,25},{25,17},{2,10},{10... | collective-permute-start | bytes 1572872 | tf_op jit(solution)/shard_map/ppermute | solution.py:526
  66.9 26.8 %collective-permute-start.8 = (bf16[512,512]{1,0:T(8,128)(2,1)}, bf16[512,512]{1,0:T(8,128)(2,1)}, u32[]{:S(2)}, u32[]{:S(2)}) collective-permute-start(bf16[512,512]{1,0:T(8,128)(2,1)} %slice.9), channel_id=1, source_target_pairs={{0,8},{8,0},{16,24},{24,16},{1,9},{9,1},{17,25},{25,17},{2,10},{10... | collective-permute-start | bytes 1572872 | tf_op jit(solution)/shard_map/ppermute | solution.py:526
  68.0 32.0 %collective-permute-start.11 = (bf16[512,512]{1,0:T(8,128)(2,1)}, bf16[512,512]{1,0:T(8,128)(2,1)}, u32[]{:S(2)}, u32[]{:S(2)}) collective-permute-start(bf16[512,512]{1,0:T(8,128)(2,1)} %collective-permute-done.7.refs_9_.refs_1_), channel_id=1, source_target_pairs={{0,16},{8,24},{16,0},{24,8},{1,17},{9,25},{17,1},{25,9},{2,18},{10... | collective-permute-start | bytes 1572872 | tf_op jit(solution)/shard_map/ppermute | solution.py:526
  77.5 24.0 %collective-permute-start.12 = (bf16[512,512]{1,0:T(8,128)(2,1)}, bf16[512,512]{1,0:T(8,128)(2,1)}, u32[]{:S(2)}, u32[]{:S(2)}) collective-permute-start(bf16[512,512]{1,0:T(8,128)(2,1)} %collective-permute-done.10.refs_12_.refs_4_), channel_id=1, source_target_pairs={{0,8},{8,0},{16,24},{24,16},{1,9},{9,1},{17,25},{25,17},{2,10},{10... | collective-permute-start | bytes 1572872 | tf_op jit(solution)/shard_map/ppermute | solution.py:526
  88.7 32.0 %collective-permute-start.17 = (bf16[256,1024]{1,0:T(8,128)(2,1)}, bf16[256,1024]{1,0:T(8,128)(2,1)S(1)}, u32[]{:S(2)}, u32[]{:S(2)}) collective-permute-start(bf16[256,1024]{1,0:T(8,128)(2,1)} %collective-permute-done.13.refs_16_.refs_8_), channel_id=1, source_target_pairs={{0,16},{8,24},{16,0},{24,8},{1,17},{9,25},{17,1},{25,9},{2,18},{10... | collective-permute-start | bytes 1572872 | tf_op jit(solution)/shard_map/ppermute | solution.py:526
  89.6 31.2 %collective-permute-start.18 = (bf16[256,1024]{1,0:T(8,128)(2,1)}, bf16[256,1024]{1,0:T(8,128)(2,1)S(1)}, u32[]{:S(2)}, u32[]{:S(2)}) collective-permute-start(bf16[256,1024]{1,0:T(8,128)(2,1)} %collective-permute-done.16.refs_19_.refs_11_), channel_id=1, source_target_pairs={{0,8},{8,0},{16,24},{24,16},{1,9},{9,1},{17,25},{25,17},{2,10},{10... | collective-permute-start | bytes 1572872 | tf_op jit(solution)/shard_map/ppermute | solution.py:526
  93.7 7.8 %collective-permute-start = (bf16[264,128]{1,0:T(8,128)(2,1)S(1)}, bf16[264,128]{1,0:T(8,128)(2,1)S(1)}, u32[]{:S(2)}, u32[]{:S(2)}) collective-permute-start(bf16[264,128]{1,0:T(8,128)(2,1)S(1)} %get-tuple-element.65), channel_id=1, source_target_pairs={{0,1},{1,0},{2,3},{3,2},{4,5},{5,4},{6,7},{7,6},{8,9},{9,8},{10,11... | collective-permute-start | bytes 202760 | tf_op jit(solution)/shard_map/ppermute | solution.py:535
  101.5 6.9 %collective-permute-start.3 = (bf16[264,128]{1,0:T(8,128)(2,1)S(1)}, bf16[264,128]{1,0:T(8,128)(2,1)S(1)}, u32[]{:S(2)}, u32[]{:S(2)}) collective-permute-start(bf16[264,128]{1,0:T(8,128)(2,1)S(1)} %get-tuple-element.68), channel_id=1, source_target_pairs={{0,4},{1,5},{2,6},{3,7},{4,0},{5,1},{6,2},{7,3},{8,12},{9,13},{10,... | collective-permute-start | bytes 202760 | tf_op jit(solution)/shard_map/ppermute | solution.py:535
  104.3 9.2 %collective-permute-start.4 = (bf16[264,128]{1,0:T(8,128)(2,1)S(1)}, bf16[264,128]{1,0:T(8,128)(2,1)S(1)}, u32[]{:S(2)}, u32[]{:S(2)}) collective-permute-start(bf16[264,128]{1,0:T(8,128)(2,1)S(1)} %get-tuple-element.69), channel_id=1, source_target_pairs={{0,5},{1,4},{2,7},{3,6},{4,1},{5,0},{6,3},{7,2},{8,13},{9,12},{10,... | collective-permute-start | bytes 202760 | tf_op jit(solution)/shard_map/ppermute | solution.py:535
  105.7 7.7 %collective-permute-start.5 = (bf16[264,128]{1,0:T(8,128)(2,1)S(1)}, bf16[264,128]{1,0:T(8,128)(2,1)S(1)}, u32[]{:S(2)}, u32[]{:S(2)}) collective-permute-start(bf16[264,128]{1,0:T(8,128)(2,1)S(1)} %get-tuple-element.70), channel_id=1, source_target_pairs={{0,6},{1,7},{2,4},{3,5},{4,2},{5,3},{6,0},{7,1},{8,14},{9,15},{10,... | collective-permute-start | bytes 202760 | tf_op jit(solution)/shard_map/ppermute | solution.py:535
  121.8 7.8 %collective-permute-start.20 = (bf16[264,128]{1,0:T(8,128)(2,1)S(1)}, bf16[264,128]{1,0:T(8,128)(2,1)S(1)}, u32[]{:S(2)}, u32[]{:S(2)}) collective-permute-start(bf16[264,128]{1,0:T(8,128)(2,1)S(1)} %get-tuple-element.78), channel_id=1, source_target_pairs={{0,2},{1,3},{2,0},{3,1},{4,6},{5,7},{6,4},{7,5},{8,10},{9,11},{10,... | collective-permute-start | bytes 202760 | tf_op jit(solution)/shard_map/ppermute | solution.py:535
  127.4 10.6 %collective-permute-start.23 = (bf16[264,128]{1,0:T(8,128)(2,1)S(1)}, bf16[264,128]{1,0:T(8,128)(2,1)S(1)}, u32[]{:S(2)}, u32[]{:S(2)}) collective-permute-start(bf16[264,128]{1,0:T(8,128)(2,1)S(1)} %get-tuple-element.81), channel_id=1, source_target_pairs={{0,5},{1,4},{2,7},{3,6},{4,1},{5,0},{6,3},{7,2},{8,13},{9,12},{10,... | collective-permute-start | bytes 202760 | tf_op jit(solution)/shard_map/ppermute | solution.py:535
  127.4 10.6 %collective-permute-start.24 = (bf16[264,128]{1,0:T(8,128)(2,1)S(1)}, bf16[264,128]{1,0:T(8,128)(2,1)S(1)}, u32[]{:S(2)}, u32[]{:S(2)}) collective-permute-start(bf16[264,128]{1,0:T(8,128)(2,1)S(1)} %get-tuple-element.82), channel_id=1, source_target_pairs={{0,6},{1,7},{2,4},{3,5},{4,2},{5,3},{6,0},{7,1},{8,14},{9,15},{10,... | collective-permute-start | bytes 202760 | tf_op jit(solution)/shard_map/ppermute | solution.py:535
  129.6 8.4 %collective-permute-start.25 = (bf16[264,128]{1,0:T(8,128)(2,1)S(1)}, bf16[264,128]{1,0:T(8,128)(2,1)S(1)}, u32[]{:S(2)}, u32[]{:S(2)}) collective-permute-start(bf16[264,128]{1,0:T(8,128)(2,1)S(1)} %get-tuple-element.83), channel_id=1, source_target_pairs={{0,7},{1,6},{2,5},{3,4},{4,3},{5,2},{6,1},{7,0},{8,15},{9,14},{10,... | collective-permute-start | bytes 202760 | tf_op jit(solution)/shard_map/ppermute | solution.py:535
  141.6 11.1 %collective-permute-start.32 = (bf16[264,128]{1,0:T(8,128)(2,1)S(1)}, bf16[264,128]{1,0:T(8,128)(2,1)S(1)}, u32[]{:S(2)}, u32[]{:S(2)}) collective-permute-start(bf16[264,128]{1,0:T(8,128)(2,1)S(1)} %get-tuple-element.109), channel_id=1, source_target_pairs={{0,4},{1,5},{2,6},{3,7},{4,0},{5,1},{6,2},{7,3},{8,12},{9,13},{10,... | collective-permute-start | bytes 202760 | tf_op jit(solution)/shard_map/ppermute | solution.py:535
  145.2 10.1 %collective-permute-start.33 = (bf16[264,128]{1,0:T(8,128)(2,1)S(1)}, bf16[264,128]{1,0:T(8,128)(2,1)S(1)}, u32[]{:S(2)}, u32[]{:S(2)}) collective-permute-start(bf16[264,128]{1,0:T(8,128)(2,1)S(1)} %get-tuple-element.110), channel_id=1, source_target_pairs={{0,5},{1,4},{2,7},{3,6},{4,1},{5,0},{6,3},{7,2},{8,13},{9,12},{10,... | collective-permute-start | bytes 202760 | tf_op jit(solution)/shard_map/ppermute | solution.py:535
  145.2 10.1 %collective-permute-start.34 = (bf16[264,128]{1,0:T(8,128)(2,1)S(1)}, bf16[264,128]{1,0:T(8,128)(2,1)S(1)}, u32[]{:S(2)}, u32[]{:S(2)}) collective-permute-start(bf16[264,128]{1,0:T(8,128)(2,1)S(1)} %get-tuple-element.111), channel_id=1, source_target_pairs={{0,6},{1,7},{2,4},{3,5},{4,2},{5,3},{6,0},{7,1},{8,14},{9,15},{10,... | collective-permute-start | bytes 202760 | tf_op jit(solution)/shard_map/ppermute | solution.py:535
  147.4 7.9 %collective-permute-start.35 = (bf16[264,128]{1,0:T(8,128)(2,1)S(1)}, bf16[264,128]{1,0:T(8,128)(2,1)S(1)}, u32[]{:S(2)}, u32[]{:S(2)}) collective-permute-start(bf16[264,128]{1,0:T(8,128)(2,1)S(1)} %get-tuple-element.112), channel_id=1, source_target_pairs={{0,7},{1,6},{2,5},{3,4},{4,3},{5,2},{6,1},{7,0},{8,15},{9,14},{10,... | collective-permute-start | bytes 202760 | tf_op jit(solution)/shard_map/ppermute | solution.py:535
  152.0 10.1 %collective-permute-start.26 = (bf16[264,128]{1,0:T(8,128)(2,1)S(1)}, bf16[264,128]{1,0:T(8,128)(2,1)S(1)}, u32[]{:S(2)}, u32[]{:S(2)}) collective-permute-start(bf16[264,128]{1,0:T(8,128)(2,1)S(1)} %get-tuple-element.87), channel_id=1, source_target_pairs={{0,1},{1,0},{2,3},{3,2},{4,5},{5,4},{6,7},{7,6},{8,9},{9,8},{10,11... | collective-permute-start | bytes 202760 | tf_op jit(solution)/shard_map/ppermute | solution.py:535
  152.7 11.6 %collective-permute-start.27 = (bf16[264,128]{1,0:T(8,128)(2,1)S(1)}, bf16[264,128]{1,0:T(8,128)(2,1)S(1)}, u32[]{:S(2)}, u32[]{:S(2)}) collective-permute-start(bf16[264,128]{1,0:T(8,128)(2,1)S(1)} %get-tuple-element.88), channel_id=1, source_target_pairs={{0,2},{1,3},{2,0},{3,1},{4,6},{5,7},{6,4},{7,5},{8,10},{9,11},{10,... | collective-permute-start | bytes 202760 | tf_op jit(solution)/shard_map/ppermute | solution.py:535
  155.3 10.1 %collective-permute-start.28 = (bf16[264,128]{1,0:T(8,128)(2,1)S(1)}, bf16[264,128]{1,0:T(8,128)(2,1)S(1)}, u32[]{:S(2)}, u32[]{:S(2)}) collective-permute-start(bf16[264,128]{1,0:T(8,128)(2,1)S(1)} %get-tuple-element.89), channel_id=1, source_target_pairs={{0,3},{1,2},{2,1},{3,0},{4,7},{5,6},{6,5},{7,4},{8,11},{9,10},{10,... | collective-permute-start | bytes 202760 | tf_op jit(solution)/shard_map/ppermute | solution.py:535
  158.4 11.0 %collective-permute-start.36 = (bf16[264,128]{1,0:T(8,128)(2,1)S(1)}, bf16[264,128]{1,0:T(8,128)(2,1)S(1)}, u32[]{:S(2)}, u32[]{:S(2)}) collective-permute-start(bf16[264,128]{1,0:T(8,128)(2,1)S(1)} %get-tuple-element.114), channel_id=1, source_target_pairs={{0,4},{1,5},{2,6},{3,7},{4,0},{5,1},{6,2},{7,3},{8,12},{9,13},{10,... | collective-permute-start | bytes 202760 | tf_op jit(solution)/shard_map/ppermute | solution.py:535
  162.2 10.0 %collective-permute-start.37 = (bf16[264,128]{1,0:T(8,128)(2,1)S(1)}, bf16[264,128]{1,0:T(8,128)(2,1)S(1)}, u32[]{:S(2)}, u32[]{:S(2)}) collective-permute-start(bf16[264,128]{1,0:T(8,128)(2,1)S(1)} %get-tuple-element.115), channel_id=1, source_target_pairs={{0,5},{1,4},{2,7},{3,6},{4,1},{5,0},{6,3},{7,2},{8,13},{9,12},{10,... | collective-permute-start | bytes 202760 | tf_op jit(solution)/shard_map/ppermute | solution.py:535
  162.2 11.5 %collective-permute-start.38 = (bf16[264,128]{1,0:T(8,128)(2,1)S(1)}, bf16[264,128]{1,0:T(8,128)(2,1)S(1)}, u32[]{:S(2)}, u32[]{:S(2)}) collective-permute-start(bf16[264,128]{1,0:T(8,128)(2,1)S(1)} %get-tuple-element.116), channel_id=1, source_target_pairs={{0,6},{1,7},{2,4},{3,5},{4,2},{5,3},{6,0},{7,1},{8,14},{9,15},{10,... | collective-permute-start | bytes 202760 | tf_op jit(solution)/shard_map/ppermute | solution.py:535
  164.3 9.4 %collective-permute-start.39 = (bf16[264,128]{1,0:T(8,128)(2,1)S(1)}, bf16[264,128]{1,0:T(8,128)(2,1)S(1)}, u32[]{:S(2)}, u32[]{:S(2)}) collective-permute-start(bf16[264,128]{1,0:T(8,128)(2,1)S(1)} %get-tuple-element.117), channel_id=1, source_target_pairs={{0,7},{1,6},{2,5},{3,4},{4,3},{5,2},{6,1},{7,0},{8,15},{9,14},{10,... | collective-permute-start | bytes 202760 | tf_op jit(solution)/shard_map/ppermute | solution.py:535
  (23 other events, 354.9 us)

commit v3 on v2

--- a/solution.py
+++ b/solution.py
@@ -610,7 +610,7 @@
     low = call(
         "cut",
         cut_kernel,
-        shape((w_in.shape[1] // 2, w_in.shape[2]), BF16),
+        pltpu.VMEM((w_in.shape[1] // 2, w_in.shape[2]), BF16),
         [pltpu.SemaphoreType.DMA(())],
         off(w_in[0]),
         in_specs=hbm(1),
@@ -669,6 +669,19 @@
     if apart:
         count = expert_count // 2
         halves = [Slots(count, cap_expert, width, count, True)] * 2
+
+    def hold(name, arrays):
+        return call(
+            name,
+            hold_kernel,
+            [pltpu.VMEM(w.shape, BF16) for w in arrays],
+            [pltpu.SemaphoreType.DMA((len(arrays),))],
+            *[off(w) for w in arrays],
+            in_specs=hbm(len(arrays)),
+        )
+
+    if apart:
+        ins[1:] = hold("holdin", ins[1:])
     total, last, *hidden = call(
         "forward",
         bind(forward_kernel, eslots),
@@ -713,15 +726,8 @@
         )
 
     if apart:
-        held = call(
-            "hold",
-            hold_kernel,
-            [pltpu.VMEM(w.shape, BF16) for w in ins + outs],
-            [pltpu.SemaphoreType.DMA((14,))],
-            *[off(w) for w in ins + outs],
-            in_specs=hbm(14),
-        )
-        ins, outs = held[:7], held[7:]
+        held = hold("hold", [ins[0]] + outs)
+        ins, outs = [held[0]] + list(ins[1:]), held[1:]
         far = back_pass("backfar", halves[1], arrived_grads[count:], hidden[1])
         far = [trade_one(eslots, x, count + i) for i, x in enumerate(far)]
         near = back_pass("backnear", halves[0], arrived_grads[:count], hidden[0])

time: 219 us -> 219 us (level)
    pallas_call x13 -> x14, Pallas kernels: 38.2 us -> 38.6 us  [call(): pl.pallas_call(kernel, out_shape=out_shape, in_specs=in_specs or vmem(len...]
  transfers between devices with their start and end apart: 41 -> 41, of which waited for: 13 -> 12; matrix products, arithmetic and copies ran while one was open for 0% -> 0% of each run, Pallas kernels for 9% -> 10%
where the time goes in v3:
time: 219 us; the launch traced here: 218 us
  waiting for transfers between devices  74.2 us (34%)
  blocking collectives  51.4 us (23%)
  starting transfers between devices  51.3 us (23%)
  Pallas kernels  38.6 us (18%)
    ppermute x12, waiting for transfers between devices, send(): return lax.ppermute(x, 'dp', [(i, i ^ bit) for i in range(4)])  57 us
    pallas_call x14, Pallas kernels, call(): pl.pallas_call(kernel, out_shape=out_shape, in_specs=in_specs or vmem(len...  38.6 us
    all_to_all x1, blocking collectives, per_device(): row_in = lax.all_to_all(row_out, both, 0, 0, tiled=True)  37.1 us
    ppermute x28, starting transfers between devices, trade_one(): lax.ppermute(chunk, 'expert', [(i, i ^ k) for i in range(eslots.peers)])  36.9 us
    ppermute x28, waiting for transfers between devices, trade_one(): lax.ppermute(chunk, 'expert', [(i, i ^ k) for i in range(eslots.peers)])  17.2 us
    all_to_all x1, blocking collectives, per_device(): wanted = lax.all_to_all(want, both, 0, 0, tiled=True)  14.3 us
    ppermute x12, starting transfers between devices, send(): return lax.ppermute(x, 'dp', [(i, i ^ bit) for i in range(4)])  11.4 us
  transfers between devices with their start and end apart: 41, of which 12 were waited for; matrix products, arithmetic and copies ran while one was open for 0% of the time, Pallas kernels for 10%

profile of v3, /device:TPU:0, one launch (start us, length us, event | category | flops | bytes accessed | tf_op | source)
XLA Modules:
  0.0 218.4 jit_solution(12811801932220403236)
XLA Ops:
  0.6 3.6 %shard_map.130 = (f32[128,160]{1,0:T(8,128)S(1)}, s32[32,128]{1,0:T(8,128)S(1)}) custom-call(s32[1]{0:T(128)} %bitcast.refs_0_, s32[16,128]{1,0:T(8,128)} %bitcast.30, s32[16,128]{1,0:T(8,128)} %bitcast.31, s32[4,128]{1,0:T(4,128)} %refs_3_.2, s32[2,128]{1,0:T(2,128)} %bitcast.32), custom_call_target="tpu_custom_call" | custom-call | tf_op jit(solution)/shard_map/pallas_call | solution.py:578
  4.3 14.3 %all_to_all.21 = s32[32,1,128]{2,1,0:T(1,128)S(1)} all-to-all(s32[32,1,128]{2,1,0:T(1,128)S(1)} %bitcast.20), channel_id=1, replica_groups=mesh['dp'=4,'expert'=8] {'dp','expert'}, dimensions={0} | all-to-all | bytes 32768 | tf_op jit(solution)/shard_map/all_to_all | solution.py:621
  18.6 4.2 %shard_map.131 = bf16[32,168,128]{2,1,0:T(8,128)(2,1)} custom-call(s32[32,128]{1,0:T(8,128)S(1)} %bitcast.16, f32[1024,256]{1,0:T(8,128)} %bitcast.29), custom_call_target="tpu_custom_call" | custom-call | tf_op jit(solution)/shard_map/pallas_call | solution.py:578
  22.8 3.0 %all-to-all-start.1 = ((bf16[32,168,128]{2,1,0:T(8,128)(2,1)}), bf16[32,168,128]{2,1,0:T(8,128)(2,1)S(1)}, u32[]{:S(2)}, u32[]{:S(2)}) async-start(bf16[32,168,128]{2,1,0:T(8,128)(2,1)} %shard_map.131), calls=%async_computation.1 | async-start | bytes 2752512 | tf_op jit(solution)/shard_map/all_to_all | solution.py:651
  33.7 19.3 %collective-permute-done.15.refs_18_.refs_4_ = bf16[256,1024]{1,0:T(8,128)(2,1)S(1)} collective-permute-done((bf16[256,1024]{1,0:T(8,128)(2,1)S(1)}, bf16[256,1024]{1,0:T(8,128)(2,1)S(1)}, u32[]{:S(2)}, u32[]{:S(2)}) %collective-permute-start.15) | collective-permute-done | bytes 524320 | tf_op jit(solution)/shard_map/ppermute | solution.py:526
  54.6 11.6 %collective-permute-done.9.refs_2_ = bf16[512,512]{1,0:T(8,128)(2,1)S(1)} collective-permute-done((bf16[512,512]{1,0:T(8,128)(2,1)S(1)}, bf16[512,512]{1,0:T(8,128)(2,1)S(1)}, u32[]{:S(2)}, u32[]{:S(2)}) %collective-permute-start.9) | collective-permute-done | bytes 524320 | tf_op jit(solution)/shard_map/ppermute | solution.py:526
  67.7 9.8 %collective-permute-done.10.refs_3_ = bf16[512,512]{1,0:T(8,128)(2,1)} collective-permute-done((bf16[512,512]{1,0:T(8,128)(2,1)}, bf16[512,512]{1,0:T(8,128)(2,1)}, u32[]{:S(2)}, u32[]{:S(2)}) %collective-permute-start.10) | collective-permute-done | bytes 524320 | tf_op jit(solution)/shard_map/ppermute | solution.py:526
  78.5 10.2 %collective-permute-done.16.refs_19_.refs_5_ = bf16[256,1024]{1,0:T(8,128)(2,1)} collective-permute-done((bf16[256,1024]{1,0:T(8,128)(2,1)S(1)}, bf16[256,1024]{1,0:T(8,128)(2,1)}, u32[]{:S(2)}, u32[]{:S(2)}) %collective-permute-start.16) | collective-permute-done | bytes 524320 | tf_op jit(solution)/shard_map/ppermute | solution.py:526
  90.9 2.7 %shard_map.132 = (bf16[264,128]{1,0:T(8,128)(2,1)S(1)}, bf16[264,128]{1,0:T(8,128)(2,1)S(1)}, bf16[264,128]{1,0:T(8,128)(2,1)S(1)}, bf16[264,128]{1,0:T(8,128)(2...) custom-call(bf16[32,168,128]{2,1,0:T(8,128)(2,1)S(1)} %all-to-all-do, ...), custom_call_target="tpu_custom_call" | custom-call | tf_op jit(solution)/shard_map/pallas_call | solution.py:578
  93.8 6.2 %collective-permute-done.11.refs_4_ = bf16[512,512]{1,0:T(8,128)(2,1)} collective-permute-done((bf16[512,512]{1,0:T(8,128)(2,1)}, bf16[512,512]{1,0:T(8,128)(2,1)}, u32[]{:S(2)}, u32[]{:S(2)}) %collective-permute-start.11) | collective-permute-done | bytes 524320 | tf_op jit(solution)/shard_map/ppermute | solution.py:526
  101.5 2.6 %collective-permute-start.3 = (bf16[264,128]{1,0:T(8,128)(2,1)S(1)}, bf16[264,128]{1,0:T(8,128)(2,1)S(1)}, u32[]{:S(2)}, u32[]{:S(2)}) collective-permute-start(bf16[264,128]{1,0:T(8,128)(2,1)S(1)} %get-tuple-element.68), channel_id=1, source_target_pairs={{0,4},{1,5},{2,6},{3,7},{4,0},{5,1},{6,2},{7,3},{8,12},{9,13},{10,... | collective-permute-start | bytes 202760 | tf_op jit(solution)/shard_map/ppermute | solution.py:535
  105.7 2.7 %collective-permute-start.5 = (bf16[264,128]{1,0:T(8,128)(2,1)S(1)}, bf16[264,128]{1,0:T(8,128)(2,1)S(1)}, u32[]{:S(2)}, u32[]{:S(2)}) collective-permute-start(bf16[264,128]{1,0:T(8,128)(2,1)S(1)} %get-tuple-element.70), channel_id=1, source_target_pairs={{0,6},{1,7},{2,4},{3,5},{4,2},{5,3},{6,0},{7,1},{8,14},{9,15},{10,... | collective-permute-start | bytes 202760 | tf_op jit(solution)/shard_map/ppermute | solution.py:535
  108.4 4.5 %collective-permute-start.6 = (bf16[264,128]{1,0:T(8,128)(2,1)S(1)}, bf16[264,128]{1,0:T(8,128)(2,1)S(1)}, u32[]{:S(2)}, u32[]{:S(2)}) collective-permute-start(bf16[264,128]{1,0:T(8,128)(2,1)S(1)} %get-tuple-element.71), channel_id=1, source_target_pairs={{0,7},{1,6},{2,5},{3,4},{4,3},{5,2},{6,1},{7,0},{8,15},{9,14},{10,... | collective-permute-start | bytes 202760 | tf_op jit(solution)/shard_map/ppermute | solution.py:535
  112.8 1.9 shard_map.134
  115.2 5.1 %shard_map.135 = (f32[264,1024]{1,0:T(8,128)S(1)}, bf16[264,512]{1,0:T(8,128)(2,1)S(1)}, bf16[4,132,512]{2,1,0:T(8,128)(2,1)S(1)}, bf16[4,132,512]{2,1,0:T(8,128)(2,1)S(1)}) custom-call(bf16[264,128]{1,0:T(8,128)(2,1)S(1)} %get-tuple-element.64.refs_0_, bf16[264,128]{1,0:T(8,128)(2,1)S(1)} %collective-permute-done.refs_1_, ...), custom_call_target="tpu_custom_call" | custom-call | tf_op jit(solution)/shard_map/pallas_call | solution.py:578
  121.3 3.0 %collective-permute-start.20 = (bf16[264,128]{1,0:T(8,128)(2,1)S(1)}, bf16[264,128]{1,0:T(8,128)(2,1)S(1)}, u32[]{:S(2)}, u32[]{:S(2)}) collective-permute-start(bf16[264,128]{1,0:T(8,128)(2,1)S(1)} %get-tuple-element.84), channel_id=1, source_target_pairs={{0,2},{1,3},{2,0},{3,1},{4,6},{5,7},{6,4},{7,5},{8,10},{9,11},{10,... | collective-permute-start | bytes 202760 | tf_op jit(solution)/shard_map/ppermute | solution.py:535
  124.3 2.6 %collective-permute-start.22 = (bf16[264,128]{1,0:T(8,128)(2,1)S(1)}, bf16[264,128]{1,0:T(8,128)(2,1)S(1)}, u32[]{:S(2)}, u32[]{:S(2)}) collective-permute-start(bf16[264,128]{1,0:T(8,128)(2,1)S(1)} %get-tuple-element.86), channel_id=1, source_target_pairs={{0,4},{1,5},{2,6},{3,7},{4,0},{5,1},{6,2},{7,3},{8,12},{9,13},{10,... | collective-permute-start | bytes 202760 | tf_op jit(solution)/shard_map/ppermute | solution.py:535
  126.9 2.2 %collective-permute-start.24 = (bf16[264,128]{1,0:T(8,128)(2,1)S(1)}, bf16[264,128]{1,0:T(8,128)(2,1)S(1)}, u32[]{:S(2)}, u32[]{:S(2)}) collective-permute-start(bf16[264,128]{1,0:T(8,128)(2,1)S(1)} %get-tuple-element.88), channel_id=1, source_target_pairs={{0,6},{1,7},{2,4},{3,5},{4,2},{5,3},{6,0},{7,1},{8,14},{9,15},{10,... | collective-permute-start | bytes 202760 | tf_op jit(solution)/shard_map/ppermute | solution.py:535
  130.5 6.9 %collective-permute-done.23.refs_5_ = bf16[264,128]{1,0:T(8,128)(2,1)S(1)} collective-permute-done((bf16[264,128]{1,0:T(8,128)(2,1)S(1)}, bf16[264,128]{1,0:T(8,128)(2,1)S(1)}, u32[]{:S(2)}, u32[]{:S(2)}) %collective-permute-start.23) | collective-permute-done | bytes 67616 | tf_op jit(solution)/shard_map/ppermute | solution.py:535
  137.5 3.6 %shard_map.137 = (f32[2,128]{1,0:T(2,128)}, f32[128,1024]{1,0:T(8,128)S(1)}, bf16[264,128]{1,0:T(8,128)(2,1)S(1)}, bf16[264,128]{1,0:T(8,128)(2,1)S(1)}, bf16[26...) custom-call(bf16[264,128]{1,0:T(8,128)(2,1)S(1)} %get-tuple-element., ...), custom_call_target="tpu_custom_call" | custom-call | tf_op jit(solution)/shard_map/pallas_call | solution.py:578
  141.1 3.6 %collective-permute-start.32 = (bf16[264,128]{1,0:T(8,128)(2,1)S(1)}, bf16[264,128]{1,0:T(8,128)(2,1)S(1)}, u32[]{:S(2)}, u32[]{:S(2)}) collective-permute-start(bf16[264,128]{1,0:T(8,128)(2,1)S(1)} %get-tuple-element.109), channel_id=1, source_target_pairs={{0,4},{1,5},{2,6},{3,7},{4,0},{5,1},{6,2},{7,3},{8,12},{9,13},{10,... | collective-permute-start | bytes 202760 | tf_op jit(solution)/shard_map/ppermute | solution.py:535
  144.7 2.2 %collective-permute-start.34 = (bf16[264,128]{1,0:T(8,128)(2,1)S(1)}, bf16[264,128]{1,0:T(8,128)(2,1)S(1)}, u32[]{:S(2)}, u32[]{:S(2)}) collective-permute-start(bf16[264,128]{1,0:T(8,128)(2,1)S(1)} %get-tuple-element.111), channel_id=1, source_target_pairs={{0,6},{1,7},{2,4},{3,5},{4,2},{5,3},{6,0},{7,1},{8,14},{9,15},{10,... | collective-permute-start | bytes 202760 | tf_op jit(solution)/shard_map/ppermute | solution.py:535
  148.0 2.5 %shard_map.138 = (bf16[1024,512]{1,0:T(8,128)(2,1)S(1)}, bf16[512,1024]{1,0:T(8,128)(2,1)S(1)}, bf16[256,1024]{1,0:T(8,128)(2,1)S(1)}, bf16[256,1024]{1,0:T(8,12...) custom-call(bf16[1024,512]{1,0:T(8,128)(2,1)} %bitcast.24, ...), custom_call_target="tpu_custom_call" | custom-call | tf_op jit(solution)/shard_map/pallas_call | solution.py:578
  151.6 3.3 %collective-permute-done.33.refs_1_ = bf16[264,128]{1,0:T(8,128)(2,1)S(1)} collective-permute-done((bf16[264,128]{1,0:T(8,128)(2,1)S(1)}, bf16[264,128]{1,0:T(8,128)(2,1)S(1)}, u32[]{:S(2)}, u32[]{:S(2)}) %collective-permute-start.33) | collective-permute-done | bytes 67616 | tf_op jit(solution)/shard_map/ppermute | solution.py:535
  154.9 3.1 %shard_map.140 = (bf16[264,128]{1,0:T(8,128)(2,1)S(1)}, bf16[264,128]{1,0:T(8,128)(2,1)S(1)}, bf16[264,128]{1,0:T(8,128)(2,1)S(1)}, bf16[264,128]{1,0:T(8,128)(2,1)S(1)}) custom-call(bf16[264,128]{1,0:T(8,128)(2,1)S(1)} %collective-permute-done.32.refs_0_, bf16[264,128]{1,0:T(8,128)(2,1)S(1)} %collective-permute-done.33.refs_1_, ...), custom_call_target="tpu_custom_call" | custom-call | tf_op jit(solution)/shard_map/pallas_call | solution.py:578
  158.0 3.6 %collective-permute-start.36 = (bf16[264,128]{1,0:T(8,128)(2,1)S(1)}, bf16[264,128]{1,0:T(8,128)(2,1)S(1)}, u32[]{:S(2)}, u32[]{:S(2)}) collective-permute-start(bf16[264,128]{1,0:T(8,128)(2,1)S(1)} %get-tuple-element.114), channel_id=1, source_target_pairs={{0,4},{1,5},{2,6},{3,7},{4,0},{5,1},{6,2},{7,3},{8,12},{9,13},{10,... | collective-permute-start | bytes 202760 | tf_op jit(solution)/shard_map/ppermute | solution.py:535
  161.6 2.1 collective-permute-start.38
  164.9 3.3 %shard_map.139 = (bf16[264,128]{1,0:T(8,128)(2,1)S(1)}, bf16[264,128]{1,0:T(8,128)(2,1)S(1)}, bf16[264,128]{1,0:T(8,128)(2,1)S(1)}, bf16[264,128]{1,0:T(8,128)(2,1)S(1)}) custom-call(bf16[264,128]{1,0:T(8,128)(2,1)S(1)} %get-tuple-element.92.refs_0_, bf16[264,128]{1,0:T(8,128)(2,1)S(1)} %collective-permute-done.26.refs_1_, ...), custom_call_target="tpu_custom_call" | custom-call | tf_op jit(solution)/shard_map/pallas_call | solution.py:578
  169.2 2.5 %collective-permute-done.37.refs_5_ = bf16[264,128]{1,0:T(8,128)(2,1)S(1)} collective-permute-done((bf16[264,128]{1,0:T(8,128)(2,1)S(1)}, bf16[264,128]{1,0:T(8,128)(2,1)S(1)}, u32[]{:S(2)}, u32[]{:S(2)}) %collective-permute-start.37) | collective-permute-done | bytes 67616 | tf_op jit(solution)/shard_map/ppermute | solution.py:535
  173.2 2.6 %collective-permute-done.31.refs_3_ = bf16[264,128]{1,0:T(8,128)(2,1)S(1)} collective-permute-done((bf16[264,128]{1,0:T(8,128)(2,1)S(1)}, bf16[264,128]{1,0:T(8,128)(2,1)S(1)}, u32[]{:S(2)}, u32[]{:S(2)}) %collective-permute-start.31) | collective-permute-done | bytes 67616 | tf_op jit(solution)/shard_map/ppermute | solution.py:535
  177.6 37.1 %all_to_all.22.refs_0_ = bf16[32,168,128]{2,1,0:T(8,128)(2,1)S(1)} all-to-all(bf16[32,168,128]{2,1,0:T(8,128)(2,1)S(1)} %shard_map.142), channel_id=1, replica_groups=mesh['dp'=4,'expert'=8] {'dp','expert'}, dimensions={0} | all-to-all | bytes 2752512 | tf_op jit(solution)/shard_map/all_to_all | solution.py:747
  214.7 3.5 %shard_map.143 = (f32[4,256,256]{2,1,0:T(8,128)}, f32[4,256]{1,0:T(4,128)}) custom-call(bf16[32,168,128]{2,1,0:T(8,128)(2,1)S(1)} %all_to_all.22.refs_0_, s32[32,128]{1,0:T(8,128)S(1)} %bitcast.17, f32[4,256,256]{2,1,0:T(8,128)} %refs_2_.1, f32[4,256]{1,0:T(4,128)S(1)} %copy-done.7), custom_call_target="tpu_custom_call" | custom-call | tf_op jit(solution)/shard_map/pallas_call | solution.py:578
  (95 shorter events, 28.0 us)
Async XLA Ops:
  22.8 68.1 %all-to-all-start.1 = ((bf16[32,168,128]{2,1,0:T(8,128)(2,1)}), bf16[32,168,128]{2,1,0:T(8,128)(2,1)S(1)}, u32[]{:S(2)}, u32[]{:S(2)}) async-start(bf16[32,168,128]{2,1,0:T(8,128)(2,1)} %shard_map.131), calls=%async_computation.1 | async-start | bytes 2752512 | tf_op jit(solution)/shard_map/all_to_all | solution.py:651
  25.9 27.0 %collective-permute-start.15 = (bf16[256,1024]{1,0:T(8,128)(2,1)S(1)}, bf16[256,1024]{1,0:T(8,128)(2,1)S(1)}, u32[]{:S(2)}, u32[]{:S(2)}) collective-permute-start(bf16[256,1024]{1,0:T(8,128)(2,1)S(1)} %slice_bitcast_fusion), channel_id=1, source_target_pairs={{0,16},{8,24},{16,0},{24,8},{1,17},{9,25},{17,1},{25,9},{2,18},{10... | collective-permute-start | bytes 1572872 | tf_op jit(solution)/shard_map/ppermute | solution.py:526
  27.6 25.4 %collective-permute-start.13 = (bf16[256,1024]{1,0:T(8,128)(2,1)S(1)}, bf16[256,1024]{1,0:T(8,128)(2,1)}, u32[]{:S(2)}, u32[]{:S(2)}) collective-permute-start(bf16[256,1024]{1,0:T(8,128)(2,1)S(1)} %slice_bitcast_fusion), channel_id=1, source_target_pairs={{0,8},{8,0},{16,24},{24,16},{1,9},{9,1},{17,25},{25,17},{2,10},{10... | collective-permute-start | bytes 1572872 | tf_op jit(solution)/shard_map/ppermute | solution.py:526
  30.2 36.0 %collective-permute-start.9 = (bf16[512,512]{1,0:T(8,128)(2,1)S(1)}, bf16[512,512]{1,0:T(8,128)(2,1)S(1)}, u32[]{:S(2)}, u32[]{:S(2)}) collective-permute-start(bf16[512,512]{1,0:T(8,128)(2,1)S(1)} %shard_map.133), channel_id=1, source_target_pairs={{0,16},{8,24},{16,0},{24,8},{1,17},{9,25},{17,1},{25,9},{2,18},{10... | collective-permute-start | bytes 1572872 | tf_op jit(solution)/shard_map/ppermute | solution.py:526
  30.8 36.4 %collective-permute-start.7 = (bf16[512,512]{1,0:T(8,128)(2,1)S(1)}, bf16[512,512]{1,0:T(8,128)(2,1)}, u32[]{:S(2)}, u32[]{:S(2)}) collective-permute-start(bf16[512,512]{1,0:T(8,128)(2,1)S(1)} %shard_map.133), channel_id=1, source_target_pairs={{0,8},{8,0},{16,24},{24,16},{1,9},{9,1},{17,25},{25,17},{2,10},{10... | collective-permute-start | bytes 1572872 | tf_op jit(solution)/shard_map/ppermute | solution.py:526
  32.0 45.5 %collective-permute-start.10 = (bf16[512,512]{1,0:T(8,128)(2,1)}, bf16[512,512]{1,0:T(8,128)(2,1)}, u32[]{:S(2)}, u32[]{:S(2)}) collective-permute-start(bf16[512,512]{1,0:T(8,128)(2,1)} %slice.9), channel_id=1, source_target_pairs={{0,16},{8,24},{16,0},{24,8},{1,17},{9,25},{17,1},{25,9},{2,18},{10... | collective-permute-start | bytes 1572872 | tf_op jit(solution)/shard_map/ppermute | solution.py:526
  52.9 35.8 %collective-permute-start.16 = (bf16[256,1024]{1,0:T(8,128)(2,1)S(1)}, bf16[256,1024]{1,0:T(8,128)(2,1)}, u32[]{:S(2)}, u32[]{:S(2)}) collective-permute-start(bf16[256,1024]{1,0:T(8,128)(2,1)S(1)} %slice.11), channel_id=1, source_target_pairs={{0,16},{8,24},{16,0},{24,8},{1,17},{9,25},{17,1},{25,9},{2,18},{10... | collective-permute-start | bytes 1572872 | tf_op jit(solution)/shard_map/ppermute | solution.py:526
  53.0 35.8 %collective-permute-start.14 = (bf16[256,1024]{1,0:T(8,128)(2,1)S(1)}, bf16[256,1024]{1,0:T(8,128)(2,1)S(1)}, u32[]{:S(2)}, u32[]{:S(2)}) collective-permute-start(bf16[256,1024]{1,0:T(8,128)(2,1)S(1)} %slice.11), channel_id=1, source_target_pairs={{0,8},{8,0},{16,24},{24,16},{1,9},{9,1},{17,25},{25,17},{2,10},{10... | collective-permute-start | bytes 1572872 | tf_op jit(solution)/shard_map/ppermute | solution.py:526
  66.2 27.5 %collective-permute-start.8 = (bf16[512,512]{1,0:T(8,128)(2,1)}, bf16[512,512]{1,0:T(8,128)(2,1)}, u32[]{:S(2)}, u32[]{:S(2)}) collective-permute-start(bf16[512,512]{1,0:T(8,128)(2,1)} %slice.9), channel_id=1, source_target_pairs={{0,8},{8,0},{16,24},{24,16},{1,9},{9,1},{17,25},{25,17},{2,10},{10... | collective-permute-start | bytes 1572872 | tf_op jit(solution)/shard_map/ppermute | solution.py:526
  67.2 32.8 %collective-permute-start.11 = (bf16[512,512]{1,0:T(8,128)(2,1)}, bf16[512,512]{1,0:T(8,128)(2,1)}, u32[]{:S(2)}, u32[]{:S(2)}) collective-permute-start(bf16[512,512]{1,0:T(8,128)(2,1)} %collective-permute-done.7.refs_0_), channel_id=1, source_target_pairs={{0,16},{8,24},{16,0},{24,8},{1,17},{9,25},{17,1},{25,9},{2,18},{10... | collective-permute-start | bytes 1572872 | tf_op jit(solution)/shard_map/ppermute | solution.py:526
  77.5 24.0 %collective-permute-start.12 = (bf16[512,512]{1,0:T(8,128)(2,1)}, bf16[512,512]{1,0:T(8,128)(2,1)}, u32[]{:S(2)}, u32[]{:S(2)}) collective-permute-start(bf16[512,512]{1,0:T(8,128)(2,1)} %collective-permute-done.10.refs_3_), channel_id=1, source_target_pairs={{0,8},{8,0},{16,24},{24,16},{1,9},{9,1},{17,25},{25,17},{2,10},{10... | collective-permute-start | bytes 1572872 | tf_op jit(solution)/shard_map/ppermute | solution.py:526
  88.7 31.5 %collective-permute-start.17 = (bf16[256,1024]{1,0:T(8,128)(2,1)}, bf16[256,1024]{1,0:T(8,128)(2,1)S(1)}, u32[]{:S(2)}, u32[]{:S(2)}) collective-permute-start(bf16[256,1024]{1,0:T(8,128)(2,1)} %collective-permute-done.13.refs_16_.refs_2_), channel_id=1, source_target_pairs={{0,16},{8,24},{16,0},{24,8},{1,17},{9,25},{17,1},{25,9},{2,18},{10... | collective-permute-start | bytes 1572872 | tf_op jit(solution)/shard_map/ppermute | solution.py:526
  89.6 30.7 %collective-permute-start.18 = (bf16[256,1024]{1,0:T(8,128)(2,1)}, bf16[256,1024]{1,0:T(8,128)(2,1)S(1)}, u32[]{:S(2)}, u32[]{:S(2)}) collective-permute-start(bf16[256,1024]{1,0:T(8,128)(2,1)} %collective-permute-done.16.refs_19_.refs_5_), channel_id=1, source_target_pairs={{0,8},{8,0},{16,24},{24,16},{1,9},{9,1},{17,25},{25,17},{2,10},{10... | collective-permute-start | bytes 1572872 | tf_op jit(solution)/shard_map/ppermute | solution.py:526
  93.7 7.8 %collective-permute-start = (bf16[264,128]{1,0:T(8,128)(2,1)S(1)}, bf16[264,128]{1,0:T(8,128)(2,1)S(1)}, u32[]{:S(2)}, u32[]{:S(2)}) collective-permute-start(bf16[264,128]{1,0:T(8,128)(2,1)S(1)} %get-tuple-element.65), channel_id=1, source_target_pairs={{0,1},{1,0},{2,3},{3,2},{4,5},{5,4},{6,7},{7,6},{8,9},{9,8},{10,11... | collective-permute-start | bytes 202760 | tf_op jit(solution)/shard_map/ppermute | solution.py:535
  101.5 6.9 %collective-permute-start.3 = (bf16[264,128]{1,0:T(8,128)(2,1)S(1)}, bf16[264,128]{1,0:T(8,128)(2,1)S(1)}, u32[]{:S(2)}, u32[]{:S(2)}) collective-permute-start(bf16[264,128]{1,0:T(8,128)(2,1)S(1)} %get-tuple-element.68), channel_id=1, source_target_pairs={{0,4},{1,5},{2,6},{3,7},{4,0},{5,1},{6,2},{7,3},{8,12},{9,13},{10,... | collective-permute-start | bytes 202760 | tf_op jit(solution)/shard_map/ppermute | solution.py:535
  104.3 10.5 %collective-permute-start.4 = (bf16[264,128]{1,0:T(8,128)(2,1)S(1)}, bf16[264,128]{1,0:T(8,128)(2,1)S(1)}, u32[]{:S(2)}, u32[]{:S(2)}) collective-permute-start(bf16[264,128]{1,0:T(8,128)(2,1)S(1)} %get-tuple-element.69), channel_id=1, source_target_pairs={{0,5},{1,4},{2,7},{3,6},{4,1},{5,0},{6,3},{7,2},{8,13},{9,12},{10,... | collective-permute-start | bytes 202760 | tf_op jit(solution)/shard_map/ppermute | solution.py:535
  105.7 9.0 %collective-permute-start.5 = (bf16[264,128]{1,0:T(8,128)(2,1)S(1)}, bf16[264,128]{1,0:T(8,128)(2,1)S(1)}, u32[]{:S(2)}, u32[]{:S(2)}) collective-permute-start(bf16[264,128]{1,0:T(8,128)(2,1)S(1)} %get-tuple-element.70), channel_id=1, source_target_pairs={{0,6},{1,7},{2,4},{3,5},{4,2},{5,3},{6,0},{7,1},{8,14},{9,15},{10,... | collective-permute-start | bytes 202760 | tf_op jit(solution)/shard_map/ppermute | solution.py:535
  121.3 7.8 %collective-permute-start.20 = (bf16[264,128]{1,0:T(8,128)(2,1)S(1)}, bf16[264,128]{1,0:T(8,128)(2,1)S(1)}, u32[]{:S(2)}, u32[]{:S(2)}) collective-permute-start(bf16[264,128]{1,0:T(8,128)(2,1)S(1)} %get-tuple-element.84), channel_id=1, source_target_pairs={{0,2},{1,3},{2,0},{3,1},{4,6},{5,7},{6,4},{7,5},{8,10},{9,11},{10,... | collective-permute-start | bytes 202760 | tf_op jit(solution)/shard_map/ppermute | solution.py:535
  126.9 10.6 %collective-permute-start.23 = (bf16[264,128]{1,0:T(8,128)(2,1)S(1)}, bf16[264,128]{1,0:T(8,128)(2,1)S(1)}, u32[]{:S(2)}, u32[]{:S(2)}) collective-permute-start(bf16[264,128]{1,0:T(8,128)(2,1)S(1)} %get-tuple-element.87), channel_id=1, source_target_pairs={{0,5},{1,4},{2,7},{3,6},{4,1},{5,0},{6,3},{7,2},{8,13},{9,12},{10,... | collective-permute-start | bytes 202760 | tf_op jit(solution)/shard_map/ppermute | solution.py:535
  126.9 10.6 %collective-permute-start.24 = (bf16[264,128]{1,0:T(8,128)(2,1)S(1)}, bf16[264,128]{1,0:T(8,128)(2,1)S(1)}, u32[]{:S(2)}, u32[]{:S(2)}) collective-permute-start(bf16[264,128]{1,0:T(8,128)(2,1)S(1)} %get-tuple-element.88), channel_id=1, source_target_pairs={{0,6},{1,7},{2,4},{3,5},{4,2},{5,3},{6,0},{7,1},{8,14},{9,15},{10,... | collective-permute-start | bytes 202760 | tf_op jit(solution)/shard_map/ppermute | solution.py:535
  129.1 8.3 %collective-permute-start.25 = (bf16[264,128]{1,0:T(8,128)(2,1)S(1)}, bf16[264,128]{1,0:T(8,128)(2,1)S(1)}, u32[]{:S(2)}, u32[]{:S(2)}) collective-permute-start(bf16[264,128]{1,0:T(8,128)(2,1)S(1)} %get-tuple-element.89), channel_id=1, source_target_pairs={{0,7},{1,6},{2,5},{3,4},{4,3},{5,2},{6,1},{7,0},{8,15},{9,14},{10,... | collective-permute-start | bytes 202760 | tf_op jit(solution)/shard_map/ppermute | solution.py:535
  141.1 10.2 %collective-permute-start.32 = (bf16[264,128]{1,0:T(8,128)(2,1)S(1)}, bf16[264,128]{1,0:T(8,128)(2,1)S(1)}, u32[]{:S(2)}, u32[]{:S(2)}) collective-permute-start(bf16[264,128]{1,0:T(8,128)(2,1)S(1)} %get-tuple-element.109), channel_id=1, source_target_pairs={{0,4},{1,5},{2,6},{3,7},{4,0},{5,1},{6,2},{7,3},{8,12},{9,13},{10,... | collective-permute-start | bytes 202760 | tf_op jit(solution)/shard_map/ppermute | solution.py:535
  144.7 10.2 %collective-permute-start.33 = (bf16[264,128]{1,0:T(8,128)(2,1)S(1)}, bf16[264,128]{1,0:T(8,128)(2,1)S(1)}, u32[]{:S(2)}, u32[]{:S(2)}) collective-permute-start(bf16[264,128]{1,0:T(8,128)(2,1)S(1)} %get-tuple-element.110), channel_id=1, source_target_pairs={{0,5},{1,4},{2,7},{3,6},{4,1},{5,0},{6,3},{7,2},{8,13},{9,12},{10,... | collective-permute-start | bytes 202760 | tf_op jit(solution)/shard_map/ppermute | solution.py:535
  144.7 10.2 %collective-permute-start.34 = (bf16[264,128]{1,0:T(8,128)(2,1)S(1)}, bf16[264,128]{1,0:T(8,128)(2,1)S(1)}, u32[]{:S(2)}, u32[]{:S(2)}) collective-permute-start(bf16[264,128]{1,0:T(8,128)(2,1)S(1)} %get-tuple-element.111), channel_id=1, source_target_pairs={{0,6},{1,7},{2,4},{3,5},{4,2},{5,3},{6,0},{7,1},{8,14},{9,15},{10,... | collective-permute-start | bytes 202760 | tf_op jit(solution)/shard_map/ppermute | solution.py:535
  146.9 8.0 %collective-permute-start.35 = (bf16[264,128]{1,0:T(8,128)(2,1)S(1)}, bf16[264,128]{1,0:T(8,128)(2,1)S(1)}, u32[]{:S(2)}, u32[]{:S(2)}) collective-permute-start(bf16[264,128]{1,0:T(8,128)(2,1)S(1)} %get-tuple-element.112), channel_id=1, source_target_pairs={{0,7},{1,6},{2,5},{3,4},{4,3},{5,2},{6,1},{7,0},{8,15},{9,14},{10,... | collective-permute-start | bytes 202760 | tf_op jit(solution)/shard_map/ppermute | solution.py:535
  150.6 11.1 %collective-permute-start.26 = (bf16[264,128]{1,0:T(8,128)(2,1)S(1)}, bf16[264,128]{1,0:T(8,128)(2,1)S(1)}, u32[]{:S(2)}, u32[]{:S(2)}) collective-permute-start(bf16[264,128]{1,0:T(8,128)(2,1)S(1)} %get-tuple-element.93), channel_id=1, source_target_pairs={{0,1},{1,0},{2,3},{3,2},{4,5},{5,4},{6,7},{7,6},{8,9},{9,8},{10,11... | collective-permute-start | bytes 202760 | tf_op jit(solution)/shard_map/ppermute | solution.py:535
  151.2 12.5 %collective-permute-start.27 = (bf16[264,128]{1,0:T(8,128)(2,1)S(1)}, bf16[264,128]{1,0:T(8,128)(2,1)S(1)}, u32[]{:S(2)}, u32[]{:S(2)}) collective-permute-start(bf16[264,128]{1,0:T(8,128)(2,1)S(1)} %get-tuple-element.94), channel_id=1, source_target_pairs={{0,2},{1,3},{2,0},{3,1},{4,6},{5,7},{6,4},{7,5},{8,10},{9,11},{10,... | collective-permute-start | bytes 202760 | tf_op jit(solution)/shard_map/ppermute | solution.py:535
  154.9 10.0 %collective-permute-start.28 = (bf16[264,128]{1,0:T(8,128)(2,1)S(1)}, bf16[264,128]{1,0:T(8,128)(2,1)S(1)}, u32[]{:S(2)}, u32[]{:S(2)}) collective-permute-start(bf16[264,128]{1,0:T(8,128)(2,1)S(1)} %get-tuple-element.95), channel_id=1, source_target_pairs={{0,3},{1,2},{2,1},{3,0},{4,7},{5,6},{6,5},{7,4},{8,11},{9,10},{10,... | collective-permute-start | bytes 202760 | tf_op jit(solution)/shard_map/ppermute | solution.py:535
  158.0 10.9 %collective-permute-start.36 = (bf16[264,128]{1,0:T(8,128)(2,1)S(1)}, bf16[264,128]{1,0:T(8,128)(2,1)S(1)}, u32[]{:S(2)}, u32[]{:S(2)}) collective-permute-start(bf16[264,128]{1,0:T(8,128)(2,1)S(1)} %get-tuple-element.114), channel_id=1, source_target_pairs={{0,4},{1,5},{2,6},{3,7},{4,0},{5,1},{6,2},{7,3},{8,12},{9,13},{10,... | collective-permute-start | bytes 202760 | tf_op jit(solution)/shard_map/ppermute | solution.py:535
  161.6 10.0 %collective-permute-start.37 = (bf16[264,128]{1,0:T(8,128)(2,1)S(1)}, bf16[264,128]{1,0:T(8,128)(2,1)S(1)}, u32[]{:S(2)}, u32[]{:S(2)}) collective-permute-start(bf16[264,128]{1,0:T(8,128)(2,1)S(1)} %get-tuple-element.115), channel_id=1, source_target_pairs={{0,5},{1,4},{2,7},{3,6},{4,1},{5,0},{6,3},{7,2},{8,13},{9,12},{10,... | collective-permute-start | bytes 202760 | tf_op jit(solution)/shard_map/ppermute | solution.py:535
  161.6 11.5 %collective-permute-start.38 = (bf16[264,128]{1,0:T(8,128)(2,1)S(1)}, bf16[264,128]{1,0:T(8,128)(2,1)S(1)}, u32[]{:S(2)}, u32[]{:S(2)}) collective-permute-start(bf16[264,128]{1,0:T(8,128)(2,1)S(1)} %get-tuple-element.116), channel_id=1, source_target_pairs={{0,6},{1,7},{2,4},{3,5},{4,2},{5,3},{6,0},{7,1},{8,14},{9,15},{10,... | collective-permute-start | bytes 202760 | tf_op jit(solution)/shard_map/ppermute | solution.py:535
  163.7 9.4 %collective-permute-start.39 = (bf16[264,128]{1,0:T(8,128)(2,1)S(1)}, bf16[264,128]{1,0:T(8,128)(2,1)S(1)}, u32[]{:S(2)}, u32[]{:S(2)}) collective-permute-start(bf16[264,128]{1,0:T(8,128)(2,1)S(1)} %get-tuple-element.117), channel_id=1, source_target_pairs={{0,7},{1,6},{2,5},{3,4},{4,3},{5,2},{6,1},{7,0},{8,15},{9,14},{10,... | collective-permute-start | bytes 202760 | tf_op jit(solution)/shard_map/ppermute | solution.py:535
  (22 other events, 329.5 us)
